TPU v7x, 32 devices: a whole 2x2x4 slice. The times are simulated.
32 devices in a mesh: hist: 4 (over y, x), ent: 8 (over z, core).
Axes of the slice: x: 2, y: 2, z: 4, core: 2. Of those that a mesh axis runs over, the one named last changes fastest.
Arguments:
- states: bfloat16 [4, 2048, 512], P('hist', 'ent'), may hold values from -6 to 6
- w_neigh: bfloat16 [2, 256, 256], replicated, may hold values from -0.375 to 0.375
- w_self: bfloat16 [512, 512], replicated, may hold values from -0.25 to 0.25
- w_gate: bfloat16 [512, 512], replicated, may hold values from -0.25 to 0.25
- b_gate: float32 [512], replicated, may hold values from -4 to 4
- relation: bfloat16 [460, 512], replicated, may hold values from -6 to 6
- edge_src: int32 [4, 4096], P('hist', 'ent'), may hold values from 0 to 255
- edge_rel: int32 [4, 4096], P('hist', 'ent'), may hold values from 0 to 459
- edge_dst: int32 [4, 4096], P('hist', 'ent'), may hold values from 0 to 255
- send_counts: int32 [4, 64], P('hist', 'ent'), may hold values from 8 to 64, as said below
- query_ent: int32 [1024], P('ent'), may hold values from 0 to 255
- query_rel: int32 [1024], P('ent'), may hold values from 0 to 459
- query_grad: float32 [1024, 512], P('ent'), may hold values from -6 to 6
Outputs:
- grad_states: float32 [4, 2048, 512], P('hist', 'ent')
- grad_neigh: float32 [2, 256, 256], replicated
- grad_self: float32 [512, 512], replicated
- grad_gate: float32 [512, 512], replicated
- grad_bias: float32 [512], replicated
- grad_relation: float32 [460, 512], replicated
Inputs may be any that keep to these rules, and one draw needn't show every extreme that they name: `send_counts`: slots at or beyond their bucket's count hold arbitrary ids and carry no edge. In every snapshot one target partition receives exactly 64 slots in use from every source partition; which one is drawn.
All inputs are finite; a program needn't handle non-finite values.
Results may differ from a plain program's by a relative error of at most 0.0053.
Values may be sent and summed in bfloat16 or wider, within the bound.
No kernel may reach another device: no remote copies, remote signals or barrier semaphores. Data moves between devices by JAX's collectives and lax.ppermute only.
A program may use at most 64 MiB of HBM per device.

v0:
```python
import functools
import math

import jax
import jax.numpy as jnp
from jax import lax
from jax.experimental import pallas as pl
from jax.experimental.pallas import tpu as pltpu
from jax.sharding import PartitionSpec as P

BF = jnp.bfloat16
F32 = jnp.float32
TALL = (((0,), (0,)), ((), ()))
WIDE = (((1,), (1,)), ((), ()))
LANES = 128


def dot(a, b, dims=(((1,), (0,)), ((), ()))):
    return lax.dot_general(a, b, dims, preferred_element_type=F32)


def onehot(ids, rows):
    spot = lax.broadcasted_iota(jnp.int32, (rows, ids.shape[1]), 0)
    return jnp.where(spot == ids, 1.0, 0.0).astype(BF)


def round_up(value, step):
    return -(-value // step) * step


def block(shape, lead=None):
    if lead is None:
        return pl.BlockSpec(shape, lambda i: (0,) * len(shape))
    return pl.BlockSpec((None,) + shape, lambda i: (lead,) + (0,) * len(shape))


def whole(x):
    return block(x.shape)


def run(body, name, ins, specs, outs, scratch=()):
    return pl.pallas_call(
        body,
        name=name,
        grid=(1,),
        in_specs=specs,
        out_specs=[block(s.shape) for s in outs],
        out_shape=outs,
        scratch_shapes=list(scratch),
    )(*ins)


def sds(shape, dtype):
    return jax.ShapeDtypeStruct(shape, dtype)


def send_kernel(sections, groups, x, rel, src, dst, rid, counts, wn, msg, xp):
    ent_rows, features = x.shape
    slots = src.shape[1]
    room = slots // groups
    width = features // sections
    half = wn.shape[1]
    e = lax.axis_index("ent")
    ids = src[...]
    rids = rid[...]
    xv = x[...]
    got = dot(onehot(ids, ent_rows), xv, TALL) + dot(onehot(rids, rel.shape[0]), rel[...], TALL)
    inputs = got.astype(BF)
    for b in range(wn.shape[0]):
        out = dot(inputs[:, b * half : (b + 1) * half], wn[b]).astype(BF)
        for part in range(half // width):
            target = b * (half // width) + part
            for u in range(groups):
                msg[target * groups + u, :room, :] = out[
                    u * room : (u + 1) * room, part * width : (part + 1) * width
                ]
    lane = lax.broadcasted_iota(jnp.int32, (1, slots), 1)
    limit = jnp.zeros((1, slots), jnp.int32)
    for u in range(groups):
        limit = jnp.where(lane // room == u, counts[0, u], limit)
    live = jnp.where(lane % room < limit, dst[...], -1).astype(F32)
    per = width // room
    seat = lax.broadcasted_iota(jnp.int32, (8, width), 1) // room
    for u in range(groups):
        start = u * room // width * width
        row = jnp.broadcast_to(live[:, start : start + width], (8, width))
        turn = lax.rem(e - u + per * groups, per) * room
        row = pltpu.roll(row, turn, 1)
        row = jnp.where(seat == lax.rem(e, per), row, -1.0).astype(BF)
        for target in range(sections):
            msg[target * groups + u, room:, :] = row
    lines = slots // features
    extra = jnp.zeros((8, features), F32)
    level = lax.broadcasted_iota(jnp.int32, (8, features), 0)
    for k in range(lines):
        cut = slice(k * features, (k + 1) * features)
        for j, piece in enumerate((ids[:, cut], rids[:, cut] // 256, rids[:, cut] % 256)):
            extra = jnp.where(level == 3 * k + j, piece.astype(F32), extra)
    for target in range(sections):
        xp[target, :ent_rows, :] = xv
        xp[target, ent_rows:, :] = extra.astype(BF)


def state_kernel(recv, xp, wg, ws, bias, al, be, ka, sc, odt, osr, rid):
    groups = recv.shape[0]
    width = recv.shape[2]
    room = recv.shape[1] - 8
    features = xp.shape[1]
    ent_rows = xp.shape[0] - 8
    slots = groups * room
    per = width // room
    h = lax.axis_index("hist")
    cols = pl.ds(pl.multiple_of(h * width, width), width)
    summed = jnp.zeros((ent_rows, width), F32)
    degree = jnp.zeros((ent_rows, width), F32)
    ones = jnp.ones((width, width), BF)
    for g in range(groups // per):
        ids = recv[g * per, room:, :].astype(F32)
        for j in range(1, per):
            ids = jnp.maximum(ids, recv[g * per + j, room:, :].astype(F32))
        hot = onehot(ids[:1].astype(jnp.int32), ent_rows)
        rows = jnp.concatenate([recv[g * per + j, :room, :] for j in range(per)], axis=0)
        summed = summed + dot(hot, rows)
        degree = degree + dot(hot, ones)
        odt[g * width : (g + 1) * width, :] = hot.astype(F32).T.astype(BF)
    scaling = 1.0 / jnp.maximum(degree, 1.0)
    x = xp[:ent_rows, :]
    pre_act = summed * scaling + dot(x, ws[:, cols])
    gate_open = jax.nn.sigmoid(dot(x, wg[:, cols]) + bias[:, cols])
    sig = jax.nn.sigmoid(pre_act)
    new_state = pre_act * sig
    ka[...] = 1.0 - gate_open
    al[...] = (new_state - xp[:ent_rows, cols].astype(F32)) * gate_open * (1.0 - gate_open)
    be[...] = gate_open * (sig * (1.0 + pre_act * (1.0 - sig)))
    sc[...] = scaling
    extra = xp[ent_rows:, :].astype(F32).astype(jnp.int32)
    for k in range(slots // features):
        cut = slice(k * features, (k + 1) * features)
        osr[:, cut] = onehot(extra[3 * k : 3 * k + 1], ent_rows)
        ids = extra[3 * k + 1 : 3 * k + 2] * 256 + extra[3 * k + 2 : 3 * k + 3]
        rid[:, cut] = jnp.broadcast_to(ids, (8, features))


def query_kernel(qe, qr, qg, top, qp):
    width = top.shape[1]
    h = lax.axis_index("hist")
    cols = pl.ds(pl.multiple_of(h * width, width), width)
    grad = qg[:, cols]
    for ids, out in ((qe, top), (qr, qp)):
        hot = onehot(ids[...], out.shape[0]).astype(F32)
        out[...] = lax.dot_general(
            hot,
            grad,
            (((1,), (0,)), ((), ())),
            precision=lax.Precision.HIGHEST,
            preferred_element_type=F32,
        )


def top_kernel(count, *refs):
    parts = refs[:count]
    al, be, ka, sc, odt, c_out, gp, keep, bias, rep = refs[count:]
    width = al.shape[1]
    c = parts[0][...]
    for p in parts[1:]:
        c = c + p[...].astype(F32)
    gate_term = c * al[...]
    pre_term = c * be[...]
    rep[...] = dot(odt[...], (pre_term * sc[...]).astype(BF)).astype(BF)
    gp[:, :width] = gate_term.astype(BF)
    gp[:, width:] = pre_term.astype(BF)
    keep[...] = c * ka[...]
    c_out[...] = c
    bias[...] = jnp.broadcast_to(jnp.sum(gate_term, axis=0, keepdims=True), bias.shape)


def back_kernel(sections, ret, gp, osr, keep, wg, ws, wn, base, sp, *sends):
    width = keep.shape[1]
    half = wn.shape[1]
    h = lax.axis_index("hist")
    mine = pl.ds(pl.multiple_of(h * width, width), width)
    mine_in = pl.ds(pl.multiple_of(lax.rem(h * width, half), width), width)
    own = h * width // half
    s = dot(osr[...], ret[...])
    high = s.astype(BF)
    low = (s - high.astype(F32)).astype(BF)
    sp[:, :width] = high
    sp[:, width:] = low
    left = jnp.concatenate([gp[...], high, low], axis=1)
    for k in range(sections):
        to = lax.rem(h + k, sections)
        rows = pl.ds(pl.multiple_of(to * width, width), width)
        rows_in = pl.ds(pl.multiple_of(lax.rem(to * width, half), width), width)
        match = jnp.where(to * width // half == own, 1.0, 0.0).astype(BF)
        w = wn[own, rows_in, mine_in] * match
        right = jnp.concatenate([wg[rows, mine], ws[rows, mine], w, w], axis=1)
        out = dot(left, right, WIDE)
        if k == 0:
            base[...] = keep[...] + out
        else:
            sends[k - 1][...] = out.astype(BF)


def grad_kernel(half, first, xp, gp, sp, ret, rid, bias, *refs):
    ent_rows = gp.shape[0]
    width = sp.shape[1] // 2
    if first:
        gs_in = ns_in = r_in = b_in = None
        gs, ns, rs, bs = refs
    else:
        gs_in, ns_in, r_in, b_in, gs, ns, rs, bs = refs
    h = lax.axis_index("hist")
    own = h * width // half

    def put(out, before, value):
        out[...] = value if before is None else before[...] + value

    put(gs, gs_in, dot(xp[:ent_rows, :], gp[...], TALL))
    xb = xp[:ent_rows, pl.ds(pl.multiple_of(own * half, half), half)]
    both = dot(xb, sp[...], TALL)
    put(ns, ns_in, both[:, :width] + both[:, width:])
    put(rs, r_in, dot(onehot(rid[:1, :], rs.shape[0]), ret[...]))
    put(bs, b_in, bias[...])


def pack_kernel(sizes, gs, ns, rs, qp, bs, out):
    groups = out.shape[0]
    width = out.shape[2]
    pieces = (gs[:, :width], gs[:, width:], ns[...], rs[...], qp[...])
    for u in range(groups):
        at = 0
        for piece, size in zip(pieces, sizes):
            low = min(u * size, piece.shape[0])
            high = min(low + size, piece.shape[0])
            if high > low:
                out[u, at : at + high - low, :] = piece[low:high].astype(BF)
            if high - low < size:
                out[u, at + high - low : at + size, :] = jnp.zeros((size - high + low, width), BF)
            at += size
        out[u, at:, :] = jnp.concatenate([bs[...], bs[...]], axis=0).astype(BF)


def add_kernel(x, out):
    total = x[0].astype(F32)
    for u in range(1, x.shape[0]):
        total = total + x[u].astype(F32)
    for k in range(out.shape[0]):
        out[k] = total.astype(BF)


def last_kernel(sections, groups, sizes, factor, *refs):
    mine = refs[:sections]
    other = refs[sections]
    wn, rel, neigh, self_, gate, bias, relation, r_all, q_all, n_all = refs[sections + 1 :]
    width = mine[0].shape[2]
    blocks, half = wn.shape[0], wn.shape[1]
    relations = rel.shape[0]
    h = lax.axis_index("hist")
    core = lax.rem(lax.axis_index("ent"), 2)
    pairs = groups // 2
    for k in range(sections):
        to = lax.rem(h - k + sections, sections)
        cols = pl.ds(pl.multiple_of(to * width, width), width)
        for z in range(pairs):
            for flip in range(2):
                u = 2 * z + (core if flip == 0 else 1 - core)
                piece = mine[k].at[z] if flip == 0 else other.at[k * pairs + z]
                at = 0
                for out, size, scale in zip(
                    (gate, self_, n_all, r_all, q_all), sizes, (factor, factor, 1.0, 1.0, 1.0)
                ):
                    if True:
                        value = piece[at : at + size, :].astype(F32) * scale
                        where = pl.ds(pl.multiple_of(u * size, size), size)
                        out[where, cols] = value.astype(out.dtype)
                    at += size
        bias[:, cols] = mine[k][0, at : at + 8, :].astype(F32) * factor
    for b in range(blocks):
        cut = slice(b * half, (b + 1) * half)
        r = r_all[:relations, cut]
        neigh[b] = (n_all[:half, cut] + dot(rel[:, cut], r, TALL)) * factor
        relation[:, cut] = (q_all[:relations, cut] + dot(r, wn[b], WIDE)) * factor


def on_device(
    states,
    w_neigh,
    w_self,
    w_gate,
    b_gate,
    relation,
    edge_src,
    edge_rel,
    edge_dst,
    send_counts,
    query_ent,
    query_rel,
    query_grad,
):
    groups = lax.axis_size("ent")
    sections = lax.axis_size("hist")
    ent_rows, features = states.shape[1:]
    slots = edge_src.shape[1]
    room = slots // groups
    width = features // sections
    half = w_neigh.shape[1]
    relations = relation.shape[0]
    hidden = states[0]
    bias_row = b_gate.reshape(1, features)
    smem = pl.BlockSpec(memory_space=pltpu.SMEM)

    def a2a(x, axes):
        return lax.all_to_all(x, axes, split_axis=0, concat_axis=0, tiled=True)

    msg, xp = run(
        functools.partial(send_kernel, sections, groups),
        "send",
        (hidden, relation, edge_src, edge_dst, edge_rel, send_counts, w_neigh),
        [whole(hidden), whole(relation)] + [whole(edge_src)] * 3 + [smem, whole(w_neigh)],
        [
            sds((sections * groups, room + 8, width), BF),
            sds((sections, ent_rows + 8, features), BF),
        ],
    )
    recv = a2a(msg, ("hist", "ent")).reshape(sections, groups, room + 8, width)
    xg = a2a(xp, "hist")

    sizes = tuple(
        round_up(-(-rows // groups), 16) for rows in (features, features, half, relations, relations)
    )
    rel_rows = round_up(relations, 8)
    qe = query_ent.reshape(1, -1)
    qr = query_rel.reshape(1, -1)
    top, qp = run(
        query_kernel,
        "query",
        (qe, qr, query_grad),
        [whole(qe), whole(qr), whole(query_grad)],
        [sds((ent_rows, width), F32), sds((rel_rows, width), F32)],
    )

    def prepare(t):
        return run(
            state_kernel,
            "state",
            (recv, xg, w_gate, w_self, bias_row),
            [
                block(recv.shape[1:], t),
                block(xg.shape[1:], t),
                whole(w_gate),
                whole(w_self),
                whole(bias_row),
            ],
            [sds((ent_rows, width), F32)] * 4
            + [sds((slots, ent_rows), BF), sds((ent_rows, slots), BF), sds((8, slots), jnp.int32)],
        )

    parts = (top,)
    totals = None
    collected = [None] * sections
    for t in range(sections - 1, -1, -1):
        al, be, ka, sc, odt, osr, rid = prepare(t)
        ins = (*parts, al, be, ka, sc, odt)
        c, gp, keep, bias, rep = run(
            functools.partial(top_kernel, len(parts)),
            "top",
            ins,
            [whole(x) for x in ins],
            [
                sds((ent_rows, width), F32),
                sds((ent_rows, 2 * width), BF),
                sds((ent_rows, width), F32),
                sds((8, width), F32),
                sds((slots, width), BF),
            ],
        )
        if t + 1 < sections:
            collected[t + 1] = c
        ret = a2a(rep.reshape(groups, room, width), "ent").reshape(slots, width)
        ins = (ret, gp, osr, keep, w_gate, w_self, w_neigh)
        base, sp, *sends = run(
            functools.partial(back_kernel, sections),
            "back",
            ins,
            [whole(x) for x in ins],
            [sds((ent_rows, width), F32), sds((ent_rows, 2 * width), BF)]
            + [sds((ent_rows, width), BF)] * (sections - 1),
        )
        parts = [base] + [
            lax.ppermute(x, "hist", [(i, (i + k + 1) % sections) for i in range(sections)])
            for k, x in enumerate(sends)
        ]
        ins = (xg, gp, sp, ret, rid, bias) + (() if totals is None else tuple(totals))
        totals = run(
            functools.partial(grad_kernel, half, totals is None),
            "grad",
            ins,
            [block(xg.shape[1:], t)] + [whole(x) for x in ins[1:]],
            [
                sds((features, 2 * width), F32),
                sds((half, width), F32),
                sds((rel_rows, width), F32),
                sds((8, width), F32),
            ],
        )
    total = parts[0]
    for p in parts[1:]:
        total = total + p.astype(F32)
    collected[0] = total
    result = a2a(jnp.stack(collected), "hist")
    result = result.transpose(1, 0, 2).reshape(1, ent_rows, features)

    gs, ns, rs, bs = totals
    chunk = sum(sizes) + 16
    ins = (gs, ns, rs, qp, bs)
    (packed,) = run(
        functools.partial(pack_kernel, sizes),
        "pack",
        ins,
        [whole(x) for x in ins],
        [sds((groups, chunk, width), BF)],
    )
    landed = a2a(packed, "ent")
    pairs = groups // 2
    (copies,) = run(
        add_kernel, "sum", (landed,), [whole(landed)], [sds((pairs, chunk, width), BF)]
    )
    same = [[i for i in range(groups) if i % 2 == core] for core in range(2)]
    column = lax.all_to_all(
        copies, "ent", split_axis=0, concat_axis=0, tiled=True, axis_index_groups=same
    )
    rows = [column] + [
        lax.ppermute(column, "hist", [(i, (i + k) % sections) for i in range(sections)])
        for k in range(1, sections)
    ]
    other = lax.ppermute(
        jnp.concatenate(rows, axis=0), "ent", [(i, i ^ 1) for i in range(groups)]
    )
    ins = (*rows, other, w_neigh, relation)
    factor = 1.0 / math.sqrt(sections * ent_rows * groups)
    tall = [size * groups for size in sizes]
    grads = pl.pallas_call(
        functools.partial(last_kernel, sections, groups, sizes, factor),
        name="last",
        grid=(1,),
        in_specs=[whole(x) for x in ins],
        out_specs=[
            block(w_neigh.shape),
            block((tall[1], features)),
            block((tall[0], features)),
            block((8, features)),
            block((relations, features)),
        ],
        out_shape=[
            sds(w_neigh.shape, F32),
            sds((tall[1], features), F32),
            sds((tall[0], features), F32),
            sds((8, features), F32),
            sds((relations, features), F32),
        ],
        scratch_shapes=[
            pltpu.VMEM((tall[3], features), BF),
            pltpu.VMEM((tall[4], features), BF),
            pltpu.VMEM((tall[2], features), F32),
        ],
    )(*ins)
    neigh, self_, gate, bias, rel = grads
    return (
        result,
        neigh,
        self_[:features],
        gate[:features],
        bias[0],
        rel,
    )


def solution(mesh):
    return jax.shard_map(
        on_device,
        mesh=mesh,
        in_specs=(
            P("hist", "ent", None),
            P(),
            P(),
            P(),
            P(),
            P(),
            P("hist", "ent"),
            P("hist", "ent"),
            P("hist", "ent"),
            P("hist", "ent"),
            P("ent"),
            P("ent"),
            P("ent", None),
        ),
        out_specs=(P("hist", "ent", None), P(), P(), P(), P(), P()),
        check_vma=False,
    )
```

profile of v0, /device:TPU:0, one launch (start us, length us, event | category | flops | bytes accessed | tf_op | source)
XLA Modules:
  0.0 221.7 jit_solution(16960191291694503967)
XLA Ops:
  0.6 3.0 %send.1 = (bf16[32,72,128]{2,1,0:T(8,128)(2,1)}, bf16[4,264,512]{2,1,0:T(8,128)(2,1)}) custom-call(bf16[256,512]{1,0:T(8,128)(2,1)} %bitcast.35, bf16[460,512]{1,0:T(8,128)(2,1)} %refs_6_.1, s32[1,512]{1,0:T(1,128)} %src.1, s32[1,512]{1,0:T(1,128)} %dst.1, s32[1,512]{1,0:T(1,128)} %rid.1, s32[1,8]{1,0:T(1,128)} %counts.1, bf16[2,256,256]{2,1,0:T(8,128)(2,1)} %refs_5_.1), custom_call_target="tpu_custom_call" | custom-call | tf_op jit(solution)/shard_map/send/pallas_call | solution.py:42
  3.6 20.6 %all_to_all.45.xp = bf16[4,264,512]{2,1,0:T(8,128)(2,1)} all-to-all(bf16[4,264,512]{2,1,0:T(8,128)(2,1)} %get-tuple-element.100), channel_id=1, replica_groups=mesh['hist'=4,'ent'=8] {'hist'}, dimensions={0} | all-to-all | bytes 2162688 | tf_op jit(solution)/shard_map/all_to_all | solution.py:313
  24.3 4.3 %all-to-all-start = ((bf16[32,72,128]{2,1,0:T(8,128)(2,1)}), bf16[32,72,128]{2,1,0:T(8,128)(2,1)S(1)}, u32[]{:S(2)}, u32[]{:S(2)}) async-start(bf16[32,72,128]{2,1,0:T(8,128)(2,1)} %get-tuple-element.99), calls=%async_computation | async-start | bytes 1179648 | tf_op jit(solution)/shard_map/all_to_all | solution.py:313
  30.7 15.5 %all-to-all-done = bf16[32,72,128]{2,1,0:T(8,128)(2,1)S(1)} async-done(((bf16[32,72,128]{2,1,0:T(8,128)(2,1)}), bf16[32,72,128]{2,1,0:T(8,128)(2,1)S(1)}, u32[]{:S(2)}, u32[]{:S(2)}) %all-to-all-start) | async-done | bytes 589856 | tf_op jit(solution)/shard_map/all_to_all | solution.py:313
  47.0 2.7 %state.4 = (f32[256,128]{1,0:T(8,128)}, f32[256,128]{1,0:T(8,128)}, f32[256,128]{1,0:T(8,128)}, f32[256,128]{1,0:T(8,128)}, bf16[512,256]{1,0:T(8,128)(2,1)}, /*...) custom-call(bf16[4,8,72,128]{3,2,1,0:T(8,128)(2,1)} %bitcast.21, bf16[4,264,512]{2,1,0:T(8,128)(2,1)} %all_to_all.45.xp, ...), custom_call_target="tpu_custom_call" | custom-call | tf_op jit(solution)/shard_map/state/pallas_call | solution.py:42
  51.8 10.7 %all_to_all.46 = bf16[8,64,128]{2,1,0:T(8,128)(2,1)} all-to-all(bf16[8,64,128]{2,1,0:T(8,128)(2,1)} %bitcast.39), channel_id=1, replica_groups=mesh['hist'=4,'ent'=8] {'ent'}, dimensions={0} | all-to-all | bytes 262144 | tf_op jit(solution)/shard_map/all_to_all | solution.py:313
  62.6 2.6 %back.4 = (f32[256,128]{1,0:T(8,128)}, bf16[256,256]{1,0:T(8,128)(2,1)}, bf16[256,128]{1,0:T(8,128)(2,1)}, bf16[256,128]{1,0:T(8,128)(2,1)}, bf16[256,128]{1,0:T(8,128)(2,1)}) custom-call(bf16[512,128]{1,0:T(8,128)(2,1)} %bitcast.27, bf16[256,256]{1,0:T(8,128)(2,1)} %get-tuple-element.107.gp, bf16[256,512]{1,0:T(8,128)(2,1)} %get-tuple-element.108.osr, ...), custom_call_target="tpu_custom_call" | custom-call | tf_op jit(solution)/shard_map/back/pallas_call | solution.py:42
  66.3 2.3 %collective-permute-start.2 = (bf16[256,128]{1,0:T(8,128)(2,1)}, bf16[256,128]{1,0:T(8,128)(2,1)S(1)}, u32[]{:S(2)}, u32[]{:S(2)}) collective-permute-start(bf16[256,128]{1,0:T(8,128)(2,1)} %get-tuple-element.113), channel_id=1, source_target_pairs={{0,24},{8,0},{16,8},{24,16},{1,25},{9,1},{17,9},{25,17},{2,26},{10... | collective-permute-start | bytes 196616 | tf_op jit(solution)/shard_map/ppermute | solution.py:390
  68.7 2.7 %state.5 = (f32[256,128]{1,0:T(8,128)}, f32[256,128]{1,0:T(8,128)}, f32[256,128]{1,0:T(8,128)}, f32[256,128]{1,0:T(8,128)}, bf16[512,256]{1,0:T(8,128)(2,1)}, /*...) custom-call(bf16[4,8,72,128]{3,2,1,0:T(8,128)(2,1)} %bitcast.22, bf16[4,264,512]{2,1,0:T(8,128)(2,1)} %all_to_all.45.xp, ...), custom_call_target="tpu_custom_call" | custom-call | tf_op jit(solution)/shard_map/state/pallas_call | solution.py:42
  74.3 10.7 %all_to_all.47 = bf16[8,64,128]{2,1,0:T(8,128)(2,1)} all-to-all(bf16[8,64,128]{2,1,0:T(8,128)(2,1)} %bitcast.37), channel_id=1, replica_groups=mesh['hist'=4,'ent'=8] {'ent'}, dimensions={0} | all-to-all | bytes 262144 | tf_op jit(solution)/shard_map/all_to_all | solution.py:313
  85.0 2.7 %back.5 = (f32[256,128]{1,0:T(8,128)}, bf16[256,256]{1,0:T(8,128)(2,1)}, bf16[256,128]{1,0:T(8,128)(2,1)}, bf16[256,128]{1,0:T(8,128)(2,1)}, bf16[256,128]{1,0:T(8,128)(2,1)}) custom-call(bf16[512,128]{1,0:T(8,128)(2,1)} %bitcast.29, bf16[256,256]{1,0:T(8,128)(2,1)} %get-tuple-element.120.gp, bf16[256,512]{1,0:T(8,128)(2,1)} %get-tuple-element.121.osr, ...), custom_call_target="tpu_custom_call" | custom-call | tf_op jit(solution)/shard_map/back/pallas_call | solution.py:42
  87.7 2.7 %collective-permute-start.3 = (bf16[256,128]{1,0:T(8,128)(2,1)}, bf16[256,128]{1,0:T(8,128)(2,1)S(1)}, u32[]{:S(2)}, u32[]{:S(2)}) collective-permute-start(bf16[256,128]{1,0:T(8,128)(2,1)} %get-tuple-element.124), channel_id=1, source_target_pairs={{0,8},{8,16},{16,24},{24,0},{1,9},{9,17},{17,25},{25,1},{2,10},{10... | collective-permute-start | bytes 196616 | tf_op jit(solution)/shard_map/ppermute | solution.py:390
  92.1 2.7 %state.6 = (f32[256,128]{1,0:T(8,128)}, f32[256,128]{1,0:T(8,128)}, f32[256,128]{1,0:T(8,128)}, f32[256,128]{1,0:T(8,128)}, bf16[512,256]{1,0:T(8,128)(2,1)}, /*...) custom-call(bf16[4,8,72,128]{3,2,1,0:T(8,128)(2,1)} %bitcast.23, bf16[4,264,512]{2,1,0:T(8,128)(2,1)} %all_to_all.45.xp, ...), custom_call_target="tpu_custom_call" | custom-call | tf_op jit(solution)/shard_map/state/pallas_call | solution.py:42
  96.0 2.2 %top.6 = (f32[256,128]{1,0:T(8,128)}, bf16[256,256]{1,0:T(8,128)(2,1)}, f32[256,128]{1,0:T(8,128)}, f32[8,128]{1,0:T(8,128)}, bf16[512,128]{1,0:T(8,128)(2,1)}) custom-call(f32[256,128]{1,0:T(8,128)} %get-tuple-element.123.refs_0_, bf16[256,128]{1,0:T(8,128)(2,1)} %copy-done.13, bf16[256,128]{1,0:T(8,128)(2,1)} %copy-done.16, bf16[256,128]{1,0:T(8,128)(2,1)} %copy-done.19, ...), custom_call_target="tpu_custom_call" | custom-call | tf_op jit(solution)/shard_map/top/pallas_call | solution.py:42
  98.2 10.7 %all_to_all.48 = bf16[8,64,128]{2,1,0:T(8,128)(2,1)} all-to-all(bf16[8,64,128]{2,1,0:T(8,128)(2,1)} %bitcast.38), channel_id=1, replica_groups=mesh['hist'=4,'ent'=8] {'ent'}, dimensions={0} | all-to-all | bytes 262144 | tf_op jit(solution)/shard_map/all_to_all | solution.py:313
  108.9 2.7 %back.6 = (f32[256,128]{1,0:T(8,128)}, bf16[256,256]{1,0:T(8,128)(2,1)}, bf16[256,128]{1,0:T(8,128)(2,1)}, bf16[256,128]{1,0:T(8,128)(2,1)}, bf16[256,128]{1,0:T(8,128)(2,1)}) custom-call(bf16[512,128]{1,0:T(8,128)(2,1)} %bitcast.31, bf16[256,256]{1,0:T(8,128)(2,1)} %get-tuple-element.133.gp, bf16[256,512]{1,0:T(8,128)(2,1)} %get-tuple-element.134.osr, ...), custom_call_target="tpu_custom_call" | custom-call | tf_op jit(solution)/shard_map/back/pallas_call | solution.py:42
  116.0 2.7 %state.7 = (f32[256,128]{1,0:T(8,128)}, f32[256,128]{1,0:T(8,128)}, f32[256,128]{1,0:T(8,128)}, f32[256,128]{1,0:T(8,128)}, bf16[512,256]{1,0:T(8,128)(2,1)}, /*...) custom-call(bf16[4,8,72,128]{3,2,1,0:T(8,128)(2,1)} %bitcast.24, bf16[4,264,512]{2,1,0:T(8,128)(2,1)} %all_to_all.45.xp, ...), custom_call_target="tpu_custom_call" | custom-call | tf_op jit(solution)/shard_map/state/pallas_call | solution.py:42
  121.6 3.4 %all-to-all-start.5 = ((bf16[8,64,128]{2,1,0:T(8,128)(2,1)}), bf16[8,64,128]{2,1,0:T(8,128)(2,1)S(1)}, u32[]{:S(2)}, u32[]{:S(2)}) async-start(bf16[8,64,128]{2,1,0:T(8,128)(2,1)} %bitcast.36), calls=%async_computation.5 | async-start | bytes 262144 | tf_op jit(solution)/shard_map/all_to_all | solution.py:313
  125.0 2.3 %grad.4 = (f32[512,256]{1,0:T(8,128)}, f32[256,128]{1,0:T(8,128)}, f32[464,128]{1,0:T(8,128)}, f32[8,128]{1,0:T(8,128)}) custom-call(bf16[4,264,512]{2,1,0:T(8,128)(2,1)} %all_to_all.45.xp, bf16[256,256]{1,0:T(8,128)(2,1)} %get-tuple-element.107.gp, bf16[256,256]{1,0:T(8,128)(2,1)} %get-tuple-element.165.sp, bf16[512,128]{1,0:T(8,128)(2,1)} %bitcast.28, ...), custom_call_target="tpu_custom_call" | custom-call | tf_op jit(solution)/shard_map/grad/pallas_call | solution.py:42
  127.3 2.7 %grad.5 = (f32[512,256]{1,0:T(8,128)}, f32[256,128]{1,0:T(8,128)}, f32[464,128]{1,0:T(8,128)}, f32[8,128]{1,0:T(8,128)}) custom-call(bf16[4,264,512]{2,1,0:T(8,128)(2,1)} %all_to_all.45.xp, bf16[256,256]{1,0:T(8,128)(2,1)} %get-tuple-element.120.gp, bf16[256,256]{1,0:T(8,128)(2,1)} %get-tuple-element.162.sp, bf16[512,128]{1,0:T(8,128)(2,1)} %bitcast.30, ...), custom_call_target="tpu_custom_call" | custom-call | tf_op jit(solution)/shard_map/grad/pallas_call | solution.py:42
  130.0 2.7 %grad.6 = (f32[512,256]{1,0:T(8,128)}, f32[256,128]{1,0:T(8,128)}, f32[464,128]{1,0:T(8,128)}, f32[8,128]{1,0:T(8,128)}) custom-call(bf16[4,264,512]{2,1,0:T(8,128)(2,1)} %all_to_all.45.xp, bf16[256,256]{1,0:T(8,128)(2,1)} %get-tuple-element.133.gp, bf16[256,256]{1,0:T(8,128)(2,1)} %get-tuple-element.159.sp, bf16[512,128]{1,0:T(8,128)(2,1)} %bitcast.32, ...), custom_call_target="tpu_custom_call" | custom-call | tf_op jit(solution)/shard_map/grad/pallas_call | solution.py:42
  133.3 2.7 %back.7 = (f32[256,128]{1,0:T(8,128)}, bf16[256,256]{1,0:T(8,128)(2,1)}, bf16[256,128]{1,0:T(8,128)(2,1)}, bf16[256,128]{1,0:T(8,128)(2,1)}, bf16[256,128]{1,0:T(8,128)(2,1)}) custom-call(bf16[512,128]{1,0:T(8,128)(2,1)} %bitcast.33, bf16[256,256]{1,0:T(8,128)(2,1)} %get-tuple-element.146.gp, bf16[256,512]{1,0:T(8,128)(2,1)} %get-tuple-element.147.osr, ...), custom_call_target="tpu_custom_call" | custom-call | tf_op jit(solution)/shard_map/back/pallas_call | solution.py:42
  136.0 2.7 %grad.7 = (f32[512,256]{1,0:T(8,128)}, f32[256,128]{1,0:T(8,128)}, f32[464,128]{1,0:T(8,128)}, f32[8,128]{1,0:T(8,128)}) custom-call(bf16[4,264,512]{2,1,0:T(8,128)(2,1)} %all_to_all.45.xp, bf16[256,256]{1,0:T(8,128)(2,1)} %get-tuple-element.146.gp, bf16[256,256]{1,0:T(8,128)(2,1)} %get-tuple-element.156.sp, bf16[512,128]{1,0:T(8,128)(2,1)} %bitcast.34, ...), custom_call_target="tpu_custom_call" | custom-call | tf_op jit(solution)/shard_map/grad/pallas_call | solution.py:42
  140.8 22.6 %all_to_all.49.x = bf16[8,304,128]{2,1,0:T(8,128)(2,1)} all-to-all(bf16[8,304,128]{2,1,0:T(8,128)(2,1)} %pack.1), channel_id=1, replica_groups=mesh['hist'=4,'ent'=8] {'ent'}, dimensions={0} | all-to-all | bytes 1245184 | tf_op jit(solution)/shard_map/all_to_all | solution.py:313
  165.2 13.5 %all_to_all.50.refs_0_ = bf16[4,304,128]{2,1,0:T(8,128)(2,1)S(1)} all-to-all(bf16[4,304,128]{2,1,0:T(8,128)(2,1)} %sum.1), channel_id=1, replica_groups={{0,2,4,6},{1,3,5,7},{8,10,12,14},{9,11,13,15},{16,18,20,22},{17,19,21,2..., dimensions={0} | all-to-all | bytes 622592 | tf_op jit(solution)/shard_map/all_to_all | solution.py:429
  178.8 2.7 %collective-permute-start.14 = (bf16[4,304,128]{2,1,0:T(8,128)(2,1)S(1)}, bf16[4,304,128]{2,1,0:T(8,128)(2,1)S(1)}, u32[]{:S(2)}, u32[]{:S(2)}) collective-permute-start(bf16[4,304,128]{2,1,0:T(8,128)(2,1)S(1)} %all_to_all.50.refs_0_), channel_id=1, source_target_pairs={{0,24},{8,0},{16,8},{24,16},{1,25},{9,1},{17,9},{25,17},{2,26},{10... | collective-permute-start | bytes 933896 | tf_op jit(solution)/shard_map/ppermute | solution.py:433
  182.1 7.1 %collective-permute-done.14.refs_3_ = bf16[4,304,128]{2,1,0:T(8,128)(2,1)S(1)} collective-permute-done((bf16[4,304,128]{2,1,0:T(8,128)(2,1)S(1)}, bf16[4,304,128]{2,1,0:T(8,128)(2,1)S(1)}, u32[]{:S(2)}, u32[]{:S(2)}) %collective-permute-start.14) | collective-permute-done | bytes 311328 | tf_op jit(solution)/shard_map/ppermute | solution.py:433
  189.2 6.4 %collective-permute-done.13.refs_2_ = bf16[4,304,128]{2,1,0:T(8,128)(2,1)S(1)} collective-permute-done((bf16[4,304,128]{2,1,0:T(8,128)(2,1)S(1)}, bf16[4,304,128]{2,1,0:T(8,128)(2,1)S(1)}, u32[]{:S(2)}, u32[]{:S(2)}) %collective-permute-start.13) | collective-permute-done | bytes 311328 | tf_op jit(solution)/shard_map/ppermute | solution.py:433
  197.4 2.5 %collective-permute-start.11 = (bf16[256,128]{1,0:T(8,128)(2,1)S(1)}, bf16[256,128]{1,0:T(8,128)(2,1)S(1)}, u32[]{:S(2)}, u32[]{:S(2)}) collective-permute-start(bf16[256,128]{1,0:T(8,128)(2,1)S(1)} %copy-done.20), channel_id=1, source_target_pairs={{0,24},{8,0},{16,8},{24,16},{1,25},{9,1},{17,9},{25,17},{2,26},{10... | collective-permute-start | bytes 196616 | tf_op jit(solution)/shard_map/ppermute | solution.py:390
  199.9 2.4 %collective-permute-done.9 = bf16[256,128]{1,0:T(8,128)(2,1)S(1)} collective-permute-done((bf16[256,128]{1,0:T(8,128)(2,1)S(1)}, bf16[256,128]{1,0:T(8,128)(2,1)S(1)}, u32[]{:S(2)}, u32[]{:S(2)}) %collective-permute-start.9) | collective-permute-done | bytes 65568 | tf_op jit(solution)/shard_map/ppermute | solution.py:390
  202.6 11.3 %all_to_all.51 = f32[4,256,128]{2,1,0:T(8,128)S(1)} all-to-all(f32[4,256,128]{2,1,0:T(8,128)S(1)} %pad_maximum_fusion.1), channel_id=1, replica_groups=mesh['hist'=4,'ent'=8] {'hist'}, dimensions={0} | all-to-all | bytes 1048576 | tf_op jit(solution)/shard_map/all_to_all | solution.py:313
  216.1 4.3 %last.1 = (f32[2,256,256]{2,1,0:T(8,128)}, f32[512,512]{1,0:T(8,128)}, f32[512,512]{1,0:T(8,128)}, f32[8,512]{1,0:T(8,128)}, f32[460,512]{1,0:T(8,128)}) custom-call(bf16[4,304,128]{2,1,0:T(8,128)(2,1)} %copy-done.1, bf16[4,304,128]{2,1,0:T(8,128)(2,1)} %copy-done.5, bf16[4,304,128]{2,1,0:T(8,128)(2,1)} %copy-done.4, bf16[4,304,128]{2,1,0:T(8,128)(2,1)} %copy-done.3, ...), custom_call_target="tpu_custom_call" | custom-call | tf_op jit(solution)/shard_map/last/pallas_call | solution.py:442
  (84 shorter events, 30.1 us)
Async XLA Ops:
  24.3 21.9 %all-to-all-start = ((bf16[32,72,128]{2,1,0:T(8,128)(2,1)}), bf16[32,72,128]{2,1,0:T(8,128)(2,1)S(1)}, u32[]{:S(2)}, u32[]{:S(2)}) async-start(bf16[32,72,128]{2,1,0:T(8,128)(2,1)} %get-tuple-element.99), calls=%async_computation | async-start | bytes 1179648 | tf_op jit(solution)/shard_map/all_to_all | solution.py:313
  46.2 0.8 copy-start
  65.2 6.2 %collective-permute-start = (bf16[256,128]{1,0:T(8,128)(2,1)}, bf16[256,128]{1,0:T(8,128)(2,1)S(1)}, u32[]{:S(2)}, u32[]{:S(2)}) collective-permute-start(bf16[256,128]{1,0:T(8,128)(2,1)} %get-tuple-element.111), channel_id=1, source_target_pairs={{0,8},{8,16},{16,24},{24,0},{1,9},{9,17},{17,25},{25,1},{2,10},{10... | collective-permute-start | bytes 196616 | tf_op jit(solution)/shard_map/ppermute | solution.py:390
  65.2 6.2 %collective-permute-start.1 = (bf16[256,128]{1,0:T(8,128)(2,1)}, bf16[256,128]{1,0:T(8,128)(2,1)S(1)}, u32[]{:S(2)}, u32[]{:S(2)}) collective-permute-start(bf16[256,128]{1,0:T(8,128)(2,1)} %get-tuple-element.112), channel_id=1, source_target_pairs={{0,16},{8,24},{16,0},{24,8},{1,17},{9,25},{17,1},{25,9},{2,18},{10... | collective-permute-start | bytes 196616 | tf_op jit(solution)/shard_map/ppermute | solution.py:390
  66.3 5.1 %collective-permute-start.2 = (bf16[256,128]{1,0:T(8,128)(2,1)}, bf16[256,128]{1,0:T(8,128)(2,1)S(1)}, u32[]{:S(2)}, u32[]{:S(2)}) collective-permute-start(bf16[256,128]{1,0:T(8,128)(2,1)} %get-tuple-element.113), channel_id=1, source_target_pairs={{0,24},{8,0},{16,8},{24,16},{1,25},{9,1},{17,9},{25,17},{2,26},{10... | collective-permute-start | bytes 196616 | tf_op jit(solution)/shard_map/ppermute | solution.py:390
  87.7 7.1 %collective-permute-start.3 = (bf16[256,128]{1,0:T(8,128)(2,1)}, bf16[256,128]{1,0:T(8,128)(2,1)S(1)}, u32[]{:S(2)}, u32[]{:S(2)}) collective-permute-start(bf16[256,128]{1,0:T(8,128)(2,1)} %get-tuple-element.124), channel_id=1, source_target_pairs={{0,8},{8,16},{16,24},{24,0},{1,9},{9,17},{17,25},{25,1},{2,10},{10... | collective-permute-start | bytes 196616 | tf_op jit(solution)/shard_map/ppermute | solution.py:390
  90.3 4.5 %collective-permute-start.4 = (bf16[256,128]{1,0:T(8,128)(2,1)}, bf16[256,128]{1,0:T(8,128)(2,1)S(1)}, u32[]{:S(2)}, u32[]{:S(2)}) collective-permute-start(bf16[256,128]{1,0:T(8,128)(2,1)} %get-tuple-element.125), channel_id=1, source_target_pairs={{0,16},{8,24},{16,0},{24,8},{1,17},{9,25},{17,1},{25,9},{2,18},{10... | collective-permute-start | bytes 196616 | tf_op jit(solution)/shard_map/ppermute | solution.py:390
  90.8 4.5 %collective-permute-start.5 = (bf16[256,128]{1,0:T(8,128)(2,1)}, bf16[256,128]{1,0:T(8,128)(2,1)S(1)}, u32[]{:S(2)}, u32[]{:S(2)}) collective-permute-start(bf16[256,128]{1,0:T(8,128)(2,1)} %get-tuple-element.126), channel_id=1, source_target_pairs={{0,24},{8,0},{16,8},{24,16},{1,25},{9,1},{17,9},{25,17},{2,26},{10... | collective-permute-start | bytes 196616 | tf_op jit(solution)/shard_map/ppermute | solution.py:390
  111.6 7.1 %collective-permute-start.6 = (bf16[256,128]{1,0:T(8,128)(2,1)}, bf16[256,128]{1,0:T(8,128)(2,1)S(1)}, u32[]{:S(2)}, u32[]{:S(2)}) collective-permute-start(bf16[256,128]{1,0:T(8,128)(2,1)} %get-tuple-element.137), channel_id=1, source_target_pairs={{0,8},{8,16},{16,24},{24,0},{1,9},{9,17},{17,25},{25,1},{2,10},{10... | collective-permute-start | bytes 196616 | tf_op jit(solution)/shard_map/ppermute | solution.py:390
  112.8 5.9 %collective-permute-start.7 = (bf16[256,128]{1,0:T(8,128)(2,1)}, bf16[256,128]{1,0:T(8,128)(2,1)S(1)}, u32[]{:S(2)}, u32[]{:S(2)}) collective-permute-start(bf16[256,128]{1,0:T(8,128)(2,1)} %get-tuple-element.138), channel_id=1, source_target_pairs={{0,16},{8,24},{16,0},{24,8},{1,17},{9,25},{17,1},{25,9},{2,18},{10... | collective-permute-start | bytes 196616 | tf_op jit(solution)/shard_map/ppermute | solution.py:390
  114.3 4.5 %collective-permute-start.8 = (bf16[256,128]{1,0:T(8,128)(2,1)}, bf16[256,128]{1,0:T(8,128)(2,1)S(1)}, u32[]{:S(2)}, u32[]{:S(2)}) collective-permute-start(bf16[256,128]{1,0:T(8,128)(2,1)} %get-tuple-element.139), channel_id=1, source_target_pairs={{0,24},{8,0},{16,8},{24,16},{1,25},{9,1},{17,9},{25,17},{2,26},{10... | collective-permute-start | bytes 196616 | tf_op jit(solution)/shard_map/ppermute | solution.py:390
  121.6 11.0 %all-to-all-start.5 = ((bf16[8,64,128]{2,1,0:T(8,128)(2,1)}), bf16[8,64,128]{2,1,0:T(8,128)(2,1)S(1)}, u32[]{:S(2)}, u32[]{:S(2)}) async-start(bf16[8,64,128]{2,1,0:T(8,128)(2,1)} %bitcast.36), calls=%async_computation.5 | async-start | bytes 262144 | tf_op jit(solution)/shard_map/all_to_all | solution.py:313
  132.7 0.6 copy-start.6
  178.7 17.1 %copy-start.1 = (bf16[4,304,128]{2,1,0:T(8,128)(2,1)}, bf16[4,304,128]{2,1,0:T(8,128)(2,1)S(1)}, u32[]{:S(2)}) copy-start(bf16[4,304,128]{2,1,0:T(8,128)(2,1)S(1)} %all_to_all.50.refs_0_) | copy-start | bytes 933892
  178.7 17.7 %copy-start.22 = (bf16[256,128]{1,0:T(8,128)(2,1)S(1)}, bf16[256,128]{1,0:T(8,128)(2,1)}, u32[]{:S(2)}) copy-start(bf16[256,128]{1,0:T(8,128)(2,1)} %get-tuple-element.150) | copy-start | bytes 196612
  178.7 17.9 %copy-start.21 = (bf16[256,128]{1,0:T(8,128)(2,1)S(1)}, bf16[256,128]{1,0:T(8,128)(2,1)}, u32[]{:S(2)}) copy-start(bf16[256,128]{1,0:T(8,128)(2,1)} %get-tuple-element.151) | copy-start | bytes 196612
  178.7 18.7 %copy-start.20 = (bf16[256,128]{1,0:T(8,128)(2,1)S(1)}, bf16[256,128]{1,0:T(8,128)(2,1)}, u32[]{:S(2)}) copy-start(bf16[256,128]{1,0:T(8,128)(2,1)} %get-tuple-element.152) | copy-start | bytes 196612
  178.7 23.7 %copy-start.7 = (f32[256,128]{1,0:T(8,128)S(1)}, f32[256,128]{1,0:T(8,128)}, u32[]{:S(2)}) copy-start(f32[256,128]{1,0:T(8,128)} %get-tuple-element.149) | copy-start | bytes 393220
  178.7 23.7 %copy-start.8 = (f32[256,128]{1,0:T(8,128)S(1)}, f32[256,128]{1,0:T(8,128)}, u32[]{:S(2)}) copy-start(f32[256,128]{1,0:T(8,128)} %get-tuple-element.155) | copy-start | bytes 393220
  178.7 23.7 %copy-start.9 = (f32[256,128]{1,0:T(8,128)S(1)}, f32[256,128]{1,0:T(8,128)}, u32[]{:S(2)}) copy-start(f32[256,128]{1,0:T(8,128)} %get-tuple-element.154) | copy-start | bytes 393220
  178.8 23.7 %copy-start.10 = (f32[256,128]{1,0:T(8,128)S(1)}, f32[256,128]{1,0:T(8,128)}, u32[]{:S(2)}) copy-start(f32[256,128]{1,0:T(8,128)} %get-tuple-element.153) | copy-start | bytes 393220
  178.8 10.4 %collective-permute-start.14 = (bf16[4,304,128]{2,1,0:T(8,128)(2,1)S(1)}, bf16[4,304,128]{2,1,0:T(8,128)(2,1)S(1)}, u32[]{:S(2)}, u32[]{:S(2)}) collective-permute-start(bf16[4,304,128]{2,1,0:T(8,128)(2,1)S(1)} %all_to_all.50.refs_0_), channel_id=1, source_target_pairs={{0,24},{8,0},{16,8},{24,16},{1,25},{9,1},{17,9},{25,17},{2,26},{10... | collective-permute-start | bytes 933896 | tf_op jit(solution)/shard_map/ppermute | solution.py:433
  181.4 14.2 %collective-permute-start.13 = (bf16[4,304,128]{2,1,0:T(8,128)(2,1)S(1)}, bf16[4,304,128]{2,1,0:T(8,128)(2,1)S(1)}, u32[]{:S(2)}, u32[]{:S(2)}) collective-permute-start(bf16[4,304,128]{2,1,0:T(8,128)(2,1)S(1)} %all_to_all.50.refs_0_), channel_id=1, source_target_pairs={{0,16},{8,24},{16,0},{24,8},{1,17},{9,25},{17,1},{25,9},{2,18},{10... | collective-permute-start | bytes 933896 | tf_op jit(solution)/shard_map/ppermute | solution.py:433
  182.0 13.6 %collective-permute-start.12 = (bf16[4,304,128]{2,1,0:T(8,128)(2,1)S(1)}, bf16[4,304,128]{2,1,0:T(8,128)(2,1)S(1)}, u32[]{:S(2)}, u32[]{:S(2)}) collective-permute-start(bf16[4,304,128]{2,1,0:T(8,128)(2,1)S(1)} %all_to_all.50.refs_0_), channel_id=1, source_target_pairs={{0,8},{8,16},{16,24},{24,0},{1,9},{9,17},{17,25},{25,1},{2,10},{10... | collective-permute-start | bytes 933896 | tf_op jit(solution)/shard_map/ppermute | solution.py:433
  189.2 6.6 %copy-start.3 = (bf16[4,304,128]{2,1,0:T(8,128)(2,1)}, bf16[4,304,128]{2,1,0:T(8,128)(2,1)S(1)}, u32[]{:S(2)}) copy-start(bf16[4,304,128]{2,1,0:T(8,128)(2,1)S(1)} %collective-permute-done.14.refs_3_) | copy-start | bytes 933892
  195.6 0.7 copy-start.4
  195.6 0.8 copy-start.5
  196.4 18.6 %collective-permute-start.15 = (bf16[16,304,128]{2,1,0:T(8,128)(2,1)S(1)}, bf16[16,304,128]{2,1,0:T(8,128)(2,1)S(1)}, u32[]{:S(2)}, u32[]{:S(2)}) collective-permute-start(bf16[16,304,128]{2,1,0:T(8,128)(2,1)S(1)} %pad_maximum_fusion), channel_id=1, source_target_pairs={{0,1},{1,0},{2,3},{3,2},{4,5},{5,4},{6,7},{7,6},{8,9},{9,8},{10,11... | collective-permute-start | bytes 3735560 | tf_op jit(solution)/shard_map/ppermute | solution.py:436
  196.4 5.9 %collective-permute-start.9 = (bf16[256,128]{1,0:T(8,128)(2,1)S(1)}, bf16[256,128]{1,0:T(8,128)(2,1)S(1)}, u32[]{:S(2)}, u32[]{:S(2)}) collective-permute-start(bf16[256,128]{1,0:T(8,128)(2,1)S(1)} %copy-done.22), channel_id=1, source_target_pairs={{0,8},{8,16},{16,24},{24,0},{1,9},{9,17},{17,25},{25,1},{2,10},{10... | collective-permute-start | bytes 196616 | tf_op jit(solution)/shard_map/ppermute | solution.py:390
  196.7 5.8 %collective-permute-start.10 = (bf16[256,128]{1,0:T(8,128)(2,1)S(1)}, bf16[256,128]{1,0:T(8,128)(2,1)S(1)}, u32[]{:S(2)}, u32[]{:S(2)}) collective-permute-start(bf16[256,128]{1,0:T(8,128)(2,1)S(1)} %copy-done.21), channel_id=1, source_target_pairs={{0,16},{8,24},{16,0},{24,8},{1,17},{9,25},{17,1},{25,9},{2,18},{10... | collective-permute-start | bytes 196616 | tf_op jit(solution)/shard_map/ppermute | solution.py:390
  197.4 5.1 %collective-permute-start.11 = (bf16[256,128]{1,0:T(8,128)(2,1)S(1)}, bf16[256,128]{1,0:T(8,128)(2,1)S(1)}, u32[]{:S(2)}, u32[]{:S(2)}) collective-permute-start(bf16[256,128]{1,0:T(8,128)(2,1)S(1)} %copy-done.20), channel_id=1, source_target_pairs={{0,24},{8,0},{16,8},{24,16},{1,25},{9,1},{17,9},{25,17},{2,26},{10... | collective-permute-start | bytes 196616 | tf_op jit(solution)/shard_map/ppermute | solution.py:390
  215.1 1.1 copy-start.2
  (9 other events, 5.6 us)
where the time goes:
time: 223 us; the launch traced here: 222 us
  blocking collectives  100 us (45%)
  Pallas kernels  54.1 us (24%)
  waiting for transfers between devices  32.1 us (14%)
  starting transfers between devices  26.7 us (12%)
  local copies, waits for them, and re-layouts  7.6 us (3%)
    all_to_all x6, blocking collectives, a2a(): return lax.all_to_all(x, axes, split_axis=0, concat_axis=0, tiled=True)  86.7 us
    pallas_call x20, Pallas kernels, run(): pl.pallas_call(body, name=name, grid=(1,), in_specs=specs, out_specs=[blo...  49.8 us
    ppermute x12, starting transfers between devices, on_device(): lax.ppermute(x, 'hist', [(i, (i + k + 1) % sections) for i in range(secti...  15.7 us
    all_to_all x2, waiting for transfers between devices, a2a(): return lax.all_to_all(x, axes, split_axis=0, concat_axis=0, tiled=True)  15.5 us
    ppermute x3, waiting for transfers between devices, on_device(): lax.ppermute(column, 'hist', [(i, (i + k) % sections) for i in range(sect...  13.5 us
    all_to_all x1, blocking collectives, on_device(): lax.all_to_all(copies, 'ent', split_axis=0, concat_axis=0, tiled=True, ax...  13.5 us
    all_to_all x2, starting transfers between devices, a2a(): return lax.all_to_all(x, axes, split_axis=0, concat_axis=0, tiled=True)  7.63 us
    unnamed x47, local copies, waits for them, and re-layouts  6.11 us
  transfers between devices with their start and end apart: 18, of which 6 were waited for; matrix products, arithmetic and copies ran while one was open for 1% of the time, Pallas kernels for 8%

commit v1 on v0

v1 whole, which is shorter than its diff:
```python
import functools
import math

import jax
import jax.numpy as jnp
from jax import lax
from jax.experimental import pallas as pl
from jax.experimental.pallas import tpu as pltpu
from jax.sharding import PartitionSpec as P

BF = jnp.bfloat16
F32 = jnp.float32
TALL = (((0,), (0,)), ((), ()))
WIDE = (((1,), (1,)), ((), ()))
LANES = 128


def dot(a, b, dims=(((1,), (0,)), ((), ()))):
    return lax.dot_general(a, b, dims, preferred_element_type=F32)


def onehot(ids, rows):
    spot = lax.broadcasted_iota(jnp.int32, (rows, ids.shape[1]), 0)
    return jnp.where(spot == ids, 1.0, 0.0).astype(BF)


def round_up(value, step):
    return -(-value // step) * step


def block(shape, lead=None):
    if lead is None:
        return pl.BlockSpec(shape, lambda i: (0,) * len(shape))
    return pl.BlockSpec((None,) + shape, lambda i: (lead,) + (0,) * len(shape))


def whole(x):
    return block(x.shape)


def run(body, name, ins, specs, outs, scratch=()):
    return pl.pallas_call(
        body,
        name=name,
        grid=(1,),
        in_specs=specs,
        out_specs=[block(s.shape) for s in outs],
        out_shape=outs,
        scratch_shapes=list(scratch),
    )(*ins)


def sds(shape, dtype):
    return jax.ShapeDtypeStruct(shape, dtype)


def place(value, size):
    return pl.ds(pl.multiple_of(value * size, size), size)


def pre_kernel(x, src, rid, xp):
    ent_rows, features = x.shape
    ids = src[...]
    rids = rid[...]
    extra = jnp.zeros((8, features), F32)
    level = lax.broadcasted_iota(jnp.int32, (8, features), 0)
    for k in range(src.shape[1] // features):
        cut = slice(k * features, (k + 1) * features)
        for j, piece in enumerate((ids[:, cut], rids[:, cut] // 256, rids[:, cut] % 256)):
            extra = jnp.where(level == 3 * k + j, piece.astype(F32), extra)
    xp[:ent_rows, :] = x[...]
    xp[ent_rows:, :] = extra.astype(BF)


def send_kernel(sections, groups, x, rel, src, dst, rid, counts, msg):
    ent_rows, features = x.shape
    slots = src.shape[1]
    room = slots // groups
    width = features // sections
    e = lax.axis_index("ent")
    ids = src[...]
    rids = rid[...]
    xv = x[...]
    got = dot(onehot(ids, ent_rows), xv, TALL) + dot(onehot(rids, rel.shape[0]), rel[...], TALL)
    inputs = got.astype(BF)
    for target in range(sections):
        for u in range(groups):
            msg[target * groups + u, :room, :] = inputs[
                u * room : (u + 1) * room, target * width : (target + 1) * width
            ]
    lane = lax.broadcasted_iota(jnp.int32, (1, slots), 1)
    limit = jnp.zeros((1, slots), jnp.int32)
    for u in range(groups):
        limit = jnp.where(lane // room == u, counts[0, u], limit)
    live = jnp.where(lane % room < limit, dst[...], -1).astype(F32)
    per = width // room
    seat = lax.broadcasted_iota(jnp.int32, (8, width), 1) // room
    for u in range(groups):
        start = u * room // width * width
        row = jnp.broadcast_to(live[:, start : start + width], (8, width))
        turn = lax.rem(e - u + per * groups, per) * room
        row = pltpu.roll(row, turn, 1)
        row = jnp.where(seat == lax.rem(e, per), row, -1.0).astype(BF)
        for target in range(sections):
            msg[target * groups + u, room:, :] = row

def gather_kernel(count, *refs):
    for t in range(count):
        recv = refs[t]
        od, odt, scaling, summed_out = refs[count + 4 * t : count + 4 * t + 4]
        groups = recv.shape[0]
        width = recv.shape[2]
        room = recv.shape[1] - 8
        ent_rows = od.shape[0]
        per = width // room
        degree = jnp.zeros((ent_rows, width), F32)
        summed = jnp.zeros((ent_rows, width), F32)
        ones = jnp.ones((width, width), BF)
        for g in range(groups // per):
            ids = recv[g * per, room:, :].astype(F32)
            for j in range(1, per):
                ids = jnp.maximum(ids, recv[g * per + j, room:, :].astype(F32))
            hot = onehot(ids[:1].astype(jnp.int32), ent_rows)
            rows = jnp.concatenate([recv[g * per + j, :room, :] for j in range(per)], axis=0)
            summed = summed + dot(hot, rows)
            degree = degree + dot(hot, ones)
            od[:, g * width : (g + 1) * width] = hot
            odt[g * width : (g + 1) * width, :] = hot.astype(F32).T.astype(BF)
        scaling[...] = 1.0 / jnp.maximum(degree, 1.0)
        summed_out[...] = summed


def stacked(recv):
    return jnp.concatenate([recv[i, : recv.shape[1] - 8, :] for i in range(recv.shape[0])], axis=0)


def state_values(mates, xt, scaling, summed, od, mate_rows, wg, ws, wn, bias):
    ent_rows, width = summed.shape
    half = wn.shape[1]
    h = lax.axis_index("hist")
    cols = place(h, width)
    seat = lax.rem(h, mates)
    x = xt[:ent_rows, :]
    gathered = jnp.zeros((ent_rows, width), F32)
    for m in range(mates):
        part = summed[...] if m == 0 else dot(od[...], stacked(mate_rows[m - 1]))
        high = part.astype(BF)
        low = (part - high.astype(F32)).astype(BF)
        source = lax.rem(seat - m + mates, mates)
        w = wn[h * width // half, place(source, width), place(seat, width)]
        gathered = gathered + dot(
            jnp.concatenate([high, low], axis=1), jnp.concatenate([w, w], axis=0)
        )
    pre_act = gathered * scaling + dot(x, ws[:, cols])
    gate_open = jax.nn.sigmoid(dot(x, wg[:, cols]) + bias[:, cols])
    sig = jax.nn.sigmoid(pre_act)
    new_state = pre_act * sig
    shut = 1.0 - gate_open
    return (
        (new_state - xt[:ent_rows, cols].astype(F32)) * gate_open * shut,
        gate_open * (sig * (1.0 + pre_act * (1.0 - sig))),
        shut,
    )


def choose(t, sections, xs, xt):
    h = lax.axis_index("hist")
    for k in range(sections):

        @pl.when(lax.rem(h - k + sections, sections) == t)
        def _():
            xt[...] = xs[k][...]


def index_rows(xt, ent_rows, osr, rid):
    slots = osr.shape[1]
    features = xt.shape[1]
    extra = xt[ent_rows:, :].astype(F32).astype(jnp.int32)
    for k in range(slots // features):
        cut = slice(k * features, (k + 1) * features)
        osr[:, cut] = onehot(extra[3 * k : 3 * k + 1], ent_rows)
        ids = extra[3 * k + 1 : 3 * k + 2] * 256 + extra[3 * k + 2 : 3 * k + 3]
        rid[:, cut] = jnp.broadcast_to(ids, (8, features))


def state_kernel(t, sections, mates, *refs):
    xs = refs[:sections]
    mate_rows = refs[sections : sections + mates - 1]
    scaling, summed, od, wg, ws, wn, bias, al, be, ka, osr, rid, xt = refs[sections + mates - 1 :]
    choose(t, sections, xs, xt)
    values = state_values(mates, xt, scaling[...], summed, od, mate_rows, wg, ws, wn, bias)
    al[...], be[...], ka[...] = values
    index_rows(xt, summed.shape[0], osr, rid)


def query_kernel(qe, qr, qg, top, qp):
    width = top.shape[1]
    h = lax.axis_index("hist")
    grad = qg[:, place(h, width)]
    for ids, out in ((qe, top), (qr, qp)):
        hot = onehot(ids[...], out.shape[0]).astype(F32)
        out[...] = lax.dot_general(
            hot,
            grad,
            (((1,), (0,)), ((), ())),
            precision=lax.Precision.HIGHEST,
            preferred_element_type=F32,
        )


def arrived(parts, ret, osr):
    c = parts[0][...]
    for p in parts[1:]:
        c = c + p[...].astype(F32)
    slots = osr.shape[1]
    for m in range(ret.shape[0] // slots):
        c = c + dot(osr[...], ret[m * slots : (m + 1) * slots, :])
    return c


def step_kernel(sections, mates, first, *refs):
    if first:
        c = refs[0][...]
        refs = refs[1:]
    else:
        c = arrived(refs[:sections], refs[sections], refs[sections + 1])
        refs = refs[sections + 2 :]
    al, be, ka, scaling, odt, wg, ws, wn, c_out, gp, g_out, base, rep, bias, *sends = refs
    width = al.shape[1]
    half = wn.shape[1]
    slots = odt.shape[0]
    h = lax.axis_index("hist")
    gate_term = c * al[...]
    pre_term = c * be[...]
    g = (pre_term * scaling[...]).astype(BF)
    g_out[...] = g
    seat = lax.rem(h, mates)
    w = wn[h * width // half, :, place(seat, width)]
    out = dot(odt[...], dot(g, w, WIDE).astype(BF)).astype(BF)
    for m in range(mates):
        rep[m * slots : (m + 1) * slots, :] = out[:, m * width : (m + 1) * width]
    both = jnp.concatenate([gate_term.astype(BF), pre_term.astype(BF)], axis=1)
    gp[...] = both
    for k in range(sections):
        rows = place(lax.rem(h + k, sections), width)
        right = jnp.concatenate([wg[rows, place(h, width)], ws[rows, place(h, width)]], axis=1)
        out = dot(both, right, WIDE)
        if k == 0:
            base[...] = c * ka[...] + out
        else:
            sends[k - 1][...] = out.astype(BF)
    c_out[...] = c
    bias[...] = jnp.broadcast_to(jnp.sum(gate_term, axis=0, keepdims=True), bias.shape)


def grad_kernel(steps, mates, *refs):
    outs = refs[-3:]
    gs, ns, bs = outs
    deep = 5 + mates
    h = lax.axis_index("hist")
    for t in range(steps):
        xt, gp, bias, odt, g = refs[deep * t : deep * t + 5]
        rows = refs[deep * t + 5 : deep * (t + 1)]
        ent_rows, width = g.shape
        seat = lax.rem(h, mates)

        def put(out, at, value):
            out[at] = value if t == 0 else out[at] + value

        put(gs, ..., dot(xt[:ent_rows, :], gp[...], TALL))
        put(bs, ..., bias[...])
        replies = dot(odt[...], g[...]).astype(BF)
        for m in range(mates):
            source = lax.rem(seat - m + mates, mates)
            put(ns, place(source, width), dot(stacked(rows[m]), replies, TALL))


def rel_sum(count, refs, total):
    for t in range(count):
        ret, rid = refs[2 * t : 2 * t + 2]
        slots = rid.shape[1]
        hot = onehot(rid[:1, :], total.shape[0])
        for m in range(ret.shape[0] // slots):
            total = total + dot(hot, ret[m * slots : (m + 1) * slots, :])
    return total


def rel_kernel(count, *refs):
    old, out = refs[-2:]
    out[...] = rel_sum(count, refs, old[...])


def pack_kernel(sizes, relations, gs, ns, bs, ret, rid, old, mine, other, rs):
    pairs = mine.shape[0]
    width = mine.shape[2]
    core = lax.rem(lax.axis_index("ent"), 2)
    total = rel_sum(1, (ret, rid), old[...])
    level = lax.broadcasted_iota(jnp.int32, total.shape, 0)
    rs[...] = jnp.where(level == relations, bs[:1, :], total)
    pieces = (gs.at[:, :width], gs.at[:, width:], ns, rs)
    for u in range(2 * pairs):
        rows = []
        for piece, size in zip(pieces, sizes):
            deep = piece.shape[0]
            low = min(u * size, deep)
            high = min(low + size, deep)
            if high > low:
                rows.append(piece[low:high, :])
            if high - low < size:
                rows.append(jnp.zeros((size - high + low, width), F32))
        value = jnp.concatenate(rows, axis=0).astype(BF)

        @pl.when(core == u % 2)
        def _():
            mine[u // 2] = value

        @pl.when(core != u % 2)
        def _():
            other[u // 2] = value


def pair_kernel(a, b, out):
    out[...] = (a[...].astype(F32) + b[...].astype(F32)).astype(BF)


def add_kernel(x, out):
    total = x[0].astype(F32)
    for u in range(1, x.shape[0]):
        total = total + x[u].astype(F32)
    for k in range(out.shape[0]):
        out[k] = total.astype(BF)


def pick_kernel(sections, *refs):
    parts = refs[:sections]
    ret, osr = refs[sections : sections + 2]
    saved = refs[sections + 2 : 2 * sections + 1]
    outs = refs[2 * sections + 1 :]
    h = lax.axis_index("hist")
    c = arrived(parts, ret, osr)
    for k in range(sections):
        to = lax.rem(h + k, sections)

        @pl.when(to == 0)
        def _():
            outs[k][...] = c

        for t in range(1, sections):

            @pl.when(to == t)
            def _():
                outs[k][...] = saved[t - 1][...]


def last_kernel(sections, groups, mates, sizes, factor, *refs):
    mine = refs[:sections]
    other = refs[sections : 2 * sections]
    rows = refs[2 * sections : 3 * sections]
    result, neigh, self_, gate, bias, relation, n_all, r_all = refs[3 * sections :]
    width = mine[0].shape[2]
    relations = relation.shape[0]
    h = lax.axis_index("hist")
    core = lax.rem(lax.axis_index("ent"), 2)
    for k in range(sections):
        cols = place(lax.rem(h - k + sections, sections), width)
        result[:, cols] = rows[k][...]
        for z in range(groups // 2):
            for flip, piece in enumerate((mine[k], other[k])):
                u = 2 * z + (core if flip == 0 else 1 - core)
                at = 0
                for out, size in zip((gate, self_, n_all, r_all), sizes):
                    out[place(u, size), cols] = piece[z, at : at + size, :].astype(F32) * factor
                    at += size
    relation[...] = r_all[:relations, :]
    bias[...] = r_all[relations : relations + 1, :]
    half = neigh.shape[1]
    for f in range(sections):
        neigh[f // mates, :, f % mates * width : (f % mates + 1) * width] = n_all[
            :half, f * width : (f + 1) * width
        ]


def on_device(
    states,
    w_neigh,
    w_self,
    w_gate,
    b_gate,
    relation,
    edge_src,
    edge_rel,
    edge_dst,
    send_counts,
    query_ent,
    query_rel,
    query_grad,
):
    groups = lax.axis_size("ent")
    sections = lax.axis_size("hist")
    ent_rows, features = states.shape[1:]
    slots = edge_src.shape[1]
    room = slots // groups
    width = features // sections
    blocks, half = w_neigh.shape[:2]
    mates = sections // blocks
    relations = relation.shape[0]
    hidden = states[0]
    bias_row = b_gate.reshape(1, features)
    smem = pl.BlockSpec(memory_space=pltpu.SMEM)
    members = mates * groups
    block_groups = [list(range(b * members, (b + 1) * members)) for b in range(blocks)]

    def turn(x, k):
        return lax.ppermute(x, "hist", [(i, (i + k) % sections) for i in range(sections)])

    def to_mate(x, m):
        route = [(i, i // mates * mates + (i + m) % mates) for i in range(sections)]
        return lax.ppermute(x, "hist", route)

    def to_core(x):
        return lax.ppermute(x, "ent", [(i, i ^ 1) for i in range(groups)])

    rows_f32 = sds((ent_rows, width), F32)
    rows_bf = sds((ent_rows, width), BF)

    ins = (hidden, edge_src, edge_rel)
    (xp,) = run(
        pre_kernel, "pre", ins, [whole(x) for x in ins], [sds((ent_rows + 8, features), BF)]
    )
    xs = [xp] + [turn(xp, k) for k in range(1, sections)]
    (msg,) = run(
        functools.partial(send_kernel, sections, groups),
        "send",
        (hidden, relation, edge_src, edge_dst, edge_rel, send_counts),
        [whole(hidden), whole(relation)] + [whole(edge_src)] * 3 + [smem],
        [sds((sections * groups, room + 8, width), BF)],
    )
    recv = lax.all_to_all(
        msg, ("hist", "ent"), split_axis=0, concat_axis=0, tiled=True
    ).reshape(sections, groups, room + 8, width)
    last = sections - 1
    tops = recv[last]
    rest = recv[:last]
    mate_tops = [to_mate(tops, m) for m in range(1, mates)]
    mate_rest = [to_mate(rest, m) for m in range(1, mates)]

    rel_rows = round_up(relations + 1, 8)
    qe = query_ent.reshape(1, -1)
    qr = query_rel.reshape(1, -1)
    top, rs = run(
        query_kernel,
        "query",
        (qe, qr, query_grad),
        [whole(qe), whole(qr), whole(query_grad)],
        [rows_f32, sds((rel_rows, width), F32)],
    )

    def gather(arrays, specs, count):
        outs = run(
            functools.partial(gather_kernel, count),
            "gather",
            arrays,
            specs,
            [sds((ent_rows, slots), BF), sds((slots, ent_rows), BF), rows_f32, rows_f32] * count,
        )
        return [outs[4 * t : 4 * t + 4] for t in range(count)]

    gathered = gather(
        (rest,) * last, [block(rest.shape[1:], t) for t in range(last)], last
    ) + gather((tops,), [whole(tops)], 1)

    def pick_t(arrays, tops, t):
        if t == last:
            return list(tops), [whole(x) for x in tops]
        return list(arrays), [block(x.shape[1:], t) for x in arrays]

    def prepare(t):
        od, odt, scaling, summed = gathered[t]
        mate, mate_specs = pick_t(mate_rest, mate_tops, t)
        ins = (scaling, summed, od, w_gate, w_self, w_neigh, bias_row)
        al, be, ka, osr, rid, xt = run(
            functools.partial(state_kernel, t, sections, mates),
            "state",
            (*xs, *mate, *ins),
            [whole(x) for x in xs] + mate_specs + [whole(x) for x in ins],
            [rows_f32] * 3
            + [
                sds((ent_rows, slots), BF),
                sds((8, slots), jnp.int32),
                sds((ent_rows + 8, features), BF),
            ],
        )
        return al, be, ka, scaling, odt, osr, rid, xt

    saved = [None] * (sections + 1)
    grad_ins, grad_specs, rel_ins = [], [], []
    for t in range(last, -1, -1):
        al, be, ka, scaling, odt, osr, rid, xt = prepare(t)
        came = (top,) if t == last else (*parts, ret, osr_before)
        ins = (*came, al, be, ka, scaling, odt, w_gate, w_self, w_neigh)
        c, gp, g, base, rep, bias, *sends = run(
            functools.partial(step_kernel, sections, mates, t == last),
            "step",
            ins,
            [whole(x) for x in ins],
            [rows_f32, sds((ent_rows, 2 * width), BF), rows_bf, rows_f32]
            + [sds((mates * slots, width), BF), sds((8, width), F32)]
            + [rows_bf] * (sections - 1),
        )
        saved[t + 1] = c
        ret = lax.all_to_all(
            rep.reshape(members, room, width),
            ("hist", "ent"),
            split_axis=0,
            concat_axis=0,
            tiled=True,
            axis_index_groups=block_groups,
        ).reshape(mates * slots, width)
        parts = [base] + [turn(x, k + 1) for k, x in enumerate(sends)]
        osr_before = osr
        rows, rows_specs = pick_t((rest, *mate_rest), (tops, *mate_tops), t)
        ins = (xt, gp, bias, odt, g)
        grad_ins += [*ins, *rows]
        grad_specs += [whole(x) for x in ins] + rows_specs
        rel_ins += [ret, rid]

    gs, ns, bs = run(
        functools.partial(grad_kernel, sections, mates),
        "grad",
        grad_ins,
        grad_specs,
        [sds((features, 2 * width), F32), sds((half, width), F32), sds((8, width), F32)],
    )
    ins = (*rel_ins[:-2], rs)
    (rs,) = run(
        functools.partial(rel_kernel, last),
        "rel",
        ins,
        [whole(x) for x in ins],
        [sds((rel_rows, width), F32)],
    )

    ins = (*parts, ret, osr_before, *saved[1:sections])
    picks = run(
        functools.partial(pick_kernel, sections),
        "pick",
        ins,
        [whole(x) for x in ins],
        [rows_f32] * sections,
    )
    home = [picks[0]] + [turn(picks[k], k) for k in range(1, sections)]

    sizes = tuple(
        round_up(-(-rows // groups), 16) for rows in (features, features, half, rel_rows)
    )
    chunk = sum(sizes)
    pairs = groups // 2
    ins = (gs, ns, bs, ret, rid, rs)
    mine, other = run(
        functools.partial(pack_kernel, sizes, relations),
        "pack",
        ins,
        [whole(x) for x in ins],
        [sds((pairs, chunk, width), BF)] * 2,
        [pltpu.VMEM((rel_rows, width), F32)],
    )
    ins = (mine, to_core(other))
    (landed,) = run(
        pair_kernel, "pair", ins, [whole(x) for x in ins], [sds((pairs, chunk, width), BF)]
    )
    same = [[i for i in range(groups) if i % 2 == core] for core in range(2)]

    def a2a_same(x):
        return lax.all_to_all(
            x, "ent", split_axis=0, concat_axis=0, tiled=True, axis_index_groups=same
        )

    landed, home = lax.optimization_barrier((a2a_same(landed), home))
    (copies,) = run(
        add_kernel, "sum", (landed,), [whole(landed)], [sds((pairs, chunk, width), BF)]
    )
    column = a2a_same(copies)
    mine = [column] + [turn(column, k) for k in range(1, sections)]
    other = [to_core(x) for x in mine]
    ins = (*mine, *other, *home)
    factor = 1.0 / math.sqrt(sections * ent_rows * groups)
    tall = [size * groups for size in sizes]
    result, neigh, self_, gate, bias, rel = pl.pallas_call(
        functools.partial(last_kernel, sections, groups, mates, sizes, factor),
        name="last",
        grid=(1,),
        in_specs=[whole(x) for x in ins],
        out_specs=[
            block((ent_rows, features)),
            block(w_neigh.shape),
            block((tall[1], features)),
            block((tall[0], features)),
            block((1, features)),
            block((relations, features)),
        ],
        out_shape=[
            sds((ent_rows, features), F32),
            sds(w_neigh.shape, F32),
            sds((tall[1], features), F32),
            sds((tall[0], features), F32),
            sds((1, features), F32),
            sds((relations, features), F32),
        ],
        scratch_shapes=[
            pltpu.VMEM((tall[2], features), F32),
            pltpu.VMEM((tall[3], features), F32),
        ],
    )(*ins)
    return (
        result[None],
        neigh,
        self_[:features],
        gate[:features],
        bias.reshape(features),
        rel,
    )


def solution(mesh):
    return jax.shard_map(
        on_device,
        mesh=mesh,
        in_specs=(
            P("hist", "ent", None),
            P(),
            P(),
            P(),
            P(),
            P(),
            P("hist", "ent"),
            P("hist", "ent"),
            P("hist", "ent"),
            P("hist", "ent"),
            P("ent"),
            P("ent"),
            P("ent", None),
        ),
        out_specs=(P("hist", "ent", None), P(), P(), P(), P(), P()),
        check_vma=False,
    )
```

time: 223 us -> 182 us (0.82)
  blocking collectives: 100 us -> 11.9 us
  starting transfers between devices: 26.7 us -> 59.4 us
  waiting for transfers between devices: 32.1 us -> 45.1 us
    all_to_all x7 -> x1, blocking collectives: 100 us -> 11.9 us  [a2a_same(): lax.all_to_all(x, 'ent', split_axis=0, concat_axis=0, tiled=True, axis_in...]
    all_to_all x2 -> x6, starting transfers between devices: 7.63 us -> 27.8 us  [the longest x4 16.9 us: on_device(): lax.all_to_all(rep.reshape(members, room, width), ('hist', 'ent'), split_...]
    ppermute x16 -> x28, starting transfers between devices: 19.1 us -> 31.6 us  [the longest x21 29.6 us: turn(): lax.ppermute(x, 'hist', [(i, (i + k) % sections) for i in range(sections)])]
    ppermute x16 -> x28, waiting for transfers between devices: 16.6 us -> 27.4 us  [the longest x21 15.1 us: turn(): lax.ppermute(x, 'hist', [(i, (i + k) % sections) for i in range(sections)])]
    pallas_call x20 -> x19, Pallas kernels: 49.8 us -> 52.4 us  [run(): pl.pallas_call(body, name=name, grid=(1,), in_specs=specs, out_specs=[blo...]
    all_to_all x2 -> x6, waiting for transfers between devices: 15.5 us -> 17.7 us  [the longest x1 11.3 us: on_device(): lax.all_to_all(msg, ('hist', 'ent'), split_axis=0, concat_axis=0, tiled=T...]
    unnamed x47 -> x96, local copies, waits for them, and re-layouts: 6.11 us -> 7.09 us
  transfers between devices with their start and end apart: 18 -> 34, of which waited for: 6 -> 23; matrix products, arithmetic and copies ran while one was open for 1% -> 0% of each run, Pallas kernels for 8% -> 15%
where the time goes in v1:
time: 182 us; the launch traced here: 181 us
  starting transfers between devices  59.4 us (33%)
  Pallas kernels  56.3 us (31%)
  waiting for transfers between devices  45.1 us (25%)
  blocking collectives  11.9 us (7%)
  local copies, waits for them, and re-layouts  7.14 us (4%)
    pallas_call x19, Pallas kernels, run(): pl.pallas_call(body, name=name, grid=(1,), in_specs=specs, out_specs=[blo...  52.4 us
    ppermute x21, starting transfers between devices, turn(): lax.ppermute(x, 'hist', [(i, (i + k) % sections) for i in range(sections)])  29.6 us
    all_to_all x4, starting transfers between devices, on_device(): lax.all_to_all(rep.reshape(members, room, width), ('hist', 'ent'), split_...  16.9 us
    ppermute x21, waiting for transfers between devices, turn(): lax.ppermute(x, 'hist', [(i, (i + k) % sections) for i in range(sections)])  15.1 us
    all_to_all x1, blocking collectives, a2a_same(): lax.all_to_all(x, 'ent', split_axis=0, concat_axis=0, tiled=True, axis_in...  11.9 us
    all_to_all x1, waiting for transfers between devices, on_device(): lax.all_to_all(msg, ('hist', 'ent'), split_axis=0, concat_axis=0, tiled=T...  11.3 us
    ppermute x2, waiting for transfers between devices, to_mate(): return lax.ppermute(x, 'hist', route)  9.15 us
    all_to_all x1, starting transfers between devices, on_device(): lax.all_to_all(msg, ('hist', 'ent'), split_axis=0, concat_axis=0, tiled=T...  7.33 us
  transfers between devices with their start and end apart: 34, of which 23 were waited for; matrix products, arithmetic and copies ran while one was open for 0% of the time, Pallas kernels for 15%

profile of v1, /device:TPU:0, one launch (start us, length us, event | category | flops | bytes accessed | tf_op | source)
XLA Modules:
  0.0 180.8 jit_solution(1938562220035936449)
XLA Ops:
  0.6 2.5 %send.1 = bf16[32,72,128]{2,1,0:T(8,128)(2,1)} custom-call(bf16[256,512]{1,0:T(8,128)(2,1)} %bitcast.30, bf16[460,512]{1,0:T(8,128)(2,1)} %rel.2, s32[1,512]{1,0:T(1,128)} %src.3, s32[1,512]{1,0:T(1,128)} %dst.1, s32[1,512]{1,0:T(1,128)} %rid.3, s32[1,8]{1,0:T(1,128)} %counts.1), custom_call_target="tpu_custom_call" | custom-call | tf_op jit(solution)/shard_map/send/pallas_call | solution.py:42
  3.2 7.3 %all-to-all-start = ((bf16[32,72,128]{2,1,0:T(8,128)(2,1)}), bf16[32,72,128]{2,1,0:T(8,128)(2,1)S(1)}, u32[]{:S(2)}, u32[]{:S(2)}) async-start(bf16[32,72,128]{2,1,0:T(8,128)(2,1)} %send.1), calls=%async_computation | async-start | bytes 1179648 | tf_op jit(solution)/shard_map/all_to_all | solution.py:438
  16.9 11.3 %all-to-all-done = bf16[32,72,128]{2,1,0:T(8,128)(2,1)S(1)} async-done(((bf16[32,72,128]{2,1,0:T(8,128)(2,1)}), bf16[32,72,128]{2,1,0:T(8,128)(2,1)S(1)}, u32[]{:S(2)}, u32[]{:S(2)}) %all-to-all-start) | async-done | bytes 589856 | tf_op jit(solution)/shard_map/all_to_all | solution.py:438
  28.3 2.1 %query.1 = (f32[256,128]{1,0:T(8,128)}, f32[464,128]{1,0:T(8,128)}) custom-call(s32[1,128]{1,0:T(1,128)} %bitcast.40, s32[1,128]{1,0:T(1,128)} %bitcast.41, f32[128,512]{1,0:T(8,128)} %qg.1), custom_call_target="tpu_custom_call" | custom-call | tf_op jit(solution)/shard_map/query/pallas_call | solution.py:42
  32.5 2.7 %collective-permute-done.3.refs_4_.refs_6_ = bf16[8,72,128]{2,1,0:T(8,128)(2,1)S(1)} collective-permute-done((bf16[8,72,128]{2,1,0:T(8,128)(2,1)S(1)}, bf16[8,72,128]{2,1,0:T(8,128)(2,1)S(1)}, u32[]{:S(2)}, u32[]{:S(2)}) %collective-permute-start.3) | collective-permute-done | bytes 147488 | tf_op jit(solution)/shard_map/ppermute | solution.py:418
  36.0 3.2 %state.4 = (f32[256,128]{1,0:T(8,128)}, f32[256,128]{1,0:T(8,128)}, f32[256,128]{1,0:T(8,128)}, bf16[256,512]{1,0:T(8,128)(2,1)}, s32[8,512]{1,0:T(8,128)}, /*index=5*/bf16[264,512]{1,0:T(8,128)(2,1)}) custom-call(bf16[264,512]{1,0:T(8,128)(2,1)} %pre.1.refs_0_, bf16[264,512]{1,0:T(8,128)(2,1)} %copy-done.2, bf16[264,512]{1,0:T(8,128)(2,1)} %copy-done.3, ...), custom_call_target="tpu_custom_call" | custom-call | tf_op jit(solution)/shard_map/state/pallas_call | solution.py:42
  39.2 2.8 %step.4 = (f32[256,128]{1,0:T(8,128)}, bf16[256,256]{1,0:T(8,128)(2,1)}, bf16[256,128]{1,0:T(8,128)(2,1)}, f32[256,128]{1,0:T(8,128)}, bf16[1024,128]{1,0:T(8,12...) custom-call(f32[256,128]{1,0:T(8,128)} %get-tuple-element.107.refs_0, ...), custom_call_target="tpu_custom_call" | custom-call | tf_op jit(solution)/shard_map/step/pallas_call | solution.py:42
  42.0 4.0 %all-to-all-start.1 = ((bf16[16,64,128]{2,1,0:T(8,128)(2,1)}), bf16[16,64,128]{2,1,0:T(8,128)(2,1)S(1)}, u32[]{:S(2)}, u32[]{:S(2)}) async-start(bf16[16,64,128]{2,1,0:T(8,128)(2,1)} %bitcast.32), calls=%async_computation.1 | async-start | bytes 524288 | tf_op jit(solution)/shard_map/all_to_all | solution.py:511
  50.4 2.2 %collective-permute-start.7 = (bf16[256,128]{1,0:T(8,128)(2,1)S(1)}, bf16[256,128]{1,0:T(8,128)(2,1)S(1)}, u32[]{:S(2)}, u32[]{:S(2)}) collective-permute-start(bf16[256,128]{1,0:T(8,128)(2,1)S(1)} %copy-done.39), channel_id=1, source_target_pairs={{0,24},{8,0},{16,8},{24,16},{1,25},{9,1},{17,9},{25,17},{2,26},{10... | collective-permute-start | bytes 196616 | tf_op jit(solution)/shard_map/ppermute | solution.py:414
  52.6 2.9 %gather.3 = (bf16[256,512]{1,0:T(8,128)(2,1)}, bf16[512,256]{1,0:T(8,128)(2,1)}, f32[256,128]{1,0:T(8,128)}, f32[256,128]{1,0:T(8,128)}, bf16[256,512]{1,0:T(8,1...) custom-call(bf16[3,8,72,128]{3,2,1,0:T(8,128)(2,1)} %bitcast.16, ...), custom_call_target="tpu_custom_call" | custom-call | tf_op jit(solution)/shard_map/gather/pallas_call | solution.py:42
  55.5 6.4 %collective-permute-done.4.refs_4_.refs_13_.refs_20_.refs_27_ = bf16[3,8,72,128]{3,2,1,0:T(8,128)(2,1)S(1)} collective-permute-done((bf16[3,8,72,128]{3,2,1,0:T(8,128)(2,1)S(1)}, bf16[3,8,72,128]{3,2,1,0:T(8,128)(2,1)S(1)}, u32[]{:S(2)}, u32[]{:S(2)}) %collective-permute-start.4) | collective-permute-done | bytes 442400 | tf_op jit(solution)/shard_map/ppermute | solution.py:418
  62.7 3.3 %state.5 = (f32[256,128]{1,0:T(8,128)}, f32[256,128]{1,0:T(8,128)}, f32[256,128]{1,0:T(8,128)}, bf16[256,512]{1,0:T(8,128)(2,1)}, s32[8,512]{1,0:T(8,128)}, /*index=5*/bf16[264,512]{1,0:T(8,128)(2,1)}) custom-call(bf16[264,512]{1,0:T(8,128)(2,1)} %pre.1.refs_0_, bf16[264,512]{1,0:T(8,128)(2,1)} %copy-done.2, bf16[264,512]{1,0:T(8,128)(2,1)} %copy-done.3, ...), custom_call_target="tpu_custom_call" | custom-call | tf_op jit(solution)/shard_map/state/pallas_call | solution.py:42
  66.8 3.3 %step.5 = (f32[256,128]{1,0:T(8,128)}, bf16[256,256]{1,0:T(8,128)(2,1)}, bf16[256,128]{1,0:T(8,128)(2,1)}, f32[256,128]{1,0:T(8,128)}, bf16[1024,128]{1,0:T(8,12...) custom-call(f32[256,128]{1,0:T(8,128)} %get-tuple-element.119.refs_0, ...), custom_call_target="tpu_custom_call" | custom-call | tf_op jit(solution)/shard_map/step/pallas_call | solution.py:42
  70.1 4.6 %all-to-all-start.2 = ((bf16[16,64,128]{2,1,0:T(8,128)(2,1)}), bf16[16,64,128]{2,1,0:T(8,128)(2,1)S(1)}, u32[]{:S(2)}, u32[]{:S(2)}) async-start(bf16[16,64,128]{2,1,0:T(8,128)(2,1)} %bitcast.35), calls=%async_computation.2 | async-start | bytes 524288 | tf_op jit(solution)/shard_map/all_to_all | solution.py:511
  79.3 3.2 %state.6 = (f32[256,128]{1,0:T(8,128)}, f32[256,128]{1,0:T(8,128)}, f32[256,128]{1,0:T(8,128)}, bf16[256,512]{1,0:T(8,128)(2,1)}, s32[8,512]{1,0:T(8,128)}, /*index=5*/bf16[264,512]{1,0:T(8,128)(2,1)}) custom-call(bf16[264,512]{1,0:T(8,128)(2,1)} %pre.1.refs_0_, bf16[264,512]{1,0:T(8,128)(2,1)} %copy-done.2, bf16[264,512]{1,0:T(8,128)(2,1)} %copy-done.3, ...), custom_call_target="tpu_custom_call" | custom-call | tf_op jit(solution)/shard_map/state/pallas_call | solution.py:42
  85.4 3.3 %step.6 = (f32[256,128]{1,0:T(8,128)}, bf16[256,256]{1,0:T(8,128)(2,1)}, bf16[256,128]{1,0:T(8,128)(2,1)}, f32[256,128]{1,0:T(8,128)}, bf16[1024,128]{1,0:T(8,12...) custom-call(f32[256,128]{1,0:T(8,128)} %get-tuple-element.136.refs_0, ...), custom_call_target="tpu_custom_call" | custom-call | tf_op jit(solution)/shard_map/step/pallas_call | solution.py:42
  88.7 4.6 %all-to-all-start.3 = ((bf16[16,64,128]{2,1,0:T(8,128)(2,1)}), bf16[16,64,128]{2,1,0:T(8,128)(2,1)S(1)}, u32[]{:S(2)}, u32[]{:S(2)}) async-start(bf16[16,64,128]{2,1,0:T(8,128)(2,1)} %bitcast.34), calls=%async_computation.3 | async-start | bytes 524288 | tf_op jit(solution)/shard_map/all_to_all | solution.py:511
  97.0 3.3 %state.7 = (f32[256,128]{1,0:T(8,128)}, f32[256,128]{1,0:T(8,128)}, f32[256,128]{1,0:T(8,128)}, bf16[256,512]{1,0:T(8,128)(2,1)}, s32[8,512]{1,0:T(8,128)}, /*index=5*/bf16[264,512]{1,0:T(8,128)(2,1)}) custom-call(bf16[264,512]{1,0:T(8,128)(2,1)} %pre.1.refs_0_, bf16[264,512]{1,0:T(8,128)(2,1)} %copy-done.2, bf16[264,512]{1,0:T(8,128)(2,1)} %copy-done.3, ...), custom_call_target="tpu_custom_call" | custom-call | tf_op jit(solution)/shard_map/state/pallas_call | solution.py:42
  104.1 3.2 %step.7 = (f32[256,128]{1,0:T(8,128)}, bf16[256,256]{1,0:T(8,128)(2,1)}, bf16[256,128]{1,0:T(8,128)(2,1)}, f32[256,128]{1,0:T(8,128)}, bf16[1024,128]{1,0:T(8,12...) custom-call(f32[256,128]{1,0:T(8,128)} %get-tuple-element.153.refs_0, ...), custom_call_target="tpu_custom_call" | custom-call | tf_op jit(solution)/shard_map/step/pallas_call | solution.py:42
  107.3 3.7 %all-to-all-start.4 = ((bf16[16,64,128]{2,1,0:T(8,128)(2,1)}), bf16[16,64,128]{2,1,0:T(8,128)(2,1)S(1)}, u32[]{:S(2)}, u32[]{:S(2)}) async-start(bf16[16,64,128]{2,1,0:T(8,128)(2,1)} %bitcast.33), calls=%async_computation.4 | async-start | bytes 524288 | tf_op jit(solution)/shard_map/all_to_all | solution.py:511
  111.0 2.8 %rel.3.old = f32[464,128]{1,0:T(8,128)} custom-call(bf16[1024,128]{1,0:T(8,128)(2,1)} %bitcast.23, s32[8,512]{1,0:T(8,128)} %get-tuple-element.171.refs_1_, bf16[1024,128]{1,0:T(8,128)(2,1)} %bitcast.25, s32[8,512]{1,0:T(8,128)} %get-tuple-element.172.refs_3_, bf16[1024,128]{1,0:T(8,128)(2,1)} %bitcast.27, s32[8,512]{1,0:T(8,128)} %get-tuple-element.173.refs_5_, ...), custom_call_target="tpu_custom_call" | custom-call | tf_op jit(solution)/shard_map/rel/pallas_call | solution.py:42
  113.9 4.3 %grad.1 = (f32[512,256]{1,0:T(8,128)}, f32[256,128]{1,0:T(8,128)}, f32[8,128]{1,0:T(8,128)}) custom-call(bf16[264,512]{1,0:T(8,128)(2,1)} %get-tuple-element.106.refs_0_, bf16[256,256]{1,0:T(8,128)(2,1)} %get-tuple-element.112.refs_1_, f32[8,128]{1,0:T(8,128)} %get-tuple-element.113.refs_2_, bf16[512,256]{1,0:T(8,128)(2,1)} %get-tuple-element.111.refs_5_.refs_3_, ...), custom_call_target="tpu_custom_call" | custom-call | tf_op jit(solution)/shard_map/grad/pallas_call | solution.py:42
  118.1 2.7 %all-to-all-done.4 = bf16[16,64,128]{2,1,0:T(8,128)(2,1)S(1)} async-done(((bf16[16,64,128]{2,1,0:T(8,128)(2,1)}), bf16[16,64,128]{2,1,0:T(8,128)(2,1)S(1)}, u32[]{:S(2)}, u32[]{:S(2)}) %all-to-all-start.4) | async-done | bytes 262176 | tf_op jit(solution)/shard_map/all_to_all | solution.py:511
  121.5 2.5 %pack.1 = (bf16[4,224,128]{2,1,0:T(8,128)(2,1)}, bf16[4,224,128]{2,1,0:T(8,128)(2,1)}) custom-call(f32[512,256]{1,0:T(8,128)} %get-tuple-element.166.gs, f32[256,128]{1,0:T(8,128)} %get-tuple-element.167.ns, f32[8,128]{1,0:T(8,128)} %get-tuple-element.168.bs, bf16[1024,128]{1,0:T(8,128)(2,1)} %bitcast.28, s32[8,512]{1,0:T(8,128)} %get-tuple-element.170.rid, ...), custom_call_target="tpu_custom_call" | custom-call | tf_op jit(solution)/shard_map/pack/pallas_call | solution.py:42
  128.2 3.5 %all-to-all-start.5 = ((bf16[4,224,128]{2,1,0:T(8,128)(2,1)}), bf16[4,224,128]{2,1,0:T(8,128)(2,1)S(1)}, u32[]{:S(2)}, u32[]{:S(2)}) async-start(bf16[4,224,128]{2,1,0:T(8,128)(2,1)} %pair.1), calls=%async_computation.5 | async-start | bytes 458752 | tf_op jit(solution)/shard_map/all_to_all | solution.py:574
  133.8 2.4 %collective-permute-start.17 = (bf16[256,128]{1,0:T(8,128)(2,1)S(1)}, bf16[256,128]{1,0:T(8,128)(2,1)S(1)}, u32[]{:S(2)}, u32[]{:S(2)}) collective-permute-start(bf16[256,128]{1,0:T(8,128)(2,1)S(1)} %copy-done.36), channel_id=1, source_target_pairs={{0,24},{8,0},{16,8},{24,16},{1,25},{9,1},{17,9},{25,17},{2,26},{10... | collective-permute-start | bytes 196616 | tf_op jit(solution)/shard_map/ppermute | solution.py:414
  138.8 2.5 %pick.1 = (f32[256,128]{1,0:T(8,128)}, f32[256,128]{1,0:T(8,128)}, f32[256,128]{1,0:T(8,128)}, f32[256,128]{1,0:T(8,128)}) custom-call(f32[256,128]{1,0:T(8,128)} %get-tuple-element.177.refs_0_, bf16[256,128]{1,0:T(8,128)(2,1)} %copy-done.33, bf16[256,128]{1,0:T(8,128)(2,1)} %copy-done.34, bf16[256,128]{1,0:T(8,128)(2,1)} %copy-done.35, ...), custom_call_target="tpu_custom_call" | custom-call | tf_op jit(solution)/shard_map/pick/pallas_call | solution.py:42
  141.3 2.3 %collective-permute-start.18 = (f32[256,128]{1,0:T(8,128)}, f32[256,128]{1,0:T(8,128)S(1)}, u32[]{:S(2)}, u32[]{:S(2)}) collective-permute-start(f32[256,128]{1,0:T(8,128)} %get-tuple-element.186), channel_id=1, source_target_pairs={{0,8},{8,16},{16,24},{24,0},{1,9},{9,17},{17,25},{25,1},{2,10},{10... | collective-permute-start | bytes 393224 | tf_op jit(solution)/shard_map/ppermute | solution.py:414
  145.1 3.7 %collective-permute-done.18.refs_9_ = f32[256,128]{1,0:T(8,128)S(1)} collective-permute-done((f32[256,128]{1,0:T(8,128)}, f32[256,128]{1,0:T(8,128)S(1)}, u32[]{:S(2)}, u32[]{:S(2)}) %collective-permute-start.18) | collective-permute-done | bytes 131104 | tf_op jit(solution)/shard_map/ppermute | solution.py:414
  152.5 11.9 %all_to_all.35.refs_0_ = bf16[4,224,128]{2,1,0:T(8,128)(2,1)S(1)} all-to-all(bf16[4,224,128]{2,1,0:T(8,128)(2,1)} %sum.1), channel_id=1, replica_groups={{0,2,4,6},{1,3,5,7},{8,10,12,14},{9,11,13,15},{16,18,20,22},{17,19,21,2..., dimensions={0} | all-to-all | bytes 458752 | tf_op jit(solution)/shard_map/all_to_all | solution.py:574
  168.3 3.9 %collective-permute-done.21.refs_1_ = bf16[4,224,128]{2,1,0:T(8,128)(2,1)S(1)} collective-permute-done((bf16[4,224,128]{2,1,0:T(8,128)(2,1)S(1)}, bf16[4,224,128]{2,1,0:T(8,128)(2,1)S(1)}, u32[]{:S(2)}, u32[]{:S(2)}) %collective-permute-start.21) | collective-permute-done | bytes 229408 | tf_op jit(solution)/shard_map/ppermute | solution.py:414
  176.9 3.8 %last.1 = (f32[256,512]{1,0:T(8,128)}, f32[2,256,256]{2,1,0:T(8,128)}, f32[512,512]{1,0:T(8,128)}, f32[512,512]{1,0:T(8,128)}, f32[1,512]{1,0:T(1,128)}, /*index=5*/f32[460,512]{1,0:T(8,128)}) custom-call(bf16[4,224,128]{2,1,0:T(8,128)(2,1)} %copy-done.10, bf16[4,224,128]{2,1,0:T(8,128)(2,1)} %copy-done.13, bf16[4,224,128]{2,1,0:T(8,128)(2,1)} %copy-done.14, ...), custom_call_target="tpu_custom_call" | custom-call | tf_op jit(solution)/shard_map/last/pallas_call | solution.py:588
  (155 shorter events, 53.3 us)
Async XLA Ops:
  3.2 25.1 %all-to-all-start = ((bf16[32,72,128]{2,1,0:T(8,128)(2,1)}), bf16[32,72,128]{2,1,0:T(8,128)(2,1)S(1)}, u32[]{:S(2)}, u32[]{:S(2)}) async-start(bf16[32,72,128]{2,1,0:T(8,128)(2,1)} %send.1), calls=%async_computation | async-start | bytes 1179648 | tf_op jit(solution)/shard_map/all_to_all | solution.py:438
  12.2 20.2 %collective-permute-start = (bf16[264,512]{1,0:T(8,128)(2,1)}, bf16[264,512]{1,0:T(8,128)(2,1)S(1)}, u32[]{:S(2)}, u32[]{:S(2)}) collective-permute-start(bf16[264,512]{1,0:T(8,128)(2,1)} %pre.1.refs_0_), channel_id=1, source_target_pairs={{0,8},{8,16},{16,24},{24,0},{1,9},{9,17},{17,25},{25,1},{2,10},{10... | collective-permute-start | bytes 811016 | tf_op jit(solution)/shard_map/ppermute | solution.py:414
  14.0 18.5 %collective-permute-start.1 = (bf16[264,512]{1,0:T(8,128)(2,1)}, bf16[264,512]{1,0:T(8,128)(2,1)S(1)}, u32[]{:S(2)}, u32[]{:S(2)}) collective-permute-start(bf16[264,512]{1,0:T(8,128)(2,1)} %pre.1.refs_0_), channel_id=1, source_target_pairs={{0,16},{8,24},{16,0},{24,8},{1,17},{9,25},{17,1},{25,9},{2,18},{10... | collective-permute-start | bytes 811016 | tf_op jit(solution)/shard_map/ppermute | solution.py:414
  15.5 17.1 %collective-permute-start.2 = (bf16[264,512]{1,0:T(8,128)(2,1)}, bf16[264,512]{1,0:T(8,128)(2,1)S(1)}, u32[]{:S(2)}, u32[]{:S(2)}) collective-permute-start(bf16[264,512]{1,0:T(8,128)(2,1)} %pre.1.refs_0_), channel_id=1, source_target_pairs={{0,24},{8,0},{16,8},{24,16},{1,25},{9,1},{17,9},{25,17},{2,26},{10... | collective-permute-start | bytes 811016 | tf_op jit(solution)/shard_map/ppermute | solution.py:414
  28.3 7.0 %collective-permute-start.3 = (bf16[8,72,128]{2,1,0:T(8,128)(2,1)S(1)}, bf16[8,72,128]{2,1,0:T(8,128)(2,1)S(1)}, u32[]{:S(2)}, u32[]{:S(2)}) collective-permute-start(bf16[8,72,128]{2,1,0:T(8,128)(2,1)S(1)} %slice.13.refs_0_.refs_5_), channel_id=1, source_target_pairs={{0,8},{8,0},{16,24},{24,16},{1,9},{9,1},{17,25},{25,17},{2,10},{10... | collective-permute-start | bytes 442376 | tf_op jit(solution)/shard_map/ppermute | solution.py:418
  42.0 24.0 %all-to-all-start.1 = ((bf16[16,64,128]{2,1,0:T(8,128)(2,1)}), bf16[16,64,128]{2,1,0:T(8,128)(2,1)S(1)}, u32[]{:S(2)}, u32[]{:S(2)}) async-start(bf16[16,64,128]{2,1,0:T(8,128)(2,1)} %bitcast.32), calls=%async_computation.1 | async-start | bytes 524288 | tf_op jit(solution)/shard_map/all_to_all | solution.py:511
  46.1 15.9 %collective-permute-start.4 = (bf16[3,8,72,128]{3,2,1,0:T(8,128)(2,1)S(1)}, bf16[3,8,72,128]{3,2,1,0:T(8,128)(2,1)S(1)}, u32[]{:S(2)}, u32[]{:S(2)}) collective-permute-start(bf16[3,8,72,128]{3,2,1,0:T(8,128)(2,1)S(1)} %bitcast.15), channel_id=1, source_target_pairs={{0,8},{8,0},{16,24},{24,16},{1,9},{9,1},{17,25},{25,17},{2,10},{10... | collective-permute-start | bytes 1327112 | tf_op jit(solution)/shard_map/ppermute | solution.py:418
  48.1 17.9 %collective-permute-start.5 = (bf16[256,128]{1,0:T(8,128)(2,1)S(1)}, bf16[256,128]{1,0:T(8,128)(2,1)S(1)}, u32[]{:S(2)}, u32[]{:S(2)}) collective-permute-start(bf16[256,128]{1,0:T(8,128)(2,1)S(1)} %copy-done.41), channel_id=1, source_target_pairs={{0,8},{8,16},{16,24},{24,0},{1,9},{9,17},{17,25},{25,1},{2,10},{10... | collective-permute-start | bytes 196616 | tf_op jit(solution)/shard_map/ppermute | solution.py:414
  48.8 17.2 %collective-permute-start.6 = (bf16[256,128]{1,0:T(8,128)(2,1)S(1)}, bf16[256,128]{1,0:T(8,128)(2,1)S(1)}, u32[]{:S(2)}, u32[]{:S(2)}) collective-permute-start(bf16[256,128]{1,0:T(8,128)(2,1)S(1)} %copy-done.40), channel_id=1, source_target_pairs={{0,16},{8,24},{16,0},{24,8},{1,17},{9,25},{17,1},{25,9},{2,18},{10... | collective-permute-start | bytes 196616 | tf_op jit(solution)/shard_map/ppermute | solution.py:414
  50.4 15.6 %collective-permute-start.7 = (bf16[256,128]{1,0:T(8,128)(2,1)S(1)}, bf16[256,128]{1,0:T(8,128)(2,1)S(1)}, u32[]{:S(2)}, u32[]{:S(2)}) collective-permute-start(bf16[256,128]{1,0:T(8,128)(2,1)S(1)} %copy-done.39), channel_id=1, source_target_pairs={{0,24},{8,0},{16,8},{24,16},{1,25},{9,1},{17,9},{25,17},{2,26},{10... | collective-permute-start | bytes 196616 | tf_op jit(solution)/shard_map/ppermute | solution.py:414
  70.1 14.6 %all-to-all-start.2 = ((bf16[16,64,128]{2,1,0:T(8,128)(2,1)}), bf16[16,64,128]{2,1,0:T(8,128)(2,1)S(1)}, u32[]{:S(2)}, u32[]{:S(2)}) async-start(bf16[16,64,128]{2,1,0:T(8,128)(2,1)} %bitcast.35), calls=%async_computation.2 | async-start | bytes 524288 | tf_op jit(solution)/shard_map/all_to_all | solution.py:511
  74.7 8.1 %collective-permute-start.8 = (bf16[256,128]{1,0:T(8,128)(2,1)S(1)}, bf16[256,128]{1,0:T(8,128)(2,1)S(1)}, u32[]{:S(2)}, u32[]{:S(2)}) collective-permute-start(bf16[256,128]{1,0:T(8,128)(2,1)S(1)} %copy-done.47), channel_id=1, source_target_pairs={{0,8},{8,16},{16,24},{24,0},{1,9},{9,17},{17,25},{25,1},{2,10},{10... | collective-permute-start | bytes 196616 | tf_op jit(solution)/shard_map/ppermute | solution.py:414
  76.7 6.1 %collective-permute-start.9 = (bf16[256,128]{1,0:T(8,128)(2,1)S(1)}, bf16[256,128]{1,0:T(8,128)(2,1)S(1)}, u32[]{:S(2)}, u32[]{:S(2)}) collective-permute-start(bf16[256,128]{1,0:T(8,128)(2,1)S(1)} %copy-done.46), channel_id=1, source_target_pairs={{0,16},{8,24},{16,0},{24,8},{1,17},{9,25},{17,1},{25,9},{2,18},{10... | collective-permute-start | bytes 196616 | tf_op jit(solution)/shard_map/ppermute | solution.py:414
  78.3 4.7 %collective-permute-start.10 = (bf16[256,128]{1,0:T(8,128)(2,1)S(1)}, bf16[256,128]{1,0:T(8,128)(2,1)S(1)}, u32[]{:S(2)}, u32[]{:S(2)}) collective-permute-start(bf16[256,128]{1,0:T(8,128)(2,1)S(1)} %copy-done.44), channel_id=1, source_target_pairs={{0,24},{8,0},{16,8},{24,16},{1,25},{9,1},{17,9},{25,17},{2,26},{10... | collective-permute-start | bytes 196616 | tf_op jit(solution)/shard_map/ppermute | solution.py:414
  88.7 14.6 %all-to-all-start.3 = ((bf16[16,64,128]{2,1,0:T(8,128)(2,1)}), bf16[16,64,128]{2,1,0:T(8,128)(2,1)S(1)}, u32[]{:S(2)}, u32[]{:S(2)}) async-start(bf16[16,64,128]{2,1,0:T(8,128)(2,1)} %bitcast.34), calls=%async_computation.3 | async-start | bytes 524288 | tf_op jit(solution)/shard_map/all_to_all | solution.py:511
  93.3 6.9 %collective-permute-start.11 = (bf16[256,128]{1,0:T(8,128)(2,1)S(1)}, bf16[256,128]{1,0:T(8,128)(2,1)S(1)}, u32[]{:S(2)}, u32[]{:S(2)}) collective-permute-start(bf16[256,128]{1,0:T(8,128)(2,1)S(1)} %copy-done.45), channel_id=1, source_target_pairs={{0,8},{8,16},{16,24},{24,0},{1,9},{9,17},{17,25},{25,1},{2,10},{10... | collective-permute-start | bytes 196616 | tf_op jit(solution)/shard_map/ppermute | solution.py:414
  95.3 5.1 %collective-permute-start.12 = (bf16[256,128]{1,0:T(8,128)(2,1)S(1)}, bf16[256,128]{1,0:T(8,128)(2,1)S(1)}, u32[]{:S(2)}, u32[]{:S(2)}) collective-permute-start(bf16[256,128]{1,0:T(8,128)(2,1)S(1)} %copy-done.43), channel_id=1, source_target_pairs={{0,16},{8,24},{16,0},{24,8},{1,17},{9,25},{17,1},{25,9},{2,18},{10... | collective-permute-start | bytes 196616 | tf_op jit(solution)/shard_map/ppermute | solution.py:414
  95.9 5.4 %collective-permute-start.13 = (bf16[256,128]{1,0:T(8,128)(2,1)S(1)}, bf16[256,128]{1,0:T(8,128)(2,1)S(1)}, u32[]{:S(2)}, u32[]{:S(2)}) collective-permute-start(bf16[256,128]{1,0:T(8,128)(2,1)S(1)} %copy-done.42), channel_id=1, source_target_pairs={{0,24},{8,0},{16,8},{24,16},{1,25},{9,1},{17,9},{25,17},{2,26},{10... | collective-permute-start | bytes 196616 | tf_op jit(solution)/shard_map/ppermute | solution.py:414
  107.3 13.5 %all-to-all-start.4 = ((bf16[16,64,128]{2,1,0:T(8,128)(2,1)}), bf16[16,64,128]{2,1,0:T(8,128)(2,1)S(1)}, u32[]{:S(2)}, u32[]{:S(2)}) async-start(bf16[16,64,128]{2,1,0:T(8,128)(2,1)} %bitcast.33), calls=%async_computation.4 | async-start | bytes 524288 | tf_op jit(solution)/shard_map/all_to_all | solution.py:511
  124.1 1.7 collective-permute-start.14
  128.2 21.9 %all-to-all-start.5 = ((bf16[4,224,128]{2,1,0:T(8,128)(2,1)}), bf16[4,224,128]{2,1,0:T(8,128)(2,1)S(1)}, u32[]{:S(2)}, u32[]{:S(2)}) async-start(bf16[4,224,128]{2,1,0:T(8,128)(2,1)} %pair.1), calls=%async_computation.5 | async-start | bytes 458752 | tf_op jit(solution)/shard_map/all_to_all | solution.py:574
  131.8 5.6 %collective-permute-start.15 = (bf16[256,128]{1,0:T(8,128)(2,1)S(1)}, bf16[256,128]{1,0:T(8,128)(2,1)S(1)}, u32[]{:S(2)}, u32[]{:S(2)}) collective-permute-start(bf16[256,128]{1,0:T(8,128)(2,1)S(1)} %copy-done.38), channel_id=1, source_target_pairs={{0,8},{8,16},{16,24},{24,0},{1,9},{9,17},{17,25},{25,1},{2,10},{10... | collective-permute-start | bytes 196616 | tf_op jit(solution)/shard_map/ppermute | solution.py:414
  132.4 5.3 %collective-permute-start.16 = (bf16[256,128]{1,0:T(8,128)(2,1)S(1)}, bf16[256,128]{1,0:T(8,128)(2,1)S(1)}, u32[]{:S(2)}, u32[]{:S(2)}) collective-permute-start(bf16[256,128]{1,0:T(8,128)(2,1)S(1)} %copy-done.37), channel_id=1, source_target_pairs={{0,16},{8,24},{16,0},{24,8},{1,17},{9,25},{17,1},{25,9},{2,18},{10... | collective-permute-start | bytes 196616 | tf_op jit(solution)/shard_map/ppermute | solution.py:414
  133.8 4.4 %collective-permute-start.17 = (bf16[256,128]{1,0:T(8,128)(2,1)S(1)}, bf16[256,128]{1,0:T(8,128)(2,1)S(1)}, u32[]{:S(2)}, u32[]{:S(2)}) collective-permute-start(bf16[256,128]{1,0:T(8,128)(2,1)S(1)} %copy-done.36), channel_id=1, source_target_pairs={{0,24},{8,0},{16,8},{24,16},{1,25},{9,1},{17,9},{25,17},{2,26},{10... | collective-permute-start | bytes 196616 | tf_op jit(solution)/shard_map/ppermute | solution.py:414
  141.3 7.5 %collective-permute-start.18 = (f32[256,128]{1,0:T(8,128)}, f32[256,128]{1,0:T(8,128)S(1)}, u32[]{:S(2)}, u32[]{:S(2)}) collective-permute-start(f32[256,128]{1,0:T(8,128)} %get-tuple-element.186), channel_id=1, source_target_pairs={{0,8},{8,16},{16,24},{24,0},{1,9},{9,17},{17,25},{25,1},{2,10},{10... | collective-permute-start | bytes 393224 | tf_op jit(solution)/shard_map/ppermute | solution.py:414
  143.6 6.3 %collective-permute-start.19 = (f32[256,128]{1,0:T(8,128)}, f32[256,128]{1,0:T(8,128)S(1)}, u32[]{:S(2)}, u32[]{:S(2)}) collective-permute-start(f32[256,128]{1,0:T(8,128)} %get-tuple-element.187), channel_id=1, source_target_pairs={{0,16},{8,24},{16,0},{24,8},{1,17},{9,25},{17,1},{25,9},{2,18},{10... | collective-permute-start | bytes 393224 | tf_op jit(solution)/shard_map/ppermute | solution.py:414
  145.0 5.2 %collective-permute-start.20 = (f32[256,128]{1,0:T(8,128)}, f32[256,128]{1,0:T(8,128)S(1)}, u32[]{:S(2)}, u32[]{:S(2)}) collective-permute-start(f32[256,128]{1,0:T(8,128)} %get-tuple-element.188), channel_id=1, source_target_pairs={{0,24},{8,0},{16,8},{24,16},{1,25},{9,1},{17,9},{25,17},{2,26},{10... | collective-permute-start | bytes 393224 | tf_op jit(solution)/shard_map/ppermute | solution.py:414
  164.4 7.7 %collective-permute-start.21 = (bf16[4,224,128]{2,1,0:T(8,128)(2,1)S(1)}, bf16[4,224,128]{2,1,0:T(8,128)(2,1)S(1)}, u32[]{:S(2)}, u32[]{:S(2)}) collective-permute-start(bf16[4,224,128]{2,1,0:T(8,128)(2,1)S(1)} %all_to_all.35.refs_0_), channel_id=1, source_target_pairs={{0,8},{8,16},{16,24},{24,0},{1,9},{9,17},{17,25},{25,1},{2,10},{10... | collective-permute-start | bytes 688136 | tf_op jit(solution)/shard_map/ppermute | solution.py:414
  165.6 8.4 %collective-permute-start.22 = (bf16[4,224,128]{2,1,0:T(8,128)(2,1)S(1)}, bf16[4,224,128]{2,1,0:T(8,128)(2,1)S(1)}, u32[]{:S(2)}, u32[]{:S(2)}) collective-permute-start(bf16[4,224,128]{2,1,0:T(8,128)(2,1)S(1)} %all_to_all.35.refs_0_), channel_id=1, source_target_pairs={{0,16},{8,24},{16,0},{24,8},{1,17},{9,25},{17,1},{25,9},{2,18},{10... | collective-permute-start | bytes 688136 | tf_op jit(solution)/shard_map/ppermute | solution.py:414
  166.6 8.1 %collective-permute-start.23 = (bf16[4,224,128]{2,1,0:T(8,128)(2,1)S(1)}, bf16[4,224,128]{2,1,0:T(8,128)(2,1)S(1)}, u32[]{:S(2)}, u32[]{:S(2)}) collective-permute-start(bf16[4,224,128]{2,1,0:T(8,128)(2,1)S(1)} %all_to_all.35.refs_0_), channel_id=1, source_target_pairs={{0,24},{8,0},{16,8},{24,16},{1,25},{9,1},{17,9},{25,17},{2,26},{10... | collective-permute-start | bytes 688136 | tf_op jit(solution)/shard_map/ppermute | solution.py:414
  168.3 6.4 %collective-permute-start.24 = (bf16[4,224,128]{2,1,0:T(8,128)(2,1)S(1)}, bf16[4,224,128]{2,1,0:T(8,128)(2,1)S(1)}, u32[]{:S(2)}, u32[]{:S(2)}) collective-permute-start(bf16[4,224,128]{2,1,0:T(8,128)(2,1)S(1)} %all_to_all.35.refs_0_), channel_id=1, source_target_pairs={{0,1},{1,0},{2,3},{3,2},{4,5},{5,4},{6,7},{7,6},{8,9},{9,8},{10,11... | collective-permute-start | bytes 688136 | tf_op jit(solution)/shard_map/ppermute | solution.py:421
  172.2 2.5 %collective-permute-start.25 = (bf16[4,224,128]{2,1,0:T(8,128)(2,1)S(1)}, bf16[4,224,128]{2,1,0:T(8,128)(2,1)S(1)}, u32[]{:S(2)}, u32[]{:S(2)}) collective-permute-start(bf16[4,224,128]{2,1,0:T(8,128)(2,1)S(1)} %collective-permute-done.21.refs_1_), channel_id=1, source_target_pairs={{0,1},{1,0},{2,3},{3,2},{4,5},{5,4},{6,7},{7,6},{8,9},{9,8},{10,11... | collective-permute-start | bytes 688136 | tf_op jit(solution)/shard_map/ppermute | solution.py:421
  (50 other events, 172.4 us)

commit v2 on v1

--- a/solution.py
+++ b/solution.py
@@ -24,6 +24,20 @@
     return jnp.where(spot == ids, 1.0, 0.0).astype(BF)
 
 
+class Far:
+    def __init__(self, value):
+        self.value = value
+        self.shape = value.shape
+
+
+def raw(x):
+    return x.value if isinstance(x, Far) else x
+
+
+def far(x):
+    return x if isinstance(x, Far) else Far(x)
+
+
 def round_up(value, step):
     return -(-value // step) * step
 
@@ -38,16 +52,31 @@
     return block(x.shape)
 
 
-def run(body, name, ins, specs, outs, scratch=()):
-    return pl.pallas_call(
+def run(body, name, ins, specs, outs, scratch=(), limit=16):
+    tiled = any(s.block_shape and None in s.block_shape for s in specs)
+    near = pl.BlockSpec(memory_space=pltpu.VMEM)
+
+    def spec(s):
+        return near if s.block_shape and not tiled else s
+
+    arrays = [
+        pltpu.with_memory_space_constraint(x.value, pltpu.HBM) if isinstance(x, Far) else x
+        for x in ins
+    ]
+    shapes = [
+        pltpu.HBM(o.value.shape, o.value.dtype) if isinstance(o, Far) else o for o in outs
+    ]
+    results = pl.pallas_call(
         body,
         name=name,
-        grid=(1,),
-        in_specs=specs,
-        out_specs=[block(s.shape) for s in outs],
-        out_shape=outs,
+        in_specs=[spec(s) for s in specs],
+        out_specs=[spec(block(o.shape)) for o in shapes],
+        out_shape=shapes,
         scratch_shapes=list(scratch),
-    )(*ins)
+        compiler_params=pltpu.CompilerParams(vmem_limit_bytes=limit << 20),
+        **({"grid": (1,)} if tiled else {}),
+    )(*arrays)
+    return [Far(r) if isinstance(o, Far) else r for r, o in zip(results, outs)]
 
 
 def sds(shape, dtype):
@@ -104,76 +133,65 @@
         for target in range(sections):
             msg[target * groups + u, room:, :] = row
 
-def gather_kernel(count, *refs):
-    for t in range(count):
-        recv = refs[t]
-        od, odt, scaling, summed_out = refs[count + 4 * t : count + 4 * t + 4]
-        groups = recv.shape[0]
-        width = recv.shape[2]
-        room = recv.shape[1] - 8
-        ent_rows = od.shape[0]
-        per = width // room
-        degree = jnp.zeros((ent_rows, width), F32)
-        summed = jnp.zeros((ent_rows, width), F32)
-        ones = jnp.ones((width, width), BF)
-        for g in range(groups // per):
-            ids = recv[g * per, room:, :].astype(F32)
-            for j in range(1, per):
-                ids = jnp.maximum(ids, recv[g * per + j, room:, :].astype(F32))
-            hot = onehot(ids[:1].astype(jnp.int32), ent_rows)
-            rows = jnp.concatenate([recv[g * per + j, :room, :] for j in range(per)], axis=0)
-            summed = summed + dot(hot, rows)
-            degree = degree + dot(hot, ones)
-            od[:, g * width : (g + 1) * width] = hot
-            odt[g * width : (g + 1) * width, :] = hot.astype(F32).T.astype(BF)
-        scaling[...] = 1.0 / jnp.maximum(degree, 1.0)
-        summed_out[...] = summed
-
-
 def stacked(recv):
     return jnp.concatenate([recv[i, : recv.shape[1] - 8, :] for i in range(recv.shape[0])], axis=0)
 
 
-def state_values(mates, xt, scaling, summed, od, mate_rows, wg, ws, wn, bias):
-    ent_rows, width = summed.shape
-    half = wn.shape[1]
+def choose(t, sections, act):
     h = lax.axis_index("hist")
-    cols = place(h, width)
+    for k in range(sections):
+
+        @pl.when(lax.rem(h - k + sections, sections) == t)
+        def _():
+            act(k)
+
+
+def state_kernel(t, sections, mates, *refs):
+    xs = refs[:sections]
+    recv = refs[sections]
+    mate_rows = refs[sections + 1 : sections + mates]
+    wcat, wnc, bias, coef, odt, osr, rid, xt, sem = refs[sections + mates :]
+    choose(t, sections, lambda k: pltpu.make_async_copy(xs[k], xt, sem).start())
+    groups, deep, width = recv.shape
+    room = deep - 8
+    slots, ent_rows = odt.shape
+    per = width // room
+    h = lax.axis_index("hist")
     seat = lax.rem(h, mates)
-    x = xt[:ent_rows, :]
+    degree = jnp.zeros((ent_rows, width), F32)
+    summed = [jnp.zeros((ent_rows, width), F32) for m in range(mates)]
+    ones = jnp.ones((width, width), BF)
+    for g in range(groups // per):
+        ids = recv[g * per, room:, :].astype(F32)
+        for j in range(1, per):
+            ids = jnp.maximum(ids, recv[g * per + j, room:, :].astype(F32))
+        hot = onehot(ids[:1].astype(jnp.int32), ent_rows)
+        degree = degree + dot(hot, ones)
+        for m, source in enumerate((recv, *mate_rows)):
+            rows = jnp.concatenate([source[g * per + j, :room, :] for j in range(per)], axis=0)
+            summed[m] = summed[m] + dot(hot, rows)
+        odt[g * width : (g + 1) * width, :] = hot.astype(F32).T.astype(BF)
     gathered = jnp.zeros((ent_rows, width), F32)
     for m in range(mates):
-        part = summed[...] if m == 0 else dot(od[...], stacked(mate_rows[m - 1]))
-        high = part.astype(BF)
-        low = (part - high.astype(F32)).astype(BF)
-        source = lax.rem(seat - m + mates, mates)
-        w = wn[h * width // half, place(source, width), place(seat, width)]
+        high = summed[m].astype(BF)
+        low = (summed[m] - high.astype(F32)).astype(BF)
+        w = wnc[place(lax.rem(seat - m + mates, mates), width), :]
         gathered = gathered + dot(
             jnp.concatenate([high, low], axis=1), jnp.concatenate([w, w], axis=0)
         )
-    pre_act = gathered * scaling + dot(x, ws[:, cols])
-    gate_open = jax.nn.sigmoid(dot(x, wg[:, cols]) + bias[:, cols])
+    scaling = 1.0 / jnp.maximum(degree, 1.0)
+    coef[:, 3 * width :] = scaling
+    pltpu.make_async_copy(xs[0], xt, sem).wait()
+    straight = dot(xt[:ent_rows, :], wcat[...])
+    gate_open = jax.nn.sigmoid(straight[:, :width] + bias[:1, :])
+    pre_act = gathered * scaling + straight[:, width:]
     sig = jax.nn.sigmoid(pre_act)
     new_state = pre_act * sig
     shut = 1.0 - gate_open
-    return (
-        (new_state - xt[:ent_rows, cols].astype(F32)) * gate_open * shut,
-        gate_open * (sig * (1.0 + pre_act * (1.0 - sig))),
-        shut,
-    )
-
-
-def choose(t, sections, xs, xt):
-    h = lax.axis_index("hist")
-    for k in range(sections):
-
-        @pl.when(lax.rem(h - k + sections, sections) == t)
-        def _():
-            xt[...] = xs[k][...]
-
-
-def index_rows(xt, ent_rows, osr, rid):
-    slots = osr.shape[1]
+    hidden = xt[:ent_rows, place(h, width)].astype(F32)
+    coef[:, :width] = (new_state - hidden) * gate_open * shut
+    coef[:, width : 2 * width] = gate_open * (sig * (1.0 + pre_act * (1.0 - sig)))
+    coef[:, 2 * width : 3 * width] = shut
     features = xt.shape[1]
     extra = xt[ent_rows:, :].astype(F32).astype(jnp.int32)
     for k in range(slots // features):
@@ -183,20 +201,16 @@
         rid[:, cut] = jnp.broadcast_to(ids, (8, features))
 
 
-def state_kernel(t, sections, mates, *refs):
-    xs = refs[:sections]
-    mate_rows = refs[sections : sections + mates - 1]
-    scaling, summed, od, wg, ws, wn, bias, al, be, ka, osr, rid, xt = refs[sections + mates - 1 :]
-    choose(t, sections, xs, xt)
-    values = state_values(mates, xt, scaling[...], summed, od, mate_rows, wg, ws, wn, bias)
-    al[...], be[...], ka[...] = values
-    index_rows(xt, summed.shape[0], osr, rid)
-
-
-def query_kernel(qe, qr, qg, top, qp):
+def query_kernel(qe, qr, qg, wg, ws, wn, bias, top, qp, wcat, wnc, bias_out):
     width = top.shape[1]
+    half, mates = wn.shape[1], wn.shape[1] // width
     h = lax.axis_index("hist")
-    grad = qg[:, place(h, width)]
+    cols = place(h, width)
+    wcat[:, :width] = wg[:, cols]
+    wcat[:, width:] = ws[:, cols]
+    wnc[...] = wn[h * width // half, :, place(lax.rem(h, mates), width)]
+    bias_out[...] = jnp.broadcast_to(bias[:, cols], bias_out.shape)
+    grad = qg[:, cols]
     for ids, out in ((qe, top), (qr, qp)):
         hot = onehot(ids[...], out.shape[0]).astype(F32)
         out[...] = lax.dot_general(
@@ -209,7 +223,8 @@
 
 
 def arrived(parts, ret, osr):
-    c = parts[0][...]
+    width = ret.shape[1]
+    c = parts[0][:, width:]
     for p in parts[1:]:
         c = c + p[...].astype(F32)
     slots = osr.shape[1]
@@ -225,54 +240,55 @@
     else:
         c = arrived(refs[:sections], refs[sections], refs[sections + 1])
         refs = refs[sections + 2 :]
-    al, be, ka, scaling, odt, wg, ws, wn, c_out, gp, g_out, base, rep, bias, *sends = refs
-    width = al.shape[1]
-    half = wn.shape[1]
+    coef, odt, wcat, wnc, pair, low, rep, bias, *sends = refs
     slots = odt.shape[0]
+    width = rep.shape[1]
     h = lax.axis_index("hist")
-    gate_term = c * al[...]
-    pre_term = c * be[...]
-    g = (pre_term * scaling[...]).astype(BF)
-    g_out[...] = g
-    seat = lax.rem(h, mates)
-    w = wn[h * width // half, :, place(seat, width)]
-    out = dot(odt[...], dot(g, w, WIDE).astype(BF)).astype(BF)
+    gate_term = c * coef[:, :width]
+    pre_term = c * coef[:, width : 2 * width]
+    g = (pre_term * coef[:, 3 * width :]).astype(BF)
+    low[:, 2 * width :] = g
+    out = dot(odt[...], dot(g, wnc[...], WIDE).astype(BF)).astype(BF)
     for m in range(mates):
         rep[m * slots : (m + 1) * slots, :] = out[:, m * width : (m + 1) * width]
     both = jnp.concatenate([gate_term.astype(BF), pre_term.astype(BF)], axis=1)
-    gp[...] = both
+    low[:, : 2 * width] = both
     for k in range(sections):
-        rows = place(lax.rem(h + k, sections), width)
-        right = jnp.concatenate([wg[rows, place(h, width)], ws[rows, place(h, width)]], axis=1)
-        out = dot(both, right, WIDE)
+        out = dot(both, wcat[place(lax.rem(h + k, sections), width), :], WIDE)
         if k == 0:
-            base[...] = c * ka[...] + out
+            pair[:, width:] = c * coef[:, 2 * width : 3 * width] + out
         else:
             sends[k - 1][...] = out.astype(BF)
-    c_out[...] = c
+    pair[:, :width] = c
     bias[...] = jnp.broadcast_to(jnp.sum(gate_term, axis=0, keepdims=True), bias.shape)
 
 
 def grad_kernel(steps, mates, *refs):
-    outs = refs[-3:]
-    gs, ns, bs = outs
-    deep = 5 + mates
+    xs = refs[:steps]
+    refs = refs[steps:]
+    gs, ns, bs, held = refs[-4:]
+    deep = 3 + mates
     h = lax.axis_index("hist")
     for t in range(steps):
-        xt, gp, bias, odt, g = refs[deep * t : deep * t + 5]
-        rows = refs[deep * t + 5 : deep * (t + 1)]
-        ent_rows, width = g.shape
+        snapshot = steps - 1 - t
+        low, bias, odt = refs[deep * t : deep * t + 3]
+        rows = refs[deep * t + 3 : deep * (t + 1)]
+        ent_rows = low.shape[0]
+        width = low.shape[1] // 3
         seat = lax.rem(h, mates)
 
         def put(out, at, value):
             out[at] = value if t == 0 else out[at] + value
 
-        put(gs, ..., dot(xt[:ent_rows, :], gp[...], TALL))
+        held[snapshot] = low[:, : 2 * width]
         put(bs, ..., bias[...])
-        replies = dot(odt[...], g[...]).astype(BF)
+        replies = dot(odt[...], low[:, 2 * width :]).astype(BF)
         for m in range(mates):
             source = lax.rem(seat - m + mates, mates)
             put(ns, place(source, width), dot(stacked(rows[m]), replies, TALL))
+    for k in range(steps):
+        value = dot(xs[k][:ent_rows, :], held[lax.rem(h - k + steps, steps)], TALL)
+        gs[...] = value if k == 0 else gs[...] + value
 
 
 def rel_sum(count, refs, total):
@@ -349,7 +365,7 @@
 
             @pl.when(to == t)
             def _():
-                outs[k][...] = saved[t - 1][...]
+                outs[k][...] = saved[t - 1][:, : c.shape[1]]
 
 
 def last_kernel(sections, groups, mates, sizes, factor, *refs):
@@ -404,7 +420,8 @@
     blocks, half = w_neigh.shape[:2]
     mates = sections // blocks
     relations = relation.shape[0]
-    hidden = states[0]
+    hidden = far(states[0])
+    relation, edge_src, edge_rel, edge_dst = map(far, (relation, edge_src, edge_rel, edge_dst))
     bias_row = b_gate.reshape(1, features)
     smem = pl.BlockSpec(memory_space=pltpu.SMEM)
     members = mates * groups
@@ -422,114 +439,117 @@
 
     rows_f32 = sds((ent_rows, width), F32)
     rows_bf = sds((ent_rows, width), BF)
+    last = sections - 1
 
     ins = (hidden, edge_src, edge_rel)
     (xp,) = run(
-        pre_kernel, "pre", ins, [whole(x) for x in ins], [sds((ent_rows + 8, features), BF)]
-    )
-    xs = [xp] + [turn(xp, k) for k in range(1, sections)]
+        pre_kernel, "pre", ins, [whole(x) for x in ins], [far(sds((ent_rows + 8, features), BF))]
+    )
+    xs = [xp] + [far(turn(raw(xp), k)) for k in range(1, sections)]
     (msg,) = run(
         functools.partial(send_kernel, sections, groups),
         "send",
         (hidden, relation, edge_src, edge_dst, edge_rel, send_counts),
         [whole(hidden), whole(relation)] + [whole(edge_src)] * 3 + [smem],
-        [sds((sections * groups, room + 8, width), BF)],
+        [far(sds((sections * groups, room + 8, width), BF))],
     )
     recv = lax.all_to_all(
-        msg, ("hist", "ent"), split_axis=0, concat_axis=0, tiled=True
+        raw(msg), ("hist", "ent"), split_axis=0, concat_axis=0, tiled=True
     ).reshape(sections, groups, room + 8, width)
-    last = sections - 1
-    tops = recv[last]
-    rest = recv[:last]
-    mate_tops = [to_mate(tops, m) for m in range(1, mates)]
-    mate_rest = [to_mate(rest, m) for m in range(1, mates)]
 
     rel_rows = round_up(relations + 1, 8)
     qe = query_ent.reshape(1, -1)
     qr = query_rel.reshape(1, -1)
-    top, rs = run(
+    ins = tuple(map(far, (qe, qr, query_grad, w_gate, w_self, w_neigh, bias_row)))
+    top, rs, wcat, wnc, bias_cols = run(
         query_kernel,
         "query",
-        (qe, qr, query_grad),
-        [whole(qe), whole(qr), whole(query_grad)],
-        [rows_f32, sds((rel_rows, width), F32)],
-    )
-
-    def gather(arrays, specs, count):
-        outs = run(
-            functools.partial(gather_kernel, count),
-            "gather",
-            arrays,
-            specs,
-            [sds((ent_rows, slots), BF), sds((slots, ent_rows), BF), rows_f32, rows_f32] * count,
-        )
-        return [outs[4 * t : 4 * t + 4] for t in range(count)]
-
-    gathered = gather(
-        (rest,) * last, [block(rest.shape[1:], t) for t in range(last)], last
-    ) + gather((tops,), [whole(tops)], 1)
-
-    def pick_t(arrays, tops, t):
-        if t == last:
-            return list(tops), [whole(x) for x in tops]
-        return list(arrays), [block(x.shape[1:], t) for x in arrays]
-
-    def prepare(t):
-        od, odt, scaling, summed = gathered[t]
-        mate, mate_specs = pick_t(mate_rest, mate_tops, t)
-        ins = (scaling, summed, od, w_gate, w_self, w_neigh, bias_row)
-        al, be, ka, osr, rid, xt = run(
+        ins,
+        [whole(x) for x in ins],
+        [
+            far(x)
+            for x in (
+                rows_f32,
+                sds((rel_rows, width), F32),
+                sds((features, 2 * width), BF),
+                sds((half, width), BF),
+                sds((8, width), F32),
+            )
+        ],
+    )
+    recv, held = lax.optimization_barrier((recv, raw(wnc)))
+    wnc = far(held)
+    came_rows = [recv[t] for t in range(sections)]
+    mate_rows = [[to_mate(x, m) for m in range(1, mates)] for x in came_rows]
+    any_space = pl.BlockSpec(memory_space=pl.ANY)
+
+    def prepare(t, *after):
+        received = came_rows[t] if t == last else far(came_rows[t])
+        ins = (*xs, received, *mate_rows[t], wcat, wnc, bias_cols)
+        return run(
             functools.partial(state_kernel, t, sections, mates),
             "state",
-            (*xs, *mate, *ins),
-            [whole(x) for x in xs] + mate_specs + [whole(x) for x in ins],
-            [rows_f32] * 3
-            + [
-                sds((ent_rows, slots), BF),
-                sds((8, slots), jnp.int32),
-                sds((ent_rows + 8, features), BF),
+            ins,
+            [any_space for x in xs] + [whole(x) for x in ins[sections:]],
+            [
+                far(x)
+                for x in (
+                    sds((ent_rows, 4 * width), F32),
+                    sds((slots, ent_rows), BF),
+                    sds((ent_rows, slots), BF),
+                    sds((8, slots), jnp.int32),
+                )
             ],
+            [pltpu.VMEM((ent_rows + 8, features), BF), pltpu.SemaphoreType.DMA],
         )
-        return al, be, ka, scaling, odt, osr, rid, xt
 
     saved = [None] * (sections + 1)
-    grad_ins, grad_specs, rel_ins = [], [], []
+    grad_ins, rel_ins = list(xs), []
     for t in range(last, -1, -1):
-        al, be, ka, scaling, odt, osr, rid, xt = prepare(t)
+        coef, odt, osr, rid = prepare(t)
+        if t > 0:
+            held, *mate_rows[t - 1] = lax.optimization_barrier((raw(coef), *mate_rows[t - 1]))
+            coef = far(held)
         came = (top,) if t == last else (*parts, ret, osr_before)
-        ins = (*came, al, be, ka, scaling, odt, w_gate, w_self, w_neigh)
-        c, gp, g, base, rep, bias, *sends = run(
+        ins = (*came, coef, odt, wcat, wnc)
+        pair, low, rep, bias, *sends = run(
             functools.partial(step_kernel, sections, mates, t == last),
             "step",
             ins,
             [whole(x) for x in ins],
-            [rows_f32, sds((ent_rows, 2 * width), BF), rows_bf, rows_f32]
-            + [sds((mates * slots, width), BF), sds((8, width), F32)]
-            + [rows_bf] * (sections - 1),
+            [
+                far(x)
+                for x in (
+                    sds((ent_rows, 2 * width), F32),
+                    sds((ent_rows, 3 * width), BF),
+                    sds((mates * slots, width), BF),
+                    sds((8, width), F32),
+                    *[rows_bf] * (sections - 1),
+                )
+            ],
         )
-        saved[t + 1] = c
+        saved[t + 1] = pair
         ret = lax.all_to_all(
-            rep.reshape(members, room, width),
+            raw(rep).reshape(members, room, width),
             ("hist", "ent"),
             split_axis=0,
             concat_axis=0,
             tiled=True,
             axis_index_groups=block_groups,
         ).reshape(mates * slots, width)
-        parts = [base] + [turn(x, k + 1) for k, x in enumerate(sends)]
+        parts = [pair] + [turn(raw(x), k + 1) for k, x in enumerate(sends)]
         osr_before = osr
-        rows, rows_specs = pick_t((rest, *mate_rest), (tops, *mate_tops), t)
-        ins = (xt, gp, bias, odt, g)
-        grad_ins += [*ins, *rows]
-        grad_specs += [whole(x) for x in ins] + rows_specs
-        rel_ins += [ret, rid]
+        ins = (low, bias, odt, came_rows[t], *mate_rows[t])
+        grad_ins += [far(x) for x in ins]
+        rel_ins += [far(ret), rid]
 
     gs, ns, bs = run(
         functools.partial(grad_kernel, sections, mates),
         "grad",
         grad_ins,
-        grad_specs,
-        [sds((features, 2 * width), F32), sds((half, width), F32), sds((8, width), F32)],
+        [whole(x) for x in grad_ins],
+        [far(sds((features, 2 * width), F32)), far(sds((half, width), F32)), far(sds((8, width), F32))],
+        [pltpu.VMEM((sections, ent_rows, 2 * width), BF)],
     )
     ins = (*rel_ins[:-2], rs)
     (rs,) = run(
@@ -537,9 +557,39 @@
         "rel",
         ins,
         [whole(x) for x in ins],
-        [sds((rel_rows, width), F32)],
-    )
-
+        [far(sds((rel_rows, width), F32))],
+    )
+    sizes = tuple(
+        round_up(-(-rows // groups), 16) for rows in (features, features, half, rel_rows)
+    )
+    chunk = sum(sizes)
+    pairs = groups // 2
+    ins = (gs, ns, bs, ret, rid, rs)
+    ins = tuple(ins)
+    mine, other = run(
+        functools.partial(pack_kernel, sizes, relations),
+        "pack",
+        ins,
+        [whole(x) for x in ins],
+        [sds((pairs, chunk, width), BF)] * 2,
+        [pltpu.VMEM((rel_rows, width), F32)],
+    )
+    ins = (mine, to_core(other))
+    (landed,) = run(
+        pair_kernel, "pair", ins, [whole(x) for x in ins], [sds((pairs, chunk, width), BF)]
+    )
+    same = [[i for i in range(groups) if i % 2 == core] for core in range(2)]
+
+    def a2a_same(x):
+        return lax.all_to_all(
+            x, "ent", split_axis=0, concat_axis=0, tiled=True, axis_index_groups=same
+        )
+
+    landed, *moved = lax.optimization_barrier((a2a_same(landed), *parts[1:]))
+    parts = [parts[0], *moved]
+    (copies,) = run(
+        add_kernel, "sum", (landed,), [whole(landed)], [sds((pairs, chunk, width), BF)]
+    )
     ins = (*parts, ret, osr_before, *saved[1:sections])
     picks = run(
         functools.partial(pick_kernel, sections),
@@ -549,37 +599,7 @@
         [rows_f32] * sections,
     )
     home = [picks[0]] + [turn(picks[k], k) for k in range(1, sections)]
-
-    sizes = tuple(
-        round_up(-(-rows // groups), 16) for rows in (features, features, half, rel_rows)
-    )
-    chunk = sum(sizes)
-    pairs = groups // 2
-    ins = (gs, ns, bs, ret, rid, rs)
-    mine, other = run(
-        functools.partial(pack_kernel, sizes, relations),
-        "pack",
-        ins,
-        [whole(x) for x in ins],
-        [sds((pairs, chunk, width), BF)] * 2,
-        [pltpu.VMEM((rel_rows, width), F32)],
-    )
-    ins = (mine, to_core(other))
-    (landed,) = run(
-        pair_kernel, "pair", ins, [whole(x) for x in ins], [sds((pairs, chunk, width), BF)]
-    )
-    same = [[i for i in range(groups) if i % 2 == core] for core in range(2)]
-
-    def a2a_same(x):
-        return lax.all_to_all(
-            x, "ent", split_axis=0, concat_axis=0, tiled=True, axis_index_groups=same
-        )
-
-    landed, home = lax.optimization_barrier((a2a_same(landed), home))
-    (copies,) = run(
-        add_kernel, "sum", (landed,), [whole(landed)], [sds((pairs, chunk, width), BF)]
-    )
-    column = a2a_same(copies)
+    column, *home = lax.optimization_barrier((a2a_same(copies), *home))
     mine = [column] + [turn(column, k) for k in range(1, sections)]
     other = [to_core(x) for x in mine]
     ins = (*mine, *other, *home)
@@ -588,6 +608,7 @@
     result, neigh, self_, gate, bias, rel = pl.pallas_call(
         functools.partial(last_kernel, sections, groups, mates, sizes, factor),
         name="last",
+        compiler_params=pltpu.CompilerParams(vmem_limit_bytes=24 << 20),
         grid=(1,),
         in_specs=[whole(x) for x in ins],
         out_specs=[

time: 182 us -> 161 us (0.88)
  blocking collectives: 11.9 us -> 0 us
  Pallas kernels: 56.3 us -> 45.6 us
  starting transfers between devices: 59.4 us -> 67.1 us
  local copies, waits for them, and re-layouts: 7.14 us -> 0.8 us
    all_to_all x1 -> x0, blocking collectives: 11.9 us -> none  [a2a_same(): lax.all_to_all(x, 'ent', split_axis=0, concat_axis=0, tiled=True, axis_in...]
    pallas_call x19 -> x17, Pallas kernels: 52.4 us -> 43.4 us  [run(): pl.pallas_call(body, name=name, in_specs=[spec(s) for s in specs], out_sp...]
    ppermute x21, waiting for transfers between devices: 15.1 us -> 21.9 us  [turn(): lax.ppermute(x, 'hist', [(i, (i + k) % sections) for i in range(sections)])]
    ppermute x2 -> x4, waiting for transfers between devices: 9.15 us -> 2.61 us  [to_mate(): return lax.ppermute(x, 'hist', route)]
    unnamed x96 -> x54, local copies, waits for them, and re-layouts: 7.09 us -> 0.75 us
    ppermute x2 -> x4, starting transfers between devices: 2.06 us -> 6.06 us  [to_mate(): return lax.ppermute(x, 'hist', route)]
    all_to_all x1 -> x2, starting transfers between devices: 3.52 us -> 6.9 us  [a2a_same(): lax.all_to_all(x, 'ent', split_axis=0, concat_axis=0, tiled=True, axis_in...]
    all_to_all x5, waiting for transfers between devices: 17.7 us -> 14.5 us  [the longest x1 9.82 us: on_device(): lax.all_to_all(raw(msg), ('hist', 'ent'), split_axis=0, concat_axis=0, ti...]
  transfers between devices with their start and end apart: 34 -> 37, of which waited for: 23 -> 23; matrix products, arithmetic and copies ran while one was open for 0% -> 0% of each run, Pallas kernels for 15% -> 17%
where the time goes in v2:
time: 161 us; the launch traced here: 159 us
  starting transfers between devices  67.1 us (42%)
  Pallas kernels  45.6 us (28%)
  waiting for transfers between devices  44.7 us (28%)
    pallas_call x17, Pallas kernels, run(): pl.pallas_call(body, name=name, in_specs=[spec(s) for s in specs], out_sp...  43.4 us
    ppermute x21, starting transfers between devices, turn(): lax.ppermute(x, 'hist', [(i, (i + k) % sections) for i in range(sections)])  26.8 us
    ppermute x21, waiting for transfers between devices, turn(): lax.ppermute(x, 'hist', [(i, (i + k) % sections) for i in range(sections)])  21.9 us
    all_to_all x4, starting transfers between devices, on_device(): lax.all_to_all(raw(rep).reshape(members, room, width), ('hist', 'ent'), s...  19.4 us
    all_to_all x1, waiting for transfers between devices, on_device(): lax.all_to_all(raw(msg), ('hist', 'ent'), split_axis=0, concat_axis=0, ti...  9.82 us
    all_to_all x1, starting transfers between devices, on_device(): lax.all_to_all(raw(msg), ('hist', 'ent'), split_axis=0, concat_axis=0, ti...  7.33 us
    all_to_all x2, starting transfers between devices, a2a_same(): lax.all_to_all(x, 'ent', split_axis=0, concat_axis=0, tiled=True, axis_in...  6.9 us
    ppermute x4, starting transfers between devices, to_mate(): return lax.ppermute(x, 'hist', route)  6.06 us
  transfers between devices with their start and end apart: 37, of which 23 were waited for; matrix products, arithmetic and copies ran while one was open for 0% of the time, Pallas kernels for 17%

profile of v2, /device:TPU:0, one launch (start us, length us, event | category | flops | bytes accessed | tf_op | source)
XLA Modules:
  0.0 159.1 jit_solution(9207869054050634400)
XLA Ops:
  1.3 2.5 %send.1 = bf16[32,72,128]{2,1,0:T(8,128)(2,1)} custom-call(bf16[256,512]{1,0:T(8,128)(2,1)} %bitcast.32, bf16[460,512]{1,0:T(8,128)(2,1)} %rel.2, s32[1,512]{1,0:T(1,128)} %src.3, s32[1,512]{1,0:T(1,128)} %dst.1, s32[1,512]{1,0:T(1,128)} %rid.3, s32[1,8]{1,0:T(1,128)S(1)} %copy-done.8), custom_call_target="tpu_custom_call" | custom-call | tf_op jit(solution)/shard_map/send/pallas_call | solution.py:69
  3.8 7.3 %all-to-all-start = ((bf16[32,72,128]{2,1,0:T(8,128)(2,1)}), bf16[32,72,128]{2,1,0:T(8,128)(2,1)S(1)}, u32[]{:S(2)}, u32[]{:S(2)}) async-start(bf16[32,72,128]{2,1,0:T(8,128)(2,1)} %send.1), calls=%async_computation | async-start | bytes 1179648 | tf_op jit(solution)/shard_map/all_to_all | solution.py:456
  12.9 2.7 %collective-permute-start.2 = (bf16[264,512]{1,0:T(8,128)(2,1)}, bf16[264,512]{1,0:T(8,128)(2,1)S(1)}, u32[]{:S(2)}, u32[]{:S(2)}) collective-permute-start(bf16[264,512]{1,0:T(8,128)(2,1)} %pre.1.refs_0_), channel_id=1, source_target_pairs={{0,24},{8,0},{16,8},{24,16},{1,25},{9,1},{17,9},{25,17},{2,26},{10... | collective-permute-start | bytes 811016 | tf_op jit(solution)/shard_map/ppermute | solution.py:431
  16.7 2.7 %query.1 = (f32[256,128]{1,0:T(8,128)}, f32[464,128]{1,0:T(8,128)}, bf16[512,256]{1,0:T(8,128)(2,1)}, bf16[256,128]{1,0:T(8,128)(2,1)}, f32[8,128]{1,0:T(8,128)}) custom-call(s32[1,128]{1,0:T(1,128)} %bitcast.39, s32[1,128]{1,0:T(1,128)} %bitcast.40, f32[128,512]{1,0:T(8,128)} %qg.1, bf16[512,512]{1,0:T(8,128)(2,1)} %wg.1, bf16[512,512]{1,0:T(8,128)(2,1)} %ws.1, ...), custom_call_target="tpu_custom_call" | custom-call | tf_op jit(solution)/shard_map/query/pallas_call | solution.py:69
  19.3 9.8 %all-to-all-done = bf16[32,72,128]{2,1,0:T(8,128)(2,1)S(1)} async-done(((bf16[32,72,128]{2,1,0:T(8,128)(2,1)}), bf16[32,72,128]{2,1,0:T(8,128)(2,1)S(1)}, u32[]{:S(2)}, u32[]{:S(2)}) %all-to-all-start) | async-done | bytes 589856 | tf_op jit(solution)/shard_map/all_to_all | solution.py:456
  33.5 2.5 %collective-permute-done.3.refs_5_.refs_8_ = bf16[8,72,128]{2,1,0:T(8,128)(2,1)S(1)} collective-permute-done((bf16[8,72,128]{2,1,0:T(8,128)(2,1)S(1)}, bf16[8,72,128]{2,1,0:T(8,128)(2,1)S(1)}, u32[]{:S(2)}, u32[]{:S(2)}) %collective-permute-start.3) | collective-permute-done | bytes 147488 | tf_op jit(solution)/shard_map/ppermute | solution.py:435
  36.0 3.4 %state.4 = (f32[256,512]{1,0:T(8,128)}, bf16[512,256]{1,0:T(8,128)(2,1)}, bf16[256,512]{1,0:T(8,128)(2,1)}, s32[8,512]{1,0:T(8,128)}) custom-call(bf16[264,512]{1,0:T(8,128)(2,1)} %pre.1.refs_0_, bf16[264,512]{1,0:T(8,128)(2,1)} %copy-done.11, bf16[264,512]{1,0:T(8,128)(2,1)} %copy-done.10, bf16[264,512]{1,0:T(8,128)(2,1)} %copy-done.9, ...), custom_call_target="tpu_custom_call" | custom-call | tf_op jit(solution)/shard_map/state/pallas_call | solution.py:69
  39.4 2.5 %step.4 = (f32[256,256]{1,0:T(8,128)}, bf16[256,384]{1,0:T(8,128)(2,1)}, bf16[1024,128]{1,0:T(8,128)(2,1)}, f32[8,128]{1,0:T(8,128)}, bf16[256,128]{1,0:T(8,128)...) custom-call(f32[256,128]{1,0:T(8,128)} %get-tuple-element.87.refs_0_, f32[256,512]{1,0:T(8,128)} %get-tuple-element.94.refs_1_, ...), custom_call_target="tpu_custom_call" | custom-call | tf_op jit(solution)/shard_map/step/pallas_call | solution.py:69
  42.0 4.7 %all-to-all-start.1 = ((bf16[16,64,128]{2,1,0:T(8,128)(2,1)}), bf16[16,64,128]{2,1,0:T(8,128)(2,1)S(1)}, u32[]{:S(2)}, u32[]{:S(2)}) async-start(bf16[16,64,128]{2,1,0:T(8,128)(2,1)} %bitcast.36), calls=%async_computation.1 | async-start | bytes 524288 | tf_op jit(solution)/shard_map/all_to_all | solution.py:532
  50.1 2.8 %collective-permute-start.7 = (bf16[256,128]{1,0:T(8,128)(2,1)S(1)}, bf16[256,128]{1,0:T(8,128)(2,1)S(1)}, u32[]{:S(2)}, u32[]{:S(2)}) collective-permute-start(bf16[256,128]{1,0:T(8,128)(2,1)S(1)} %copy-done.20), channel_id=1, source_target_pairs={{0,24},{8,0},{16,8},{24,16},{1,25},{9,1},{17,9},{25,17},{2,26},{10... | collective-permute-start | bytes 196616 | tf_op jit(solution)/shard_map/ppermute | solution.py:431
  52.9 3.4 %state.5 = (f32[256,512]{1,0:T(8,128)}, bf16[512,256]{1,0:T(8,128)(2,1)}, bf16[256,512]{1,0:T(8,128)(2,1)}, s32[8,512]{1,0:T(8,128)}) custom-call(bf16[264,512]{1,0:T(8,128)(2,1)} %pre.1.refs_0_, bf16[264,512]{1,0:T(8,128)(2,1)} %copy-done.11, bf16[264,512]{1,0:T(8,128)(2,1)} %copy-done.10, bf16[264,512]{1,0:T(8,128)(2,1)} %copy-done.9, ...), custom_call_target="tpu_custom_call" | custom-call | tf_op jit(solution)/shard_map/state/pallas_call | solution.py:69
  58.6 2.9 %step.5 = (f32[256,256]{1,0:T(8,128)}, bf16[256,384]{1,0:T(8,128)(2,1)}, bf16[1024,128]{1,0:T(8,128)(2,1)}, f32[8,128]{1,0:T(8,128)}, bf16[256,128]{1,0:T(8,128)...) custom-call(f32[256,256]{1,0:T(8,128)} %get-tuple-element.98.refs_0_, ...), custom_call_target="tpu_custom_call" | custom-call | tf_op jit(solution)/shard_map/step/pallas_call | solution.py:69
  61.5 5.6 %all-to-all-start.2 = ((bf16[16,64,128]{2,1,0:T(8,128)(2,1)}), bf16[16,64,128]{2,1,0:T(8,128)(2,1)S(1)}, u32[]{:S(2)}, u32[]{:S(2)}) async-start(bf16[16,64,128]{2,1,0:T(8,128)(2,1)} %bitcast.35), calls=%async_computation.2 | async-start | bytes 524288 | tf_op jit(solution)/shard_map/all_to_all | solution.py:532
  69.9 2.8 %collective-permute-start.11 = (bf16[256,128]{1,0:T(8,128)(2,1)S(1)}, bf16[256,128]{1,0:T(8,128)(2,1)S(1)}, u32[]{:S(2)}, u32[]{:S(2)}) collective-permute-start(bf16[256,128]{1,0:T(8,128)(2,1)S(1)} %copy-done.18), channel_id=1, source_target_pairs={{0,24},{8,0},{16,8},{24,16},{1,25},{9,1},{17,9},{25,17},{2,26},{10... | collective-permute-start | bytes 196616 | tf_op jit(solution)/shard_map/ppermute | solution.py:431
  72.8 3.4 %state.6 = (f32[256,512]{1,0:T(8,128)}, bf16[512,256]{1,0:T(8,128)(2,1)}, bf16[256,512]{1,0:T(8,128)(2,1)}, s32[8,512]{1,0:T(8,128)}) custom-call(bf16[264,512]{1,0:T(8,128)(2,1)} %pre.1.refs_0_, bf16[264,512]{1,0:T(8,128)(2,1)} %copy-done.11, bf16[264,512]{1,0:T(8,128)(2,1)} %copy-done.10, bf16[264,512]{1,0:T(8,128)(2,1)} %copy-done.9, ...), custom_call_target="tpu_custom_call" | custom-call | tf_op jit(solution)/shard_map/state/pallas_call | solution.py:69
  79.0 2.9 %step.6 = (f32[256,256]{1,0:T(8,128)}, bf16[256,384]{1,0:T(8,128)(2,1)}, bf16[1024,128]{1,0:T(8,128)(2,1)}, f32[8,128]{1,0:T(8,128)}, bf16[256,128]{1,0:T(8,128)...) custom-call(f32[256,256]{1,0:T(8,128)} %get-tuple-element.110.refs_0_.refs_8_, ...), custom_call_target="tpu_custom_call" | custom-call | tf_op jit(solution)/shard_map/step/pallas_call | solution.py:69
  81.9 5.0 %all-to-all-start.3 = ((bf16[16,64,128]{2,1,0:T(8,128)(2,1)}), bf16[16,64,128]{2,1,0:T(8,128)(2,1)S(1)}, u32[]{:S(2)}, u32[]{:S(2)}) async-start(bf16[16,64,128]{2,1,0:T(8,128)(2,1)} %bitcast.37), calls=%async_computation.3 | async-start | bytes 524288 | tf_op jit(solution)/shard_map/all_to_all | solution.py:532
  91.2 3.3 %state.7 = (f32[256,512]{1,0:T(8,128)}, bf16[512,256]{1,0:T(8,128)(2,1)}, bf16[256,512]{1,0:T(8,128)(2,1)}, s32[8,512]{1,0:T(8,128)}) custom-call(bf16[264,512]{1,0:T(8,128)(2,1)} %pre.1.refs_0_, bf16[264,512]{1,0:T(8,128)(2,1)} %copy-done.11, bf16[264,512]{1,0:T(8,128)(2,1)} %copy-done.10, bf16[264,512]{1,0:T(8,128)(2,1)} %copy-done.9, ...), custom_call_target="tpu_custom_call" | custom-call | tf_op jit(solution)/shard_map/state/pallas_call | solution.py:69
  96.9 2.9 %step.7 = (f32[256,256]{1,0:T(8,128)}, bf16[256,384]{1,0:T(8,128)(2,1)}, bf16[1024,128]{1,0:T(8,128)(2,1)}, f32[8,128]{1,0:T(8,128)}, bf16[256,128]{1,0:T(8,128)...) custom-call(f32[256,256]{1,0:T(8,128)} %get-tuple-element.122.refs_0_.refs_7_, ...), custom_call_target="tpu_custom_call" | custom-call | tf_op jit(solution)/shard_map/step/pallas_call | solution.py:69
  99.8 4.1 %all-to-all-start.4 = ((bf16[16,64,128]{2,1,0:T(8,128)(2,1)}), bf16[16,64,128]{2,1,0:T(8,128)(2,1)S(1)}, u32[]{:S(2)}, u32[]{:S(2)}) async-start(bf16[16,64,128]{2,1,0:T(8,128)(2,1)} %bitcast.34), calls=%async_computation.4 | async-start | bytes 524288 | tf_op jit(solution)/shard_map/all_to_all | solution.py:532
  104.0 2.8 %rel.3.old = f32[464,128]{1,0:T(8,128)} custom-call(bf16[1024,128]{1,0:T(8,128)(2,1)} %bitcast.26, s32[8,512]{1,0:T(8,128)} %get-tuple-element.138.refs_1_, bf16[1024,128]{1,0:T(8,128)(2,1)} %bitcast.28, s32[8,512]{1,0:T(8,128)} %get-tuple-element.139.refs_3_, bf16[1024,128]{1,0:T(8,128)(2,1)} %bitcast.30, s32[8,512]{1,0:T(8,128)} %get-tuple-element.140.refs_5_, ...), custom_call_target="tpu_custom_call" | custom-call | tf_op jit(solution)/shard_map/rel/pallas_call | solution.py:69
  106.8 4.1 %grad.1 = (f32[512,256]{1,0:T(8,128)}, f32[256,128]{1,0:T(8,128)}, f32[8,128]{1,0:T(8,128)}) custom-call(bf16[264,512]{1,0:T(8,128)(2,1)} %pre.1.refs_0_, bf16[264,512]{1,0:T(8,128)(2,1)} %copy-done.11, bf16[264,512]{1,0:T(8,128)(2,1)} %copy-done.10, bf16[264,512]{1,0:T(8,128)(2,1)} %copy-done.9, bf16[256,384]{1,0:T(8,128)(2,1)} %get-tuple-element.96.refs_4_, ...), custom_call_target="tpu_custom_call" | custom-call | tf_op jit(solution)/shard_map/grad/pallas_call | solution.py:69
  110.9 3.0 %all-to-all-done.4 = bf16[16,64,128]{2,1,0:T(8,128)(2,1)S(1)} async-done(((bf16[16,64,128]{2,1,0:T(8,128)(2,1)}), bf16[16,64,128]{2,1,0:T(8,128)(2,1)S(1)}, u32[]{:S(2)}, u32[]{:S(2)}) %all-to-all-start.4) | async-done | bytes 262176 | tf_op jit(solution)/shard_map/all_to_all | solution.py:532
  118.0 3.5 %all-to-all-start.5 = ((bf16[4,224,128]{2,1,0:T(8,128)(2,1)}), bf16[4,224,128]{2,1,0:T(8,128)(2,1)S(1)}, u32[]{:S(2)}, u32[]{:S(2)}) async-start(bf16[4,224,128]{2,1,0:T(8,128)(2,1)} %pair.1), calls=%async_computation.5 | async-start | bytes 458752 | tf_op jit(solution)/shard_map/all_to_all | solution.py:584
  122.9 2.4 %collective-permute-start.19 = (bf16[256,128]{1,0:T(8,128)(2,1)S(1)}, bf16[256,128]{1,0:T(8,128)(2,1)S(1)}, u32[]{:S(2)}, u32[]{:S(2)}) collective-permute-start(bf16[256,128]{1,0:T(8,128)(2,1)S(1)} %copy-done.15), channel_id=1, source_target_pairs={{0,24},{8,0},{16,8},{24,16},{1,25},{9,1},{17,9},{25,17},{2,26},{10... | collective-permute-start | bytes 196616 | tf_op jit(solution)/shard_map/ppermute | solution.py:431
  127.4 2.8 %all-to-all-done.5.x = bf16[4,224,128]{2,1,0:T(8,128)(2,1)S(1)} async-done(((bf16[4,224,128]{2,1,0:T(8,128)(2,1)}), bf16[4,224,128]{2,1,0:T(8,128)(2,1)S(1)}, u32[]{:S(2)}, u32[]{:S(2)}) %all-to-all-start.5) | async-done | bytes 229408 | tf_op jit(solution)/shard_map/all_to_all | solution.py:584
  130.9 3.4 %all-to-all-start.6 = ((bf16[4,224,128]{2,1,0:T(8,128)(2,1)}), bf16[4,224,128]{2,1,0:T(8,128)(2,1)S(1)}, u32[]{:S(2)}, u32[]{:S(2)}) async-start(bf16[4,224,128]{2,1,0:T(8,128)(2,1)} %sum.1), calls=%async_computation.6 | async-start | bytes 458752 | tf_op jit(solution)/shard_map/all_to_all | solution.py:584
  139.7 2.5 %collective-permute-done.20.refs_9_ = f32[256,128]{1,0:T(8,128)S(1)} collective-permute-done((f32[256,128]{1,0:T(8,128)S(1)}, f32[256,128]{1,0:T(8,128)S(1)}, u32[]{:S(2)}, u32[]{:S(2)}) %collective-permute-start.20) | collective-permute-done | bytes 131104 | tf_op jit(solution)/shard_map/ppermute | solution.py:431
  143.5 2.1 %collective-permute-start.25 = (bf16[4,224,128]{2,1,0:T(8,128)(2,1)S(1)}, bf16[4,224,128]{2,1,0:T(8,128)(2,1)S(1)}, u32[]{:S(2)}, u32[]{:S(2)}) collective-permute-start(bf16[4,224,128]{2,1,0:T(8,128)(2,1)S(1)} %all-to-all-done.6.refs_0_), channel_id=1, source_target_pairs={{0,24},{8,0},{16,8},{24,16},{1,25},{9,1},{17,9},{25,17},{2,26},{10... | collective-permute-start | bytes 688136 | tf_op jit(solution)/shard_map/ppermute | solution.py:431
  146.9 4.4 %collective-permute-done.25.refs_3_ = bf16[4,224,128]{2,1,0:T(8,128)(2,1)S(1)} collective-permute-done((bf16[4,224,128]{2,1,0:T(8,128)(2,1)S(1)}, bf16[4,224,128]{2,1,0:T(8,128)(2,1)S(1)}, u32[]{:S(2)}, u32[]{:S(2)}) %collective-permute-start.25) | collective-permute-done | bytes 229408 | tf_op jit(solution)/shard_map/ppermute | solution.py:431
  151.3 3.9 %collective-permute-done.24.refs_2_ = bf16[4,224,128]{2,1,0:T(8,128)(2,1)S(1)} collective-permute-done((bf16[4,224,128]{2,1,0:T(8,128)(2,1)S(1)}, bf16[4,224,128]{2,1,0:T(8,128)(2,1)S(1)}, u32[]{:S(2)}, u32[]{:S(2)}) %collective-permute-start.24) | collective-permute-done | bytes 229408 | tf_op jit(solution)/shard_map/ppermute | solution.py:431
  157.0 2.1 %last.1 = (f32[256,512]{1,0:T(8,128)}, f32[2,256,256]{2,1,0:T(8,128)}, f32[512,512]{1,0:T(8,128)}, f32[512,512]{1,0:T(8,128)}, f32[1,512]{1,0:T(1,128)}, /*index=5*/f32[460,512]{1,0:T(8,128)}) custom-call(bf16[4,224,128]{2,1,0:T(8,128)(2,1)S(1)} %all-to-all-done.6.refs_0_, bf16[4,224,128]{2,1,0:T(8,128)(2,1)S(1)} %collective-permute-done.23.refs_1_, ...), custom_call_target="tpu_custom_call" | custom-call | tf_op jit(solution)/shard_map/last/pallas_call | solution.py:608
  (115 shorter events, 43.7 us)
Async XLA Ops:
  3.8 25.3 %all-to-all-start = ((bf16[32,72,128]{2,1,0:T(8,128)(2,1)}), bf16[32,72,128]{2,1,0:T(8,128)(2,1)S(1)}, u32[]{:S(2)}, u32[]{:S(2)}) async-start(bf16[32,72,128]{2,1,0:T(8,128)(2,1)} %send.1), calls=%async_computation | async-start | bytes 1179648 | tf_op jit(solution)/shard_map/all_to_all | solution.py:456
  12.9 18.5 %collective-permute-start.2 = (bf16[264,512]{1,0:T(8,128)(2,1)}, bf16[264,512]{1,0:T(8,128)(2,1)S(1)}, u32[]{:S(2)}, u32[]{:S(2)}) collective-permute-start(bf16[264,512]{1,0:T(8,128)(2,1)} %pre.1.refs_0_), channel_id=1, source_target_pairs={{0,24},{8,0},{16,8},{24,16},{1,25},{9,1},{17,9},{25,17},{2,26},{10... | collective-permute-start | bytes 811016 | tf_op jit(solution)/shard_map/ppermute | solution.py:431
  15.5 17.0 %collective-permute-start.1 = (bf16[264,512]{1,0:T(8,128)(2,1)}, bf16[264,512]{1,0:T(8,128)(2,1)S(1)}, u32[]{:S(2)}, u32[]{:S(2)}) collective-permute-start(bf16[264,512]{1,0:T(8,128)(2,1)} %pre.1.refs_0_), channel_id=1, source_target_pairs={{0,16},{8,24},{16,0},{24,8},{1,17},{9,25},{17,1},{25,9},{2,18},{10... | collective-permute-start | bytes 811016 | tf_op jit(solution)/shard_map/ppermute | solution.py:431
  16.1 17.4 %collective-permute-start = (bf16[264,512]{1,0:T(8,128)(2,1)}, bf16[264,512]{1,0:T(8,128)(2,1)S(1)}, u32[]{:S(2)}, u32[]{:S(2)}) collective-permute-start(bf16[264,512]{1,0:T(8,128)(2,1)} %pre.1.refs_0_), channel_id=1, source_target_pairs={{0,8},{8,16},{16,24},{24,0},{1,9},{9,17},{17,25},{25,1},{2,10},{10... | collective-permute-start | bytes 811016 | tf_op jit(solution)/shard_map/ppermute | solution.py:431
  29.2 6.8 %collective-permute-start.3 = (bf16[8,72,128]{2,1,0:T(8,128)(2,1)S(1)}, bf16[8,72,128]{2,1,0:T(8,128)(2,1)S(1)}, u32[]{:S(2)}, u32[]{:S(2)}) collective-permute-start(bf16[8,72,128]{2,1,0:T(8,128)(2,1)S(1)} %get-tuple-element.171.refs_4_.refs_7_), channel_id=1, source_target_pairs={{0,8},{8,0},{16,24},{24,16},{1,9},{9,1},{17,25},{25,17},{2,10},{10... | collective-permute-start | bytes 442376 | tf_op jit(solution)/shard_map/ppermute | solution.py:435
  29.3 10.1 %collective-permute-start.4 = (bf16[8,72,128]{2,1,0:T(8,128)(2,1)S(1)}, bf16[8,72,128]{2,1,0:T(8,128)(2,1)S(1)}, u32[]{:S(2)}, u32[]{:S(2)}) collective-permute-start(bf16[8,72,128]{2,1,0:T(8,128)(2,1)S(1)} %get-tuple-element.170.refs_4_.refs_12_), channel_id=1, source_target_pairs={{0,8},{8,0},{16,24},{24,16},{1,9},{9,1},{17,25},{25,17},{2,10},{10... | collective-permute-start | bytes 442376 | tf_op jit(solution)/shard_map/ppermute | solution.py:435
  42.0 16.6 %all-to-all-start.1 = ((bf16[16,64,128]{2,1,0:T(8,128)(2,1)}), bf16[16,64,128]{2,1,0:T(8,128)(2,1)S(1)}, u32[]{:S(2)}, u32[]{:S(2)}) async-start(bf16[16,64,128]{2,1,0:T(8,128)(2,1)} %bitcast.36), calls=%async_computation.1 | async-start | bytes 524288 | tf_op jit(solution)/shard_map/all_to_all | solution.py:532
  46.7 9.7 %collective-permute-start.8 = (bf16[8,72,128]{2,1,0:T(8,128)(2,1)S(1)}, bf16[8,72,128]{2,1,0:T(8,128)(2,1)S(1)}, u32[]{:S(2)}, u32[]{:S(2)}) collective-permute-start(bf16[8,72,128]{2,1,0:T(8,128)(2,1)S(1)} %get-tuple-element.169.refs_4_.refs_17_), channel_id=1, source_target_pairs={{0,8},{8,0},{16,24},{24,16},{1,9},{9,1},{17,25},{25,17},{2,10},{10... | collective-permute-start | bytes 442376 | tf_op jit(solution)/shard_map/ppermute | solution.py:435
  48.7 9.8 %collective-permute-start.5 = (bf16[256,128]{1,0:T(8,128)(2,1)S(1)}, bf16[256,128]{1,0:T(8,128)(2,1)S(1)}, u32[]{:S(2)}, u32[]{:S(2)}) collective-permute-start(bf16[256,128]{1,0:T(8,128)(2,1)S(1)} %copy-done.24), channel_id=1, source_target_pairs={{0,8},{8,16},{16,24},{24,0},{1,9},{9,17},{17,25},{25,1},{2,10},{10... | collective-permute-start | bytes 196616 | tf_op jit(solution)/shard_map/ppermute | solution.py:431
  48.8 9.7 %collective-permute-start.6 = (bf16[256,128]{1,0:T(8,128)(2,1)S(1)}, bf16[256,128]{1,0:T(8,128)(2,1)S(1)}, u32[]{:S(2)}, u32[]{:S(2)}) collective-permute-start(bf16[256,128]{1,0:T(8,128)(2,1)S(1)} %copy-done.22), channel_id=1, source_target_pairs={{0,16},{8,24},{16,0},{24,8},{1,17},{9,25},{17,1},{25,9},{2,18},{10... | collective-permute-start | bytes 196616 | tf_op jit(solution)/shard_map/ppermute | solution.py:431
  50.1 8.5 %collective-permute-start.7 = (bf16[256,128]{1,0:T(8,128)(2,1)S(1)}, bf16[256,128]{1,0:T(8,128)(2,1)S(1)}, u32[]{:S(2)}, u32[]{:S(2)}) collective-permute-start(bf16[256,128]{1,0:T(8,128)(2,1)S(1)} %copy-done.20), channel_id=1, source_target_pairs={{0,24},{8,0},{16,8},{24,16},{1,25},{9,1},{17,9},{25,17},{2,26},{10... | collective-permute-start | bytes 196616 | tf_op jit(solution)/shard_map/ppermute | solution.py:431
  61.5 17.5 %all-to-all-start.2 = ((bf16[16,64,128]{2,1,0:T(8,128)(2,1)}), bf16[16,64,128]{2,1,0:T(8,128)(2,1)S(1)}, u32[]{:S(2)}, u32[]{:S(2)}) async-start(bf16[16,64,128]{2,1,0:T(8,128)(2,1)} %bitcast.35), calls=%async_computation.2 | async-start | bytes 524288 | tf_op jit(solution)/shard_map/all_to_all | solution.py:532
  67.1 9.2 %collective-permute-start.12 = (bf16[8,72,128]{2,1,0:T(8,128)(2,1)S(1)}, bf16[8,72,128]{2,1,0:T(8,128)(2,1)S(1)}, u32[]{:S(2)}, u32[]{:S(2)}) collective-permute-start(bf16[8,72,128]{2,1,0:T(8,128)(2,1)S(1)} %get-tuple-element.168.refs_4_.refs_22_), channel_id=1, source_target_pairs={{0,8},{8,0},{16,24},{24,16},{1,9},{9,1},{17,25},{25,17},{2,10},{10... | collective-permute-start | bytes 442376 | tf_op jit(solution)/shard_map/ppermute | solution.py:435
  69.1 9.2 %collective-permute-start.9 = (bf16[256,128]{1,0:T(8,128)(2,1)S(1)}, bf16[256,128]{1,0:T(8,128)(2,1)S(1)}, u32[]{:S(2)}, u32[]{:S(2)}) collective-permute-start(bf16[256,128]{1,0:T(8,128)(2,1)S(1)} %copy-done.21), channel_id=1, source_target_pairs={{0,8},{8,16},{16,24},{24,0},{1,9},{9,17},{17,25},{25,1},{2,10},{10... | collective-permute-start | bytes 196616 | tf_op jit(solution)/shard_map/ppermute | solution.py:431
  69.2 9.1 %collective-permute-start.10 = (bf16[256,128]{1,0:T(8,128)(2,1)S(1)}, bf16[256,128]{1,0:T(8,128)(2,1)S(1)}, u32[]{:S(2)}, u32[]{:S(2)}) collective-permute-start(bf16[256,128]{1,0:T(8,128)(2,1)S(1)} %copy-done.19), channel_id=1, source_target_pairs={{0,16},{8,24},{16,0},{24,8},{1,17},{9,25},{17,1},{25,9},{2,18},{10... | collective-permute-start | bytes 196616 | tf_op jit(solution)/shard_map/ppermute | solution.py:431
  69.9 9.0 %collective-permute-start.11 = (bf16[256,128]{1,0:T(8,128)(2,1)S(1)}, bf16[256,128]{1,0:T(8,128)(2,1)S(1)}, u32[]{:S(2)}, u32[]{:S(2)}) collective-permute-start(bf16[256,128]{1,0:T(8,128)(2,1)S(1)} %copy-done.18), channel_id=1, source_target_pairs={{0,24},{8,0},{16,8},{24,16},{1,25},{9,1},{17,9},{25,17},{2,26},{10... | collective-permute-start | bytes 196616 | tf_op jit(solution)/shard_map/ppermute | solution.py:431
  81.9 15.0 %all-to-all-start.3 = ((bf16[16,64,128]{2,1,0:T(8,128)(2,1)}), bf16[16,64,128]{2,1,0:T(8,128)(2,1)S(1)}, u32[]{:S(2)}, u32[]{:S(2)}) async-start(bf16[16,64,128]{2,1,0:T(8,128)(2,1)} %bitcast.37), calls=%async_computation.3 | async-start | bytes 524288 | tf_op jit(solution)/shard_map/all_to_all | solution.py:532
  86.9 7.7 %collective-permute-start.13 = (bf16[256,128]{1,0:T(8,128)(2,1)S(1)}, bf16[256,128]{1,0:T(8,128)(2,1)S(1)}, u32[]{:S(2)}, u32[]{:S(2)}) collective-permute-start(bf16[256,128]{1,0:T(8,128)(2,1)S(1)} %copy-done.26), channel_id=1, source_target_pairs={{0,8},{8,16},{16,24},{24,0},{1,9},{9,17},{17,25},{25,1},{2,10},{10... | collective-permute-start | bytes 196616 | tf_op jit(solution)/shard_map/ppermute | solution.py:431
  88.9 5.8 %collective-permute-start.14 = (bf16[256,128]{1,0:T(8,128)(2,1)S(1)}, bf16[256,128]{1,0:T(8,128)(2,1)S(1)}, u32[]{:S(2)}, u32[]{:S(2)}) collective-permute-start(bf16[256,128]{1,0:T(8,128)(2,1)S(1)} %copy-done.25), channel_id=1, source_target_pairs={{0,16},{8,24},{16,0},{24,8},{1,17},{9,25},{17,1},{25,9},{2,18},{10... | collective-permute-start | bytes 196616 | tf_op jit(solution)/shard_map/ppermute | solution.py:431
  90.2 5.0 %collective-permute-start.15 = (bf16[256,128]{1,0:T(8,128)(2,1)S(1)}, bf16[256,128]{1,0:T(8,128)(2,1)S(1)}, u32[]{:S(2)}, u32[]{:S(2)}) collective-permute-start(bf16[256,128]{1,0:T(8,128)(2,1)S(1)} %copy-done.23), channel_id=1, source_target_pairs={{0,24},{8,0},{16,8},{24,16},{1,25},{9,1},{17,9},{25,17},{2,26},{10... | collective-permute-start | bytes 196616 | tf_op jit(solution)/shard_map/ppermute | solution.py:431
  99.8 14.1 %all-to-all-start.4 = ((bf16[16,64,128]{2,1,0:T(8,128)(2,1)}), bf16[16,64,128]{2,1,0:T(8,128)(2,1)S(1)}, u32[]{:S(2)}, u32[]{:S(2)}) async-start(bf16[16,64,128]{2,1,0:T(8,128)(2,1)} %bitcast.34), calls=%async_computation.4 | async-start | bytes 524288 | tf_op jit(solution)/shard_map/all_to_all | solution.py:532
  118.0 12.2 %all-to-all-start.5 = ((bf16[4,224,128]{2,1,0:T(8,128)(2,1)}), bf16[4,224,128]{2,1,0:T(8,128)(2,1)S(1)}, u32[]{:S(2)}, u32[]{:S(2)}) async-start(bf16[4,224,128]{2,1,0:T(8,128)(2,1)} %pair.1), calls=%async_computation.5 | async-start | bytes 458752 | tf_op jit(solution)/shard_map/all_to_all | solution.py:584
  121.5 5.8 %collective-permute-start.17 = (bf16[256,128]{1,0:T(8,128)(2,1)S(1)}, bf16[256,128]{1,0:T(8,128)(2,1)S(1)}, u32[]{:S(2)}, u32[]{:S(2)}) collective-permute-start(bf16[256,128]{1,0:T(8,128)(2,1)S(1)} %copy-done.17), channel_id=1, source_target_pairs={{0,8},{8,16},{16,24},{24,0},{1,9},{9,17},{17,25},{25,1},{2,10},{10... | collective-permute-start | bytes 196616 | tf_op jit(solution)/shard_map/ppermute | solution.py:431
  122.1 5.3 %collective-permute-start.18 = (bf16[256,128]{1,0:T(8,128)(2,1)S(1)}, bf16[256,128]{1,0:T(8,128)(2,1)S(1)}, u32[]{:S(2)}, u32[]{:S(2)}) collective-permute-start(bf16[256,128]{1,0:T(8,128)(2,1)S(1)} %copy-done.16), channel_id=1, source_target_pairs={{0,16},{8,24},{16,0},{24,8},{1,17},{9,25},{17,1},{25,9},{2,18},{10... | collective-permute-start | bytes 196616 | tf_op jit(solution)/shard_map/ppermute | solution.py:431
  130.9 12.6 %all-to-all-start.6 = ((bf16[4,224,128]{2,1,0:T(8,128)(2,1)}), bf16[4,224,128]{2,1,0:T(8,128)(2,1)S(1)}, u32[]{:S(2)}, u32[]{:S(2)}) async-start(bf16[4,224,128]{2,1,0:T(8,128)(2,1)} %sum.1), calls=%async_computation.6 | async-start | bytes 458752 | tf_op jit(solution)/shard_map/all_to_all | solution.py:584
  136.0 6.2 %collective-permute-start.20 = (f32[256,128]{1,0:T(8,128)S(1)}, f32[256,128]{1,0:T(8,128)S(1)}, u32[]{:S(2)}, u32[]{:S(2)}) collective-permute-start(f32[256,128]{1,0:T(8,128)S(1)} %get-tuple-element.154), channel_id=1, source_target_pairs={{0,8},{8,16},{16,24},{24,0},{1,9},{9,17},{17,25},{25,1},{2,10},{10... | collective-permute-start | bytes 393224 | tf_op jit(solution)/shard_map/ppermute | solution.py:431
  137.6 5.8 %collective-permute-start.21 = (f32[256,128]{1,0:T(8,128)S(1)}, f32[256,128]{1,0:T(8,128)S(1)}, u32[]{:S(2)}, u32[]{:S(2)}) collective-permute-start(f32[256,128]{1,0:T(8,128)S(1)} %get-tuple-element.155), channel_id=1, source_target_pairs={{0,16},{8,24},{16,0},{24,8},{1,17},{9,25},{17,1},{25,9},{2,18},{10... | collective-permute-start | bytes 393224 | tf_op jit(solution)/shard_map/ppermute | solution.py:431
  138.4 5.1 %collective-permute-start.22 = (f32[256,128]{1,0:T(8,128)S(1)}, f32[256,128]{1,0:T(8,128)S(1)}, u32[]{:S(2)}, u32[]{:S(2)}) collective-permute-start(f32[256,128]{1,0:T(8,128)S(1)} %get-tuple-element.156), channel_id=1, source_target_pairs={{0,24},{8,0},{16,8},{24,16},{1,25},{9,1},{17,9},{25,17},{2,26},{10... | collective-permute-start | bytes 393224 | tf_op jit(solution)/shard_map/ppermute | solution.py:431
  143.5 7.8 %collective-permute-start.25 = (bf16[4,224,128]{2,1,0:T(8,128)(2,1)S(1)}, bf16[4,224,128]{2,1,0:T(8,128)(2,1)S(1)}, u32[]{:S(2)}, u32[]{:S(2)}) collective-permute-start(bf16[4,224,128]{2,1,0:T(8,128)(2,1)S(1)} %all-to-all-done.6.refs_0_), channel_id=1, source_target_pairs={{0,24},{8,0},{16,8},{24,16},{1,25},{9,1},{17,9},{25,17},{2,26},{10... | collective-permute-start | bytes 688136 | tf_op jit(solution)/shard_map/ppermute | solution.py:431
  145.6 9.5 %collective-permute-start.24 = (bf16[4,224,128]{2,1,0:T(8,128)(2,1)S(1)}, bf16[4,224,128]{2,1,0:T(8,128)(2,1)S(1)}, u32[]{:S(2)}, u32[]{:S(2)}) collective-permute-start(bf16[4,224,128]{2,1,0:T(8,128)(2,1)S(1)} %all-to-all-done.6.refs_0_), channel_id=1, source_target_pairs={{0,16},{8,24},{16,0},{24,8},{1,17},{9,25},{17,1},{25,9},{2,18},{10... | collective-permute-start | bytes 688136 | tf_op jit(solution)/shard_map/ppermute | solution.py:431
  146.9 8.3 %collective-permute-start.23 = (bf16[4,224,128]{2,1,0:T(8,128)(2,1)S(1)}, bf16[4,224,128]{2,1,0:T(8,128)(2,1)S(1)}, u32[]{:S(2)}, u32[]{:S(2)}) collective-permute-start(bf16[4,224,128]{2,1,0:T(8,128)(2,1)S(1)} %all-to-all-done.6.refs_0_), channel_id=1, source_target_pairs={{0,8},{8,16},{16,24},{24,0},{1,9},{9,17},{17,25},{25,1},{2,10},{10... | collective-permute-start | bytes 688136 | tf_op jit(solution)/shard_map/ppermute | solution.py:431
  146.9 8.8 %collective-permute-start.26 = (bf16[4,224,128]{2,1,0:T(8,128)(2,1)S(1)}, bf16[4,224,128]{2,1,0:T(8,128)(2,1)S(1)}, u32[]{:S(2)}, u32[]{:S(2)}) collective-permute-start(bf16[4,224,128]{2,1,0:T(8,128)(2,1)S(1)} %all-to-all-done.6.refs_0_), channel_id=1, source_target_pairs={{0,1},{1,0},{2,3},{3,2},{4,5},{5,4},{6,7},{7,6},{8,9},{9,8},{10,11... | collective-permute-start | bytes 688136 | tf_op jit(solution)/shard_map/ppermute | solution.py:438
  (32 other events, 236.3 us)

commit v3 on v2

--- a/solution.py
+++ b/solution.py
@@ -8,11 +8,11 @@
 from jax.experimental.pallas import tpu as pltpu
 from jax.sharding import PartitionSpec as P
 
+
 BF = jnp.bfloat16
 F32 = jnp.float32
 TALL = (((0,), (0,)), ((), ()))
 WIDE = (((1,), (1,)), ((), ()))
-LANES = 128
 
 
 def dot(a, b, dims=(((1,), (0,)), ((), ()))):
@@ -52,7 +52,7 @@
     return block(x.shape)
 
 
-def run(body, name, ins, specs, outs, scratch=(), limit=16):
+def run(body, ins, specs, outs, scratch=(), limit=16):
     tiled = any(s.block_shape and None in s.block_shape for s in specs)
     near = pl.BlockSpec(memory_space=pltpu.VMEM)
 
@@ -68,7 +68,6 @@
     ]
     results = pl.pallas_call(
         body,
-        name=name,
         in_specs=[spec(s) for s in specs],
         out_specs=[spec(block(o.shape)) for o in shapes],
         out_shape=shapes,
@@ -133,6 +132,7 @@
         for target in range(sections):
             msg[target * groups + u, room:, :] = row
 
+
 def stacked(recv):
     return jnp.concatenate([recv[i, : recv.shape[1] - 8, :] for i in range(recv.shape[0])], axis=0)
 
@@ -146,59 +146,108 @@
             act(k)
 
 
-def state_kernel(t, sections, mates, *refs):
-    xs = refs[:sections]
-    recv = refs[sections]
-    mate_rows = refs[sections + 1 : sections + mates]
-    wcat, wnc, bias, coef, odt, osr, rid, xt, sem = refs[sections + mates :]
-    choose(t, sections, lambda k: pltpu.make_async_copy(xs[k], xt, sem).start())
-    groups, deep, width = recv.shape
+def by_target(sources, odt):
+    groups, deep, width = sources[0].shape
     room = deep - 8
-    slots, ent_rows = odt.shape
     per = width // room
-    h = lax.axis_index("hist")
-    seat = lax.rem(h, mates)
-    degree = jnp.zeros((ent_rows, width), F32)
-    summed = [jnp.zeros((ent_rows, width), F32) for m in range(mates)]
+    ent_rows = odt.shape[1]
+    hots, tables = [], []
     ones = jnp.ones((width, width), BF)
     for g in range(groups // per):
-        ids = recv[g * per, room:, :].astype(F32)
+        ids = sources[0][g * per, room:, :].astype(F32)
         for j in range(1, per):
-            ids = jnp.maximum(ids, recv[g * per + j, room:, :].astype(F32))
+            ids = jnp.maximum(ids, sources[0][g * per + j, room:, :].astype(F32))
         hot = onehot(ids[:1].astype(jnp.int32), ent_rows)
-        degree = degree + dot(hot, ones)
-        for m, source in enumerate((recv, *mate_rows)):
-            rows = jnp.concatenate([source[g * per + j, :room, :] for j in range(per)], axis=0)
-            summed[m] = summed[m] + dot(hot, rows)
+        rows = [
+            jnp.concatenate([source[g * per + j, :room, :] for j in range(per)], axis=0)
+            for source in sources
+        ]
+        hots.append(hot)
+        tables.append(jnp.concatenate(rows + [ones], axis=1))
         odt[g * width : (g + 1) * width, :] = hot.astype(F32).T.astype(BF)
-    gathered = jnp.zeros((ent_rows, width), F32)
-    for m in range(mates):
-        high = summed[m].astype(BF)
-        low = (summed[m] - high.astype(F32)).astype(BF)
+    hot = jnp.concatenate(hots, axis=1)
+    got = dot(hot, jnp.concatenate(tables, axis=0))
+    count = len(sources)
+    summed = [got[:, m * width : (m + 1) * width] for m in range(count)]
+    return hot, summed, 1.0 / jnp.maximum(got[:, count * width :], 1.0)
+
+
+def through_weight(summed, mates, seat, wnc, first=0):
+    total = None
+    width = wnc.shape[1]
+    for m, part in enumerate(summed, start=first):
+        high = part.astype(BF)
+        low = (part - high.astype(F32)).astype(BF)
         w = wnc[place(lax.rem(seat - m + mates, mates), width), :]
-        gathered = gathered + dot(
-            jnp.concatenate([high, low], axis=1), jnp.concatenate([w, w], axis=0)
-        )
-    scaling = 1.0 / jnp.maximum(degree, 1.0)
-    coef[:, 3 * width :] = scaling
-    pltpu.make_async_copy(xs[0], xt, sem).wait()
-    straight = dot(xt[:ent_rows, :], wcat[...])
-    gate_open = jax.nn.sigmoid(straight[:, :width] + bias[:1, :])
-    pre_act = gathered * scaling + straight[:, width:]
-    sig = jax.nn.sigmoid(pre_act)
-    new_state = pre_act * sig
-    shut = 1.0 - gate_open
-    hidden = xt[:ent_rows, place(h, width)].astype(F32)
-    coef[:, :width] = (new_state - hidden) * gate_open * shut
-    coef[:, width : 2 * width] = gate_open * (sig * (1.0 + pre_act * (1.0 - sig)))
-    coef[:, 2 * width : 3 * width] = shut
+        out = dot(jnp.concatenate([high, low], axis=1), jnp.concatenate([w, w], axis=0))
+        total = out if total is None else total + out
+    return total
+
+
+def index_rows(xt, ent_rows, osr, rid):
     features = xt.shape[1]
     extra = xt[ent_rows:, :].astype(F32).astype(jnp.int32)
-    for k in range(slots // features):
+    for k in range(osr.shape[1] // features):
         cut = slice(k * features, (k + 1) * features)
         osr[:, cut] = onehot(extra[3 * k : 3 * k + 1], ent_rows)
         ids = extra[3 * k + 1 : 3 * k + 2] * 256 + extra[3 * k + 2 : 3 * k + 3]
         rid[:, cut] = jnp.broadcast_to(ids, (8, features))
+
+
+def factors(pre_act, gate_open, hidden):
+    sig = jax.nn.sigmoid(pre_act)
+    new_state = pre_act * sig
+    shut = 1.0 - gate_open
+    return (
+        (new_state - hidden) * gate_open * shut,
+        gate_open * (sig * (1.0 + pre_act * (1.0 - sig))),
+        shut,
+    )
+
+
+def early_kernel(t, sections, mates, *refs):
+    xs = refs[:sections]
+    tops, wcat, wnc, bias, odt, osr, rid, hot_out, partial, xt, sem = refs[sections:]
+    choose(t, sections, lambda k: pltpu.make_async_copy(xs[k], xt, sem).start())
+    ent_rows, width = odt.shape[1], wnc.shape[1]
+    h = lax.axis_index("hist")
+    hot, summed, scaling = by_target((tops,), odt)
+    hot_out[...] = hot
+    gathered = through_weight(summed, mates, lax.rem(h, mates), wnc)
+    pltpu.make_async_copy(xs[0], xt, sem).wait()
+    index_rows(xt, ent_rows, osr, rid)
+    straight = dot(xt[:ent_rows, :], wcat[...])
+    partial[0] = scaling
+    partial[1] = gathered * scaling + straight[:, width:]
+    partial[2] = jax.nn.sigmoid(straight[:, :width] + bias[:1, :])
+    partial[3] = xt[:ent_rows, place(h, width)].astype(F32)
+
+
+def state_kernel(t, sections, mates, *refs):
+    xs = refs[:sections]
+    sources = refs[sections : sections + mates]
+    wcat, wnc, bias, coef, odt, osr, rid, xt, sem = refs[sections + mates : sections + mates + 9]
+    held, sems = refs[sections + mates + 9 : -1], refs[-1]
+    copies = [
+        pltpu.make_async_copy(source.at[t], held[m], sems.at[m]) for m, source in enumerate(sources)
+    ]
+    for copy in copies:
+        copy.start()
+    choose(t, sections, lambda k: pltpu.make_async_copy(xs[k], xt, sem).start())
+    for copy in copies:
+        copy.wait()
+    ent_rows, width = odt.shape[1], wnc.shape[1]
+    h = lax.axis_index("hist")
+    _, summed, scaling = by_target(held, odt)
+    gathered = through_weight(summed, mates, lax.rem(h, mates), wnc)
+    pltpu.make_async_copy(xs[0], xt, sem).wait()
+    index_rows(xt, ent_rows, osr, rid)
+    straight = dot(xt[:ent_rows, :], wcat[...])
+    gate_open = jax.nn.sigmoid(straight[:, :width] + bias[:1, :])
+    hidden = xt[:ent_rows, place(h, width)].astype(F32)
+    values = factors(gathered * scaling + straight[:, width:], gate_open, hidden)
+    for k, value in enumerate((*values, scaling)):
+        coef[:, k * width : (k + 1) * width] = value
 
 
 def query_kernel(qe, qr, qg, wg, ws, wn, bias, top, qp, wcat, wnc, bias_out):
@@ -223,72 +272,88 @@
 
 
 def arrived(parts, ret, osr):
-    width = ret.shape[1]
-    c = parts[0][:, width:]
+    c = parts[0][...]
     for p in parts[1:]:
         c = c + p[...].astype(F32)
-    slots = osr.shape[1]
-    for m in range(ret.shape[0] // slots):
-        c = c + dot(osr[...], ret[m * slots : (m + 1) * slots, :])
+    slots, width = osr.shape[1], c.shape[1]
+    count = ret.shape[0] // slots
+    blocks = [ret[m * slots : (m + 1) * slots, :] for m in range(count)]
+    got = dot(osr[...], jnp.concatenate(blocks, axis=1))
+    for m in range(count):
+        c = c + got[:, m * width : (m + 1) * width]
     return c
 
 
 def step_kernel(sections, mates, first, *refs):
+    h = lax.axis_index("hist")
     if first:
+        partial, hot, *mate_rows = refs[1 : 2 + mates]
         c = refs[0][...]
-        refs = refs[1:]
+        odt, wcat, wnc, c_out, base, low, rep, bias, *sends = refs[2 + mates :]
+        table = jnp.concatenate([stacked(x) for x in mate_rows], axis=1)
+        width = wnc.shape[1]
+        got = dot(hot[...], table)
+        summed = [got[:, m * width : (m + 1) * width] for m in range(mates - 1)]
+        scaling = partial[0]
+        more = through_weight(summed, mates, lax.rem(h, mates), wnc, first=1)
+        al, be, shut = factors(partial[1] + more * scaling, partial[2], partial[3])
     else:
         c = arrived(refs[:sections], refs[sections], refs[sections + 1])
-        refs = refs[sections + 2 :]
-    coef, odt, wcat, wnc, pair, low, rep, bias, *sends = refs
+        coef, odt, wcat, wnc, c_out, base, low, rep, bias, *sends = refs[sections + 2 :]
+        width = wnc.shape[1]
+        al, be, shut, scaling = [coef[:, k * width : (k + 1) * width] for k in range(4)]
     slots = odt.shape[0]
-    width = rep.shape[1]
-    h = lax.axis_index("hist")
-    gate_term = c * coef[:, :width]
-    pre_term = c * coef[:, width : 2 * width]
-    g = (pre_term * coef[:, 3 * width :]).astype(BF)
-    low[:, 2 * width :] = g
+    gate_term = c * al
+    pre_term = c * be
+    g = (pre_term * scaling).astype(BF)
     out = dot(odt[...], dot(g, wnc[...], WIDE).astype(BF)).astype(BF)
     for m in range(mates):
         rep[m * slots : (m + 1) * slots, :] = out[:, m * width : (m + 1) * width]
     both = jnp.concatenate([gate_term.astype(BF), pre_term.astype(BF)], axis=1)
+    outs = []
+    for k in range(0, sections, 2):
+        rights = [
+            wcat[place(lax.rem(h + n, sections), width), :] for n in range(k, min(k + 2, sections))
+        ]
+        out = dot(both, jnp.concatenate(rights, axis=0), WIDE)
+        outs += [out[:, n * width : (n + 1) * width] for n in range(len(rights))]
+    for k in range(1, sections):
+        sends[k - 1][...] = outs[k].astype(BF)
+    low[:, 2 * width :] = g
     low[:, : 2 * width] = both
-    for k in range(sections):
-        out = dot(both, wcat[place(lax.rem(h + k, sections), width), :], WIDE)
-        if k == 0:
-            pair[:, width:] = c * coef[:, 2 * width : 3 * width] + out
-        else:
-            sends[k - 1][...] = out.astype(BF)
-    pair[:, :width] = c
+    c_out[...] = c
     bias[...] = jnp.broadcast_to(jnp.sum(gate_term, axis=0, keepdims=True), bias.shape)
+    base[...] = c * shut + outs[0]
 
 
 def grad_kernel(steps, mates, *refs):
-    xs = refs[:steps]
-    refs = refs[steps:]
-    gs, ns, bs, held = refs[-4:]
-    deep = 3 + mates
+    xs, recv = refs[:steps], refs[steps]
+    rest, tops = refs[steps + 1 : steps + mates], refs[steps + mates : steps + 2 * mates - 1]
+    refs = refs[steps + 2 * mates - 1 :]
+    rel_in = refs[3 * steps : 5 * steps - 2]
+    rs_in, gs, ns, bs, rs, held = refs[5 * steps - 2 :]
     h = lax.axis_index("hist")
-    for t in range(steps):
-        snapshot = steps - 1 - t
-        low, bias, odt = refs[deep * t : deep * t + 3]
-        rows = refs[deep * t + 3 : deep * (t + 1)]
+    for k in range(steps):
+        t = steps - 1 - k
+        low, bias, odt = refs[3 * k : 3 * k + 3]
         ent_rows = low.shape[0]
         width = low.shape[1] // 3
         seat = lax.rem(h, mates)
 
         def put(out, at, value):
-            out[at] = value if t == 0 else out[at] + value
-
-        held[snapshot] = low[:, : 2 * width]
+            out[at] = value if k == 0 else out[at] + value
+
+        held[t] = low[:, : 2 * width]
         put(bs, ..., bias[...])
         replies = dot(odt[...], low[:, 2 * width :]).astype(BF)
         for m in range(mates):
             source = lax.rem(seat - m + mates, mates)
-            put(ns, place(source, width), dot(stacked(rows[m]), replies, TALL))
+            rows = recv.at[t] if m == 0 else (tops[m - 1] if k == 0 else rest[m - 1].at[t])
+            put(ns, place(source, width), dot(stacked(rows), replies, TALL))
     for k in range(steps):
         value = dot(xs[k][:ent_rows, :], held[lax.rem(h - k + steps, steps)], TALL)
         gs[...] = value if k == 0 else gs[...] + value
+    rs[...] = rel_sum(steps - 1, rel_in, rs_in[...])
 
 
 def rel_sum(count, refs, total):
@@ -299,11 +364,6 @@
         for m in range(ret.shape[0] // slots):
             total = total + dot(hot, ret[m * slots : (m + 1) * slots, :])
     return total
-
-
-def rel_kernel(count, *refs):
-    old, out = refs[-2:]
-    out[...] = rel_sum(count, refs, old[...])
 
 
 def pack_kernel(sizes, relations, gs, ns, bs, ret, rid, old, mine, other, rs):
@@ -365,7 +425,7 @@
 
             @pl.when(to == t)
             def _():
-                outs[k][...] = saved[t - 1][:, : c.shape[1]]
+                outs[k][...] = saved[t - 1][...]
 
 
 def last_kernel(sections, groups, mates, sizes, factor, *refs):
@@ -442,13 +502,11 @@
     last = sections - 1
 
     ins = (hidden, edge_src, edge_rel)
-    (xp,) = run(
-        pre_kernel, "pre", ins, [whole(x) for x in ins], [far(sds((ent_rows + 8, features), BF))]
-    )
-    xs = [xp] + [far(turn(raw(xp), k)) for k in range(1, sections)]
+    (xp,) = run(pre_kernel, ins, [whole(x) for x in ins], [far(sds((ent_rows + 8, features), BF))])
+    turned = [turn(raw(xp), k) for k in range(1, sections)]
+    xs = [xp] + [far(x) for x in turned]
     (msg,) = run(
         functools.partial(send_kernel, sections, groups),
-        "send",
         (hidden, relation, edge_src, edge_dst, edge_rel, send_counts),
         [whole(hidden), whole(relation)] + [whole(edge_src)] * 3 + [smem],
         [far(sds((sections * groups, room + 8, width), BF))],
@@ -463,7 +521,6 @@
     ins = tuple(map(far, (qe, qr, query_grad, w_gate, w_self, w_neigh, bias_row)))
     top, rs, wcat, wnc, bias_cols = run(
         query_kernel,
-        "query",
         ins,
         [whole(x) for x in ins],
         [
@@ -479,48 +536,63 @@
     )
     recv, held = lax.optimization_barrier((recv, raw(wnc)))
     wnc = far(held)
-    came_rows = [recv[t] for t in range(sections)]
-    mate_rows = [[to_mate(x, m) for m in range(1, mates)] for x in came_rows]
+    tops, rest = recv[last], recv[:last]
+    mate_tops = [to_mate(tops, m) for m in range(1, mates)]
+    rest, *mate_tops = lax.optimization_barrier((rest, *mate_tops))
+    mate_rest = [to_mate(rest, m) for m in range(1, mates)]
     any_space = pl.BlockSpec(memory_space=pl.ANY)
 
-    def prepare(t, *after):
-        received = came_rows[t] if t == last else far(came_rows[t])
-        ins = (*xs, received, *mate_rows[t], wcat, wnc, bias_cols)
+    shapes = [
+        far(x)
+        for x in (
+            sds((slots, ent_rows), BF),
+            sds((ent_rows, slots), BF),
+            sds((8, slots), jnp.int32),
+        )
+    ]
+    row_scratch = [pltpu.VMEM((ent_rows + 8, features), BF), pltpu.SemaphoreType.DMA]
+
+    def prepare_first():
+        ins = (xp, *turned, tops, wcat, wnc, bias_cols)
+        return run(
+            functools.partial(early_kernel, last, sections, mates),
+            ins,
+            [any_space] * sections + [whole(x) for x in ins[sections:]],
+            shapes + [sds((ent_rows, slots), BF), sds((4, ent_rows, width), F32)],
+            row_scratch,
+        )
+
+    def prepare(t):
+        ins = (*xs, far(recv), *map(far, mate_rest), wcat, wnc, bias_cols)
         return run(
             functools.partial(state_kernel, t, sections, mates),
-            "state",
             ins,
-            [any_space for x in xs] + [whole(x) for x in ins[sections:]],
-            [
-                far(x)
-                for x in (
-                    sds((ent_rows, 4 * width), F32),
-                    sds((slots, ent_rows), BF),
-                    sds((ent_rows, slots), BF),
-                    sds((8, slots), jnp.int32),
-                )
-            ],
-            [pltpu.VMEM((ent_rows + 8, features), BF), pltpu.SemaphoreType.DMA],
+            [any_space] * (sections + mates) + [whole(x) for x in ins[sections + mates :]],
+            [far(sds((ent_rows, 4 * width), F32))] + shapes,
+            row_scratch
+            + [pltpu.VMEM(tops.shape, BF)] * mates
+            + [pltpu.SemaphoreType.DMA((mates,))],
         )
 
     saved = [None] * (sections + 1)
-    grad_ins, rel_ins = list(xs), []
+    grad_ins = [*xs, far(recv), *map(far, mate_rest), *map(far, mate_tops)]
+    rel_ins = []
     for t in range(last, -1, -1):
-        coef, odt, osr, rid = prepare(t)
-        if t > 0:
-            held, *mate_rows[t - 1] = lax.optimization_barrier((raw(coef), *mate_rows[t - 1]))
-            coef = far(held)
-        came = (top,) if t == last else (*parts, ret, osr_before)
-        ins = (*came, coef, odt, wcat, wnc)
-        pair, low, rep, bias, *sends = run(
+        if t == last:
+            odt, osr, rid, hot, partial = prepare_first()
+            ins = (top, partial, hot, *mate_tops, odt, wcat, wnc)
+        else:
+            coef, odt, osr, rid = prepare(t)
+            ins = (*parts, ret, osr_before, coef, odt, wcat, wnc)
+        c, base, low, rep, bias, *sends = run(
             functools.partial(step_kernel, sections, mates, t == last),
-            "step",
             ins,
             [whole(x) for x in ins],
             [
                 far(x)
                 for x in (
-                    sds((ent_rows, 2 * width), F32),
+                    rows_f32,
+                    rows_f32,
                     sds((ent_rows, 3 * width), BF),
                     sds((mates * slots, width), BF),
                     sds((8, width), F32),
@@ -528,7 +600,10 @@
                 )
             ],
         )
-        saved[t + 1] = pair
+        if t == last:
+            sent, *mate_rest = lax.optimization_barrier((raw(sends[0]), *mate_rest))
+            sends[0] = far(sent)
+        saved[t + 1] = c
         ret = lax.all_to_all(
             raw(rep).reshape(members, room, width),
             ("hist", "ent"),
@@ -537,28 +612,29 @@
             tiled=True,
             axis_index_groups=block_groups,
         ).reshape(mates * slots, width)
-        parts = [pair] + [turn(raw(x), k + 1) for k, x in enumerate(sends)]
+        parts = [base] + [turn(raw(x), k + 1) for k, x in enumerate(sends)]
         osr_before = osr
-        ins = (low, bias, odt, came_rows[t], *mate_rows[t])
-        grad_ins += [far(x) for x in ins]
+        grad_ins += [low, bias, odt]
         rel_ins += [far(ret), rid]
 
-    gs, ns, bs = run(
+    grad_ins += [*rel_ins[:-2], rs]
+    gs, ns, bs, rs = run(
         functools.partial(grad_kernel, sections, mates),
-        "grad",
         grad_ins,
         [whole(x) for x in grad_ins],
-        [far(sds((features, 2 * width), F32)), far(sds((half, width), F32)), far(sds((8, width), F32))],
+        [far(sds((features, 2 * width), F32)), far(sds((half, width), F32)), far(sds((8, width), F32)), far(sds((rel_rows, width), F32))],
         [pltpu.VMEM((sections, ent_rows, 2 * width), BF)],
     )
-    ins = (*rel_ins[:-2], rs)
-    (rs,) = run(
-        functools.partial(rel_kernel, last),
-        "rel",
+    ret, *moved = lax.optimization_barrier((ret, *parts[1:]))
+    parts = [parts[0], *moved]
+    ins = (*parts, ret, osr_before, *saved[1:sections])
+    picks = run(
+        functools.partial(pick_kernel, sections),
         ins,
         [whole(x) for x in ins],
-        [far(sds((rel_rows, width), F32))],
-    )
+        [rows_f32] * sections,
+    )
+    home = [picks[0]] + [turn(picks[k], k) for k in range(1, sections)]
     sizes = tuple(
         round_up(-(-rows // groups), 16) for rows in (features, features, half, rel_rows)
     )
@@ -568,16 +644,13 @@
     ins = tuple(ins)
     mine, other = run(
         functools.partial(pack_kernel, sizes, relations),
-        "pack",
         ins,
         [whole(x) for x in ins],
         [sds((pairs, chunk, width), BF)] * 2,
         [pltpu.VMEM((rel_rows, width), F32)],
     )
     ins = (mine, to_core(other))
-    (landed,) = run(
-        pair_kernel, "pair", ins, [whole(x) for x in ins], [sds((pairs, chunk, width), BF)]
-    )
+    (landed,) = run(pair_kernel, ins, [whole(x) for x in ins], [sds((pairs, chunk, width), BF)])
     same = [[i for i in range(groups) if i % 2 == core] for core in range(2)]
 
     def a2a_same(x):
@@ -585,21 +658,9 @@
             x, "ent", split_axis=0, concat_axis=0, tiled=True, axis_index_groups=same
         )
 
-    landed, *moved = lax.optimization_barrier((a2a_same(landed), *parts[1:]))
-    parts = [parts[0], *moved]
-    (copies,) = run(
-        add_kernel, "sum", (landed,), [whole(landed)], [sds((pairs, chunk, width), BF)]
-    )
-    ins = (*parts, ret, osr_before, *saved[1:sections])
-    picks = run(
-        functools.partial(pick_kernel, sections),
-        "pick",
-        ins,
-        [whole(x) for x in ins],
-        [rows_f32] * sections,
-    )
-    home = [picks[0]] + [turn(picks[k], k) for k in range(1, sections)]
-    column, *home = lax.optimization_barrier((a2a_same(copies), *home))
+    landed, *home = lax.optimization_barrier((a2a_same(landed), *home))
+    (copies,) = run(add_kernel, (landed,), [whole(landed)], [sds((pairs, chunk, width), BF)])
+    column = a2a_same(copies)
     mine = [column] + [turn(column, k) for k in range(1, sections)]
     other = [to_core(x) for x in mine]
     ins = (*mine, *other, *home)

time: 161 us -> 154 us (0.957)
  blocking collectives: 0 us -> 12.2 us
  waiting for transfers between devices: 44.7 us -> 35.7 us
  starting transfers between devices: 67.1 us -> 59.5 us
  Pallas kernels: 45.6 us -> 43 us
    all_to_all x0 -> x1, blocking collectives: none -> 12.2 us  [a2a_same(): lax.all_to_all(x, 'ent', split_axis=0, concat_axis=0, tiled=True, axis_in...]
    ppermute x21, waiting for transfers between devices: 21.9 us -> 11.7 us  [turn(): lax.ppermute(x, 'hist', [(i, (i + k) % sections) for i in range(sections)])]
    ppermute x4 -> x2, starting transfers between devices: 6.06 us -> 0.41 us  [to_mate(): return lax.ppermute(x, 'hist', route)]
    ppermute x4 -> x2, waiting for transfers between devices: 2.61 us -> 6.23 us  [to_mate(): return lax.ppermute(x, 'hist', route)]
    all_to_all x2 -> x1, waiting for transfers between devices: 2.79 us -> 0.01 us  [a2a_same(): lax.all_to_all(x, 'ent', split_axis=0, concat_axis=0, tiled=True, axis_in...]
    pallas_call x17 -> x16, Pallas kernels: 43.4 us -> 40.9 us  [run(): pl.pallas_call(body, in_specs=[spec(s) for s in specs], out_specs=[spec(b...]
    all_to_all x2 -> x1, starting transfers between devices: 6.9 us -> 4.59 us  [a2a_same(): lax.all_to_all(x, 'ent', split_axis=0, concat_axis=0, tiled=True, axis_in...]
    ppermute x21, starting transfers between devices: 26.8 us -> 28.8 us  [turn(): lax.ppermute(x, 'hist', [(i, (i + k) % sections) for i in range(sections)])]
  transfers between devices with their start and end apart: 37 -> 34, of which waited for: 23 -> 17; matrix products, arithmetic and copies ran while one was open for 0% -> 0% of each run, Pallas kernels for 17% -> 18%
where the time goes in v3:
time: 154 us; the launch traced here: 153 us
  starting transfers between devices  59.5 us (39%)
  Pallas kernels  43 us (28%)
  waiting for transfers between devices  35.7 us (23%)
  blocking collectives  12.2 us (8%)
  local copies, waits for them, and re-layouts  1.57 us (1%)
    pallas_call x16, Pallas kernels, run(): pl.pallas_call(body, in_specs=[spec(s) for s in specs], out_specs=[spec(b...  40.9 us
    ppermute x21, starting transfers between devices, turn(): lax.ppermute(x, 'hist', [(i, (i + k) % sections) for i in range(sections)])  28.8 us
    all_to_all x4, starting transfers between devices, on_device(): lax.all_to_all(raw(rep).reshape(members, room, width), ('hist', 'ent'), s...  18.2 us
    all_to_all x1, blocking collectives, a2a_same(): lax.all_to_all(x, 'ent', split_axis=0, concat_axis=0, tiled=True, axis_in...  12.2 us
    ppermute x21, waiting for transfers between devices, turn(): lax.ppermute(x, 'hist', [(i, (i + k) % sections) for i in range(sections)])  11.7 us
    all_to_all x1, waiting for transfers between devices, on_device(): lax.all_to_all(raw(msg), ('hist', 'ent'), split_axis=0, concat_axis=0, ti...  8.66 us
    all_to_all x1, starting transfers between devices, on_device(): lax.all_to_all(raw(msg), ('hist', 'ent'), split_axis=0, concat_axis=0, ti...  7.32 us
    all_to_all x4, waiting for transfers between devices, on_device(): lax.all_to_all(raw(rep).reshape(members, room, width), ('hist', 'ent'), s...  6.26 us
  transfers between devices with their start and end apart: 34, of which 17 were waited for; matrix products, arithmetic and copies ran while one was open for 0% of the time, Pallas kernels for 18%

profile of v3, /device:TPU:0, one launch (start us, length us, event | category | flops | bytes accessed | tf_op | source)
XLA Modules:
  0.0 153.1 jit_solution(5172725969553278173)
XLA Ops:
  1.3 2.5 %shard_map.173 = bf16[32,72,128]{2,1,0:T(8,128)(2,1)} custom-call(bf16[256,512]{1,0:T(8,128)(2,1)} %bitcast.31, bf16[460,512]{1,0:T(8,128)(2,1)} %rel.1, s32[1,512]{1,0:T(1,128)} %src.3, s32[1,512]{1,0:T(1,128)} %dst.1, s32[1,512]{1,0:T(1,128)} %rid.3, s32[1,8]{1,0:T(1,128)S(1)} %copy-done.7), custom_call_target="tpu_custom_call" | custom-call | tf_op jit(solution)/shard_map/pallas_call | solution.py:69
  3.8 7.3 %all-to-all-start = ((bf16[32,72,128]{2,1,0:T(8,128)(2,1)}), bf16[32,72,128]{2,1,0:T(8,128)(2,1)S(1)}, u32[]{:S(2)}, u32[]{:S(2)}) async-start(bf16[32,72,128]{2,1,0:T(8,128)(2,1)} %shard_map.173), calls=%async_computation | async-start | bytes 1179648 | tf_op jit(solution)/shard_map/all_to_all | solution.py:514
  12.9 1.8 %collective-permute-start = (bf16[264,512]{1,0:T(8,128)(2,1)}, bf16[264,512]{1,0:T(8,128)(2,1)S(1)}, u32[]{:S(2)}, u32[]{:S(2)}) collective-permute-start(bf16[264,512]{1,0:T(8,128)(2,1)} %shard_map.172.refs_0_), channel_id=1, source_target_pairs={{0,8},{8,16},{16,24},{24,0},{1,9},{9,17},{17,25},{25,1},{2,10},{10... | collective-permute-start | bytes 811016 | tf_op jit(solution)/shard_map/ppermute | solution.py:491
  17.6 2.7 %shard_map.174 = (f32[256,128]{1,0:T(8,128)}, f32[464,128]{1,0:T(8,128)}, bf16[512,256]{1,0:T(8,128)(2,1)}, bf16[256,128]{1,0:T(8,128)(2,1)}, f32[8,128]{1,0:T(8,128)}) custom-call(s32[1,128]{1,0:T(1,128)} %bitcast.38, s32[1,128]{1,0:T(1,128)} %bitcast.39, f32[128,512]{1,0:T(8,128)} %qg.1, bf16[512,512]{1,0:T(8,128)(2,1)} %wg.1, bf16[512,512]{1,0:T(8,128)(2,1)} %ws.1, ...), custom_call_target="tpu_custom_call" | custom-call | tf_op jit(solution)/shard_map/pallas_call | solution.py:69
  20.2 8.7 %all-to-all-done = bf16[32,72,128]{2,1,0:T(8,128)(2,1)S(1)} async-done(((bf16[32,72,128]{2,1,0:T(8,128)(2,1)}), bf16[32,72,128]{2,1,0:T(8,128)(2,1)S(1)}, u32[]{:S(2)}, u32[]{:S(2)}) %all-to-all-start) | async-done | bytes 589856 | tf_op jit(solution)/shard_map/all_to_all | solution.py:514
  29.7 6.2 %collective-permute-done.3.refs_3_.refs_6_ = bf16[8,72,128]{2,1,0:T(8,128)(2,1)S(1)} collective-permute-done((bf16[8,72,128]{2,1,0:T(8,128)(2,1)S(1)}, bf16[8,72,128]{2,1,0:T(8,128)(2,1)S(1)}, u32[]{:S(2)}, u32[]{:S(2)}) %collective-permute-start.3) | collective-permute-done | bytes 147488 | tf_op jit(solution)/shard_map/ppermute | solution.py:495
  36.3 2.8 %shard_map.175 = (bf16[512,256]{1,0:T(8,128)(2,1)}, bf16[256,512]{1,0:T(8,128)(2,1)}, s32[8,512]{1,0:T(8,128)}, bf16[256,512]{1,0:T(8,128)(2,1)S(1)}, f32[4,256,128]{2,1,0:T(8,128)S(1)}) custom-call(bf16[264,512]{1,0:T(8,128)(2,1)} %shard_map.172.refs_0_, bf16[264,512]{1,0:T(8,128)(2,1)S(1)} %collective-permute-done.refs_1_, ...), custom_call_target="tpu_custom_call" | custom-call | tf_op jit(solution)/shard_map/pallas_call | solution.py:69
  39.2 2.5 %shard_map.176 = (f32[256,128]{1,0:T(8,128)}, f32[256,128]{1,0:T(8,128)}, bf16[256,384]{1,0:T(8,128)(2,1)}, bf16[1024,128]{1,0:T(8,128)(2,1)}, f32[8,128]{1,0:T(...) custom-call(f32[256,128]{1,0:T(8,128)} %get-tuple-element.94.refs_0_, ...), custom_call_target="tpu_custom_call" | custom-call | tf_op jit(solution)/shard_map/pallas_call | solution.py:69
  41.7 5.2 %all-to-all-start.1 = ((bf16[16,64,128]{2,1,0:T(8,128)(2,1)}), bf16[16,64,128]{2,1,0:T(8,128)(2,1)S(1)}, u32[]{:S(2)}, u32[]{:S(2)}) async-start(bf16[16,64,128]{2,1,0:T(8,128)(2,1)} %bitcast.36), calls=%async_computation.1 | async-start | bytes 524288 | tf_op jit(solution)/shard_map/all_to_all | solution.py:607
  46.9 2.2 %collective-permute-start.6 = (bf16[256,128]{1,0:T(8,128)(2,1)S(1)}, bf16[256,128]{1,0:T(8,128)(2,1)S(1)}, u32[]{:S(2)}, u32[]{:S(2)}) collective-permute-start(bf16[256,128]{1,0:T(8,128)(2,1)S(1)} %copy-done.19), channel_id=1, source_target_pairs={{0,16},{8,24},{16,0},{24,8},{1,17},{9,25},{17,1},{25,9},{2,18},{10... | collective-permute-start | bytes 196616 | tf_op jit(solution)/shard_map/ppermute | solution.py:491
  51.4 3.6 %shard_map.177 = (f32[256,512]{1,0:T(8,128)}, bf16[512,256]{1,0:T(8,128)(2,1)}, bf16[256,512]{1,0:T(8,128)(2,1)}, s32[8,512]{1,0:T(8,128)}) custom-call(bf16[264,512]{1,0:T(8,128)(2,1)} %shard_map.172.refs_0_, bf16[264,512]{1,0:T(8,128)(2,1)} %copy-done, bf16[264,512]{1,0:T(8,128)(2,1)} %copy-done.1, bf16[264,512]{1,0:T(8,128)(2,1)} %copy-done.2, ...), custom_call_target="tpu_custom_call" | custom-call | tf_op jit(solution)/shard_map/pallas_call | solution.py:69
  55.0 2.0 %all-to-all-done.1 = bf16[16,64,128]{2,1,0:T(8,128)(2,1)S(1)} async-done(((bf16[16,64,128]{2,1,0:T(8,128)(2,1)}), bf16[16,64,128]{2,1,0:T(8,128)(2,1)S(1)}, u32[]{:S(2)}, u32[]{:S(2)}) %all-to-all-start.1) | async-done | bytes 262176 | tf_op jit(solution)/shard_map/all_to_all | solution.py:607
  57.0 2.8 %shard_map.178 = (f32[256,128]{1,0:T(8,128)}, f32[256,128]{1,0:T(8,128)}, bf16[256,384]{1,0:T(8,128)(2,1)}, bf16[1024,128]{1,0:T(8,128)(2,1)}, f32[8,128]{1,0:T(...) custom-call(f32[256,128]{1,0:T(8,128)} %get-tuple-element.103.refs_0_, ...), custom_call_target="tpu_custom_call" | custom-call | tf_op jit(solution)/shard_map/pallas_call | solution.py:69
  59.8 5.0 %all-to-all-start.2 = ((bf16[16,64,128]{2,1,0:T(8,128)(2,1)}), bf16[16,64,128]{2,1,0:T(8,128)(2,1)S(1)}, u32[]{:S(2)}, u32[]{:S(2)}) async-start(bf16[16,64,128]{2,1,0:T(8,128)(2,1)} %bitcast.35), calls=%async_computation.2 | async-start | bytes 524288 | tf_op jit(solution)/shard_map/all_to_all | solution.py:607
  64.8 2.0 %collective-permute-start.8 = (bf16[256,128]{1,0:T(8,128)(2,1)S(1)}, bf16[256,128]{1,0:T(8,128)(2,1)S(1)}, u32[]{:S(2)}, u32[]{:S(2)}) collective-permute-start(bf16[256,128]{1,0:T(8,128)(2,1)S(1)} %copy-done.21), channel_id=1, source_target_pairs={{0,8},{8,16},{16,24},{24,0},{1,9},{9,17},{17,25},{25,1},{2,10},{10... | collective-permute-start | bytes 196616 | tf_op jit(solution)/shard_map/ppermute | solution.py:491
  68.8 3.6 %shard_map.179 = (f32[256,512]{1,0:T(8,128)}, bf16[512,256]{1,0:T(8,128)(2,1)}, bf16[256,512]{1,0:T(8,128)(2,1)}, s32[8,512]{1,0:T(8,128)}) custom-call(bf16[264,512]{1,0:T(8,128)(2,1)} %shard_map.172.refs_0_, bf16[264,512]{1,0:T(8,128)(2,1)} %copy-done, bf16[264,512]{1,0:T(8,128)(2,1)} %copy-done.1, bf16[264,512]{1,0:T(8,128)(2,1)} %copy-done.2, ...), custom_call_target="tpu_custom_call" | custom-call | tf_op jit(solution)/shard_map/pallas_call | solution.py:69
  72.9 1.9 %all-to-all-done.2 = bf16[16,64,128]{2,1,0:T(8,128)(2,1)S(1)} async-done(((bf16[16,64,128]{2,1,0:T(8,128)(2,1)}), bf16[16,64,128]{2,1,0:T(8,128)(2,1)S(1)}, u32[]{:S(2)}, u32[]{:S(2)}) %all-to-all-start.2) | async-done | bytes 262176 | tf_op jit(solution)/shard_map/all_to_all | solution.py:607
  74.8 2.8 %shard_map.180 = (f32[256,128]{1,0:T(8,128)}, f32[256,128]{1,0:T(8,128)}, bf16[256,384]{1,0:T(8,128)(2,1)}, bf16[1024,128]{1,0:T(8,128)(2,1)}, f32[8,128]{1,0:T(...) custom-call(f32[256,128]{1,0:T(8,128)} %get-tuple-element.115.refs_0_, ...), custom_call_target="tpu_custom_call" | custom-call | tf_op jit(solution)/shard_map/pallas_call | solution.py:69
  77.7 4.0 %all-to-all-start.3 = ((bf16[16,64,128]{2,1,0:T(8,128)(2,1)}), bf16[16,64,128]{2,1,0:T(8,128)(2,1)S(1)}, u32[]{:S(2)}, u32[]{:S(2)}) async-start(bf16[16,64,128]{2,1,0:T(8,128)(2,1)} %bitcast.34), calls=%async_computation.3 | async-start | bytes 524288 | tf_op jit(solution)/shard_map/all_to_all | solution.py:607
  81.7 2.0 %collective-permute-start.11 = (bf16[256,128]{1,0:T(8,128)(2,1)S(1)}, bf16[256,128]{1,0:T(8,128)(2,1)S(1)}, u32[]{:S(2)}, u32[]{:S(2)}) collective-permute-start(bf16[256,128]{1,0:T(8,128)(2,1)S(1)} %copy-done.20), channel_id=1, source_target_pairs={{0,8},{8,16},{16,24},{24,0},{1,9},{9,17},{17,25},{25,1},{2,10},{10... | collective-permute-start | bytes 196616 | tf_op jit(solution)/shard_map/ppermute | solution.py:491
  85.7 3.6 %shard_map.181 = (f32[256,512]{1,0:T(8,128)}, bf16[512,256]{1,0:T(8,128)(2,1)}, bf16[256,512]{1,0:T(8,128)(2,1)}, s32[8,512]{1,0:T(8,128)}) custom-call(bf16[264,512]{1,0:T(8,128)(2,1)} %shard_map.172.refs_0_, bf16[264,512]{1,0:T(8,128)(2,1)} %copy-done, bf16[264,512]{1,0:T(8,128)(2,1)} %copy-done.1, bf16[264,512]{1,0:T(8,128)(2,1)} %copy-done.2, ...), custom_call_target="tpu_custom_call" | custom-call | tf_op jit(solution)/shard_map/pallas_call | solution.py:69
  89.7 2.0 %all-to-all-done.3 = bf16[16,64,128]{2,1,0:T(8,128)(2,1)S(1)} async-done(((bf16[16,64,128]{2,1,0:T(8,128)(2,1)}), bf16[16,64,128]{2,1,0:T(8,128)(2,1)S(1)}, u32[]{:S(2)}, u32[]{:S(2)}) %all-to-all-start.3) | async-done | bytes 262176 | tf_op jit(solution)/shard_map/all_to_all | solution.py:607
  91.7 2.8 %shard_map.182 = (f32[256,128]{1,0:T(8,128)}, f32[256,128]{1,0:T(8,128)}, bf16[256,384]{1,0:T(8,128)(2,1)}, bf16[1024,128]{1,0:T(8,128)(2,1)}, f32[8,128]{1,0:T(...) custom-call(f32[256,128]{1,0:T(8,128)} %get-tuple-element.125.refs_0_, ...), custom_call_target="tpu_custom_call" | custom-call | tf_op jit(solution)/shard_map/pallas_call | solution.py:69
  94.5 4.0 %all-to-all-start.4 = ((bf16[16,64,128]{2,1,0:T(8,128)(2,1)}), bf16[16,64,128]{2,1,0:T(8,128)(2,1)S(1)}, u32[]{:S(2)}, u32[]{:S(2)}) async-start(bf16[16,64,128]{2,1,0:T(8,128)(2,1)} %bitcast.33), calls=%async_computation.4 | async-start | bytes 524288 | tf_op jit(solution)/shard_map/all_to_all | solution.py:607
  98.5 2.0 %collective-permute-start.14 = (bf16[256,128]{1,0:T(8,128)(2,1)S(1)}, bf16[256,128]{1,0:T(8,128)(2,1)S(1)}, u32[]{:S(2)}, u32[]{:S(2)}) collective-permute-start(bf16[256,128]{1,0:T(8,128)(2,1)S(1)} %copy-done.12), channel_id=1, source_target_pairs={{0,8},{8,16},{16,24},{24,0},{1,9},{9,17},{17,25},{25,1},{2,10},{10... | collective-permute-start | bytes 196616 | tf_op jit(solution)/shard_map/ppermute | solution.py:491
  102.5 5.5 %shard_map.183 = (f32[512,256]{1,0:T(8,128)}, f32[256,128]{1,0:T(8,128)}, f32[8,128]{1,0:T(8,128)}, f32[464,128]{1,0:T(8,128)}) custom-call(bf16[264,512]{1,0:T(8,128)(2,1)} %shard_map.172.refs_0_, bf16[264,512]{1,0:T(8,128)(2,1)} %copy-done, bf16[264,512]{1,0:T(8,128)(2,1)} %copy-done.1, bf16[264,512]{1,0:T(8,128)(2,1)} %copy-done.2, ...), custom_call_target="tpu_custom_call" | custom-call | tf_op jit(solution)/shard_map/pallas_call | solution.py:69
  112.5 4.6 %all-to-all-start.5 = ((bf16[4,224,128]{2,1,0:T(8,128)(2,1)}), bf16[4,224,128]{2,1,0:T(8,128)(2,1)S(1)}, u32[]{:S(2)}, u32[]{:S(2)}) async-start(bf16[4,224,128]{2,1,0:T(8,128)(2,1)} %shard_map.185), calls=%async_computation.5 | async-start | bytes 458752 | tf_op jit(solution)/shard_map/all_to_all | solution.py:657
  120.2 2.4 %collective-permute-start.20 = (f32[256,128]{1,0:T(8,128)S(1)}, f32[256,128]{1,0:T(8,128)S(1)}, u32[]{:S(2)}, u32[]{:S(2)}) collective-permute-start(f32[256,128]{1,0:T(8,128)S(1)} %get-tuple-element.162), channel_id=1, source_target_pairs={{0,24},{8,0},{16,8},{24,16},{1,25},{9,1},{17,9},{25,17},{2,26},{10... | collective-permute-start | bytes 393224 | tf_op jit(solution)/shard_map/ppermute | solution.py:491
  122.5 3.3 %collective-permute-done.18.refs_9_ = f32[256,128]{1,0:T(8,128)S(1)} collective-permute-done((f32[256,128]{1,0:T(8,128)S(1)}, f32[256,128]{1,0:T(8,128)S(1)}, u32[]{:S(2)}, u32[]{:S(2)}) %collective-permute-start.18) | collective-permute-done | bytes 131104 | tf_op jit(solution)/shard_map/ppermute | solution.py:491
  127.2 12.2 %all_to_all.35.refs_0_ = bf16[4,224,128]{2,1,0:T(8,128)(2,1)S(1)} all-to-all(bf16[4,224,128]{2,1,0:T(8,128)(2,1)S(1)} %shard_map.187), channel_id=1, replica_groups={{0,2,4,6},{1,3,5,7},{8,10,12,14},{9,11,13,15},{16,18,20,22},{17,19,21,2..., dimensions={0} | all-to-all | bytes 458752 | tf_op jit(solution)/shard_map/all_to_all | solution.py:657
  143.3 4.2 %collective-permute-done.21.refs_1_ = bf16[4,224,128]{2,1,0:T(8,128)(2,1)S(1)} collective-permute-done((bf16[4,224,128]{2,1,0:T(8,128)(2,1)S(1)}, bf16[4,224,128]{2,1,0:T(8,128)(2,1)S(1)}, u32[]{:S(2)}, u32[]{:S(2)}) %collective-permute-start.21) | collective-permute-done | bytes 229408 | tf_op jit(solution)/shard_map/ppermute | solution.py:491
  150.9 2.1 %last.1 = (f32[256,512]{1,0:T(8,128)}, f32[2,256,256]{2,1,0:T(8,128)}, f32[512,512]{1,0:T(8,128)}, f32[512,512]{1,0:T(8,128)}, f32[1,512]{1,0:T(1,128)}, /*index=5*/f32[460,512]{1,0:T(8,128)}) custom-call(bf16[4,224,128]{2,1,0:T(8,128)(2,1)S(1)} %all_to_all.35.refs_0_, bf16[4,224,128]{2,1,0:T(8,128)(2,1)S(1)} %collective-permute-done.21.refs_1_, ...), custom_call_target="tpu_custom_call" | custom-call | tf_op jit(solution)/shard_map/last/pallas_call | solution.py:669
  (100 shorter events, 31.7 us)
Async XLA Ops:
  3.8 25.1 %all-to-all-start = ((bf16[32,72,128]{2,1,0:T(8,128)(2,1)}), bf16[32,72,128]{2,1,0:T(8,128)(2,1)S(1)}, u32[]{:S(2)}, u32[]{:S(2)}) async-start(bf16[32,72,128]{2,1,0:T(8,128)(2,1)} %shard_map.173), calls=%async_computation | async-start | bytes 1179648 | tf_op jit(solution)/shard_map/all_to_all | solution.py:514
  12.9 23.4 %collective-permute-start = (bf16[264,512]{1,0:T(8,128)(2,1)}, bf16[264,512]{1,0:T(8,128)(2,1)S(1)}, u32[]{:S(2)}, u32[]{:S(2)}) collective-permute-start(bf16[264,512]{1,0:T(8,128)(2,1)} %shard_map.172.refs_0_), channel_id=1, source_target_pairs={{0,8},{8,16},{16,24},{24,0},{1,9},{9,17},{17,25},{25,1},{2,10},{10... | collective-permute-start | bytes 811016 | tf_op jit(solution)/shard_map/ppermute | solution.py:491
  14.6 21.6 %collective-permute-start.1 = (bf16[264,512]{1,0:T(8,128)(2,1)}, bf16[264,512]{1,0:T(8,128)(2,1)S(1)}, u32[]{:S(2)}, u32[]{:S(2)}) collective-permute-start(bf16[264,512]{1,0:T(8,128)(2,1)} %shard_map.172.refs_0_), channel_id=1, source_target_pairs={{0,16},{8,24},{16,0},{24,8},{1,17},{9,25},{17,1},{25,9},{2,18},{10... | collective-permute-start | bytes 811016 | tf_op jit(solution)/shard_map/ppermute | solution.py:491
  16.1 20.2 %collective-permute-start.2 = (bf16[264,512]{1,0:T(8,128)(2,1)}, bf16[264,512]{1,0:T(8,128)(2,1)S(1)}, u32[]{:S(2)}, u32[]{:S(2)}) collective-permute-start(bf16[264,512]{1,0:T(8,128)(2,1)} %shard_map.172.refs_0_), channel_id=1, source_target_pairs={{0,24},{8,0},{16,8},{24,16},{1,25},{9,1},{17,9},{25,17},{2,26},{10... | collective-permute-start | bytes 811016 | tf_op jit(solution)/shard_map/ppermute | solution.py:491
  28.9 7.0 %collective-permute-start.3 = (bf16[8,72,128]{2,1,0:T(8,128)(2,1)S(1)}, bf16[8,72,128]{2,1,0:T(8,128)(2,1)S(1)}, u32[]{:S(2)}, u32[]{:S(2)}) collective-permute-start(bf16[8,72,128]{2,1,0:T(8,128)(2,1)S(1)} %slice_bitcast_fusion.refs_4_), channel_id=1, source_target_pairs={{0,8},{8,0},{16,24},{24,16},{1,9},{9,1},{17,25},{25,17},{2,10},{10... | collective-permute-start | bytes 442376 | tf_op jit(solution)/shard_map/ppermute | solution.py:495
  35.9 14.7 %collective-permute-start.4 = (bf16[3,8,72,128]{3,2,1,0:T(8,128)(2,1)S(1)}, bf16[3,8,72,128]{3,2,1,0:T(8,128)(2,1)S(1)}, u32[]{:S(2)}, u32[]{:S(2)}) collective-permute-start(bf16[3,8,72,128]{3,2,1,0:T(8,128)(2,1)S(1)} %slice.6), channel_id=1, source_target_pairs={{0,8},{8,0},{16,24},{24,16},{1,9},{9,1},{17,25},{25,17},{2,10},{10... | collective-permute-start | bytes 1327112 | tf_op jit(solution)/shard_map/ppermute | solution.py:495
  41.7 15.2 %all-to-all-start.1 = ((bf16[16,64,128]{2,1,0:T(8,128)(2,1)}), bf16[16,64,128]{2,1,0:T(8,128)(2,1)S(1)}, u32[]{:S(2)}, u32[]{:S(2)}) async-start(bf16[16,64,128]{2,1,0:T(8,128)(2,1)} %bitcast.36), calls=%async_computation.1 | async-start | bytes 524288 | tf_op jit(solution)/shard_map/all_to_all | solution.py:607
  46.9 8.0 %collective-permute-start.6 = (bf16[256,128]{1,0:T(8,128)(2,1)S(1)}, bf16[256,128]{1,0:T(8,128)(2,1)S(1)}, u32[]{:S(2)}, u32[]{:S(2)}) collective-permute-start(bf16[256,128]{1,0:T(8,128)(2,1)S(1)} %copy-done.19), channel_id=1, source_target_pairs={{0,16},{8,24},{16,0},{24,8},{1,17},{9,25},{17,1},{25,9},{2,18},{10... | collective-permute-start | bytes 196616 | tf_op jit(solution)/shard_map/ppermute | solution.py:491
  49.2 5.8 %collective-permute-start.7 = (bf16[256,128]{1,0:T(8,128)(2,1)S(1)}, bf16[256,128]{1,0:T(8,128)(2,1)S(1)}, u32[]{:S(2)}, u32[]{:S(2)}) collective-permute-start(bf16[256,128]{1,0:T(8,128)(2,1)S(1)} %copy-done.16), channel_id=1, source_target_pairs={{0,24},{8,0},{16,8},{24,16},{1,25},{9,1},{17,9},{25,17},{2,26},{10... | collective-permute-start | bytes 196616 | tf_op jit(solution)/shard_map/ppermute | solution.py:491
  50.6 6.4 %collective-permute-start.5 = (bf16[256,128]{1,0:T(8,128)(2,1)S(1)}, bf16[256,128]{1,0:T(8,128)(2,1)S(1)}, u32[]{:S(2)}, u32[]{:S(2)}) collective-permute-start(bf16[256,128]{1,0:T(8,128)(2,1)S(1)} %copy-done.13), channel_id=1, source_target_pairs={{0,8},{8,16},{16,24},{24,0},{1,9},{9,17},{17,25},{25,1},{2,10},{10... | collective-permute-start | bytes 196616 | tf_op jit(solution)/shard_map/ppermute | solution.py:491
  59.8 15.0 %all-to-all-start.2 = ((bf16[16,64,128]{2,1,0:T(8,128)(2,1)}), bf16[16,64,128]{2,1,0:T(8,128)(2,1)S(1)}, u32[]{:S(2)}, u32[]{:S(2)}) async-start(bf16[16,64,128]{2,1,0:T(8,128)(2,1)} %bitcast.35), calls=%async_computation.2 | async-start | bytes 524288 | tf_op jit(solution)/shard_map/all_to_all | solution.py:607
  64.8 7.6 %collective-permute-start.8 = (bf16[256,128]{1,0:T(8,128)(2,1)S(1)}, bf16[256,128]{1,0:T(8,128)(2,1)S(1)}, u32[]{:S(2)}, u32[]{:S(2)}) collective-permute-start(bf16[256,128]{1,0:T(8,128)(2,1)S(1)} %copy-done.21), channel_id=1, source_target_pairs={{0,8},{8,16},{16,24},{24,0},{1,9},{9,17},{17,25},{25,1},{2,10},{10... | collective-permute-start | bytes 196616 | tf_op jit(solution)/shard_map/ppermute | solution.py:491
  66.8 5.7 %collective-permute-start.9 = (bf16[256,128]{1,0:T(8,128)(2,1)S(1)}, bf16[256,128]{1,0:T(8,128)(2,1)S(1)}, u32[]{:S(2)}, u32[]{:S(2)}) collective-permute-start(bf16[256,128]{1,0:T(8,128)(2,1)S(1)} %copy-done.18), channel_id=1, source_target_pairs={{0,16},{8,24},{16,0},{24,8},{1,17},{9,25},{17,1},{25,9},{2,18},{10... | collective-permute-start | bytes 196616 | tf_op jit(solution)/shard_map/ppermute | solution.py:491
  67.8 5.1 %collective-permute-start.10 = (bf16[256,128]{1,0:T(8,128)(2,1)S(1)}, bf16[256,128]{1,0:T(8,128)(2,1)S(1)}, u32[]{:S(2)}, u32[]{:S(2)}) collective-permute-start(bf16[256,128]{1,0:T(8,128)(2,1)S(1)} %copy-done.15), channel_id=1, source_target_pairs={{0,24},{8,0},{16,8},{24,16},{1,25},{9,1},{17,9},{25,17},{2,26},{10... | collective-permute-start | bytes 196616 | tf_op jit(solution)/shard_map/ppermute | solution.py:491
  77.7 14.0 %all-to-all-start.3 = ((bf16[16,64,128]{2,1,0:T(8,128)(2,1)}), bf16[16,64,128]{2,1,0:T(8,128)(2,1)S(1)}, u32[]{:S(2)}, u32[]{:S(2)}) async-start(bf16[16,64,128]{2,1,0:T(8,128)(2,1)} %bitcast.34), calls=%async_computation.3 | async-start | bytes 524288 | tf_op jit(solution)/shard_map/all_to_all | solution.py:607
  81.7 7.6 %collective-permute-start.11 = (bf16[256,128]{1,0:T(8,128)(2,1)S(1)}, bf16[256,128]{1,0:T(8,128)(2,1)S(1)}, u32[]{:S(2)}, u32[]{:S(2)}) collective-permute-start(bf16[256,128]{1,0:T(8,128)(2,1)S(1)} %copy-done.20), channel_id=1, source_target_pairs={{0,8},{8,16},{16,24},{24,0},{1,9},{9,17},{17,25},{25,1},{2,10},{10... | collective-permute-start | bytes 196616 | tf_op jit(solution)/shard_map/ppermute | solution.py:491
  83.7 5.6 %collective-permute-start.12 = (bf16[256,128]{1,0:T(8,128)(2,1)S(1)}, bf16[256,128]{1,0:T(8,128)(2,1)S(1)}, u32[]{:S(2)}, u32[]{:S(2)}) collective-permute-start(bf16[256,128]{1,0:T(8,128)(2,1)S(1)} %copy-done.17), channel_id=1, source_target_pairs={{0,16},{8,24},{16,0},{24,8},{1,17},{9,25},{17,1},{25,9},{2,18},{10... | collective-permute-start | bytes 196616 | tf_op jit(solution)/shard_map/ppermute | solution.py:491
  84.7 5.1 %collective-permute-start.13 = (bf16[256,128]{1,0:T(8,128)(2,1)S(1)}, bf16[256,128]{1,0:T(8,128)(2,1)S(1)}, u32[]{:S(2)}, u32[]{:S(2)}) collective-permute-start(bf16[256,128]{1,0:T(8,128)(2,1)S(1)} %copy-done.14), channel_id=1, source_target_pairs={{0,24},{8,0},{16,8},{24,16},{1,25},{9,1},{17,9},{25,17},{2,26},{10... | collective-permute-start | bytes 196616 | tf_op jit(solution)/shard_map/ppermute | solution.py:491
  94.5 14.0 %all-to-all-start.4 = ((bf16[16,64,128]{2,1,0:T(8,128)(2,1)}), bf16[16,64,128]{2,1,0:T(8,128)(2,1)S(1)}, u32[]{:S(2)}, u32[]{:S(2)}) async-start(bf16[16,64,128]{2,1,0:T(8,128)(2,1)} %bitcast.33), calls=%async_computation.4 | async-start | bytes 524288 | tf_op jit(solution)/shard_map/all_to_all | solution.py:607
  98.5 9.6 %collective-permute-start.14 = (bf16[256,128]{1,0:T(8,128)(2,1)S(1)}, bf16[256,128]{1,0:T(8,128)(2,1)S(1)}, u32[]{:S(2)}, u32[]{:S(2)}) collective-permute-start(bf16[256,128]{1,0:T(8,128)(2,1)S(1)} %copy-done.12), channel_id=1, source_target_pairs={{0,8},{8,16},{16,24},{24,0},{1,9},{9,17},{17,25},{25,1},{2,10},{10... | collective-permute-start | bytes 196616 | tf_op jit(solution)/shard_map/ppermute | solution.py:491
  100.5 7.6 %collective-permute-start.15 = (bf16[256,128]{1,0:T(8,128)(2,1)S(1)}, bf16[256,128]{1,0:T(8,128)(2,1)S(1)}, u32[]{:S(2)}, u32[]{:S(2)}) collective-permute-start(bf16[256,128]{1,0:T(8,128)(2,1)S(1)} %copy-done.11), channel_id=1, source_target_pairs={{0,16},{8,24},{16,0},{24,8},{1,17},{9,25},{17,1},{25,9},{2,18},{10... | collective-permute-start | bytes 196616 | tf_op jit(solution)/shard_map/ppermute | solution.py:491
  101.5 6.6 %collective-permute-start.16 = (bf16[256,128]{1,0:T(8,128)(2,1)S(1)}, bf16[256,128]{1,0:T(8,128)(2,1)S(1)}, u32[]{:S(2)}, u32[]{:S(2)}) collective-permute-start(bf16[256,128]{1,0:T(8,128)(2,1)S(1)} %copy-done.10), channel_id=1, source_target_pairs={{0,24},{8,0},{16,8},{24,16},{1,25},{9,1},{17,9},{25,17},{2,26},{10... | collective-permute-start | bytes 196616 | tf_op jit(solution)/shard_map/ppermute | solution.py:491
  110.2 1.6 %collective-permute-start.17 = (bf16[4,224,128]{2,1,0:T(8,128)(2,1)S(1)}, bf16[4,224,128]{2,1,0:T(8,128)(2,1)S(1)}, u32[]{:S(2)}, u32[]{:S(2)}) collective-permute-start(bf16[4,224,128]{2,1,0:T(8,128)(2,1)S(1)} %get-tuple-element.150), channel_id=1, source_target_pairs={{0,1},{1,0},{2,3},{3,2},{4,5},{5,4},{6,7},{7,6},{8,9},{9,8},{10,11... | collective-permute-start | bytes 688136 | tf_op jit(solution)/shard_map/ppermute | solution.py:498
  112.5 14.7 %all-to-all-start.5 = ((bf16[4,224,128]{2,1,0:T(8,128)(2,1)}), bf16[4,224,128]{2,1,0:T(8,128)(2,1)S(1)}, u32[]{:S(2)}, u32[]{:S(2)}) async-start(bf16[4,224,128]{2,1,0:T(8,128)(2,1)} %shard_map.185), calls=%async_computation.5 | async-start | bytes 458752 | tf_op jit(solution)/shard_map/all_to_all | solution.py:657
  118.5 7.3 %collective-permute-start.18 = (f32[256,128]{1,0:T(8,128)S(1)}, f32[256,128]{1,0:T(8,128)S(1)}, u32[]{:S(2)}, u32[]{:S(2)}) collective-permute-start(f32[256,128]{1,0:T(8,128)S(1)} %get-tuple-element.160), channel_id=1, source_target_pairs={{0,8},{8,16},{16,24},{24,0},{1,9},{9,17},{17,25},{25,1},{2,10},{10... | collective-permute-start | bytes 393224 | tf_op jit(solution)/shard_map/ppermute | solution.py:491
  119.2 7.8 %collective-permute-start.19 = (f32[256,128]{1,0:T(8,128)S(1)}, f32[256,128]{1,0:T(8,128)S(1)}, u32[]{:S(2)}, u32[]{:S(2)}) collective-permute-start(f32[256,128]{1,0:T(8,128)S(1)} %get-tuple-element.161), channel_id=1, source_target_pairs={{0,16},{8,24},{16,0},{24,8},{1,17},{9,25},{17,1},{25,9},{2,18},{10... | collective-permute-start | bytes 393224 | tf_op jit(solution)/shard_map/ppermute | solution.py:491
  120.2 7.0 %collective-permute-start.20 = (f32[256,128]{1,0:T(8,128)S(1)}, f32[256,128]{1,0:T(8,128)S(1)}, u32[]{:S(2)}, u32[]{:S(2)}) collective-permute-start(f32[256,128]{1,0:T(8,128)S(1)} %get-tuple-element.162), channel_id=1, source_target_pairs={{0,24},{8,0},{16,8},{24,16},{1,25},{9,1},{17,9},{25,17},{2,26},{10... | collective-permute-start | bytes 393224 | tf_op jit(solution)/shard_map/ppermute | solution.py:491
  139.4 8.1 %collective-permute-start.21 = (bf16[4,224,128]{2,1,0:T(8,128)(2,1)S(1)}, bf16[4,224,128]{2,1,0:T(8,128)(2,1)S(1)}, u32[]{:S(2)}, u32[]{:S(2)}) collective-permute-start(bf16[4,224,128]{2,1,0:T(8,128)(2,1)S(1)} %all_to_all.35.refs_0_), channel_id=1, source_target_pairs={{0,8},{8,16},{16,24},{24,0},{1,9},{9,17},{17,25},{25,1},{2,10},{10... | collective-permute-start | bytes 688136 | tf_op jit(solution)/shard_map/ppermute | solution.py:491
  140.6 8.3 %collective-permute-start.22 = (bf16[4,224,128]{2,1,0:T(8,128)(2,1)S(1)}, bf16[4,224,128]{2,1,0:T(8,128)(2,1)S(1)}, u32[]{:S(2)}, u32[]{:S(2)}) collective-permute-start(bf16[4,224,128]{2,1,0:T(8,128)(2,1)S(1)} %all_to_all.35.refs_0_), channel_id=1, source_target_pairs={{0,16},{8,24},{16,0},{24,8},{1,17},{9,25},{17,1},{25,9},{2,18},{10... | collective-permute-start | bytes 688136 | tf_op jit(solution)/shard_map/ppermute | solution.py:491
  141.7 7.8 %collective-permute-start.23 = (bf16[4,224,128]{2,1,0:T(8,128)(2,1)S(1)}, bf16[4,224,128]{2,1,0:T(8,128)(2,1)S(1)}, u32[]{:S(2)}, u32[]{:S(2)}) collective-permute-start(bf16[4,224,128]{2,1,0:T(8,128)(2,1)S(1)} %all_to_all.35.refs_0_), channel_id=1, source_target_pairs={{0,24},{8,0},{16,8},{24,16},{1,25},{9,1},{17,9},{25,17},{2,26},{10... | collective-permute-start | bytes 688136 | tf_op jit(solution)/shard_map/ppermute | solution.py:491
  143.3 6.2 %collective-permute-start.24 = (bf16[4,224,128]{2,1,0:T(8,128)(2,1)S(1)}, bf16[4,224,128]{2,1,0:T(8,128)(2,1)S(1)}, u32[]{:S(2)}, u32[]{:S(2)}) collective-permute-start(bf16[4,224,128]{2,1,0:T(8,128)(2,1)S(1)} %all_to_all.35.refs_0_), channel_id=1, source_target_pairs={{0,1},{1,0},{2,3},{3,2},{4,5},{5,4},{6,7},{7,6},{8,9},{9,8},{10,11... | collective-permute-start | bytes 688136 | tf_op jit(solution)/shard_map/ppermute | solution.py:498
  147.5 1.9 %collective-permute-start.25 = (bf16[4,224,128]{2,1,0:T(8,128)(2,1)S(1)}, bf16[4,224,128]{2,1,0:T(8,128)(2,1)S(1)}, u32[]{:S(2)}, u32[]{:S(2)}) collective-permute-start(bf16[4,224,128]{2,1,0:T(8,128)(2,1)S(1)} %collective-permute-done.21.refs_1_), channel_id=1, source_target_pairs={{0,1},{1,0},{2,3},{3,2},{4,5},{5,4},{6,7},{7,6},{8,9},{9,8},{10,11... | collective-permute-start | bytes 688136 | tf_op jit(solution)/shard_map/ppermute | solution.py:498
  (24 other events, 101.1 us)
